TPU v7x, 512 devices: a whole 4x8x8 slice. The times are simulated.
512 devices in a mesh: ctx: 32 (over z, y_hi), heads: 16 (over y_lo, x, core).
Axes of the slice: x: 4, y: 8 (y_hi: 4, y_lo: 2; y = y_hi * 2 + y_lo), z: 8, core: 2. Of those that a mesh axis runs over, the one named last changes fastest.
Arguments:
- resid_in: bfloat16 [4096, 5376], P('ctx', 'heads'), may hold values from -6 to 6
- first_layer_queries: bfloat16 [4096, 4096], P('ctx', 'heads'), may hold values from -270 to 270
- first_layer_keys: bfloat16 [4096, 2048], P('ctx', 'heads'), may hold values from -7 to 7
- first_layer_values: bfloat16 [4096, 2048], P('ctx', 'heads'), may hold values from -6 to 6
- out_one: bfloat16 [4096, 5376], P('heads'), may hold values from -6 to 6
- post_gain: float32 [5376], replicated, may hold values from 0.1 to 1.9
- pre_gain: float32 [5376], replicated, may hold values from 0.1 to 1.9
- proj_query: bfloat16 [5376, 4096], P('ctx', 'heads'), may hold values from -30 to 30
- key_projection: bfloat16 [5376, 2048], P('ctx', 'heads'), may hold values from -1 to 1
- value_projection: bfloat16 [5376, 2048], P('ctx', 'heads'), may hold values from -0.078125 to 0.078125
- window: int32 [32], P('heads'), may hold values from 512 to 1024, as said below
- positions: int32 [4096], replicated, may hold values from 0 to 2047, as said below
Outputs:
- resid_out: bfloat16 [4096, 5376], P('ctx', 'heads')
- attended: bfloat16 [4096, 4096], P('ctx', 'heads')
Inputs may be any that keep to these rules, and one draw needn't show every extreme that they name: Each query head's window counts back from and includes its own token; some head's window is exactly 1024. `positions`: tokens form three packed documents: a position is 0 at a document's first token and one more than the previous token's otherwise; one document has exactly 2048 tokens and none has more.
All inputs are finite; a program needn't handle non-finite values.
Results may differ from a plain program's by a relative error of at most 0.03.
Values may be sent and summed in bfloat16 or wider, within the bound.
No kernel may reach another device: no remote copies, remote signals or barrier semaphores. Data moves between devices by JAX's collectives and lax.ppermute only.
A program may use at most 64 MiB of HBM per device.

v0:
```python
from functools import partial

import jax
import jax.numpy as jnp
from jax import lax
from jax.sharding import PartitionSpec as P

HEAD_SIZE = 128
LONGEST_WINDOW = 1024


SCALE = 168.0 ** (-0.5)
EPS = 1e-06
THETA = 1000000.0
POSITION_FACTOR = 0.125


def shifted(value, axis, steps):
    count = lax.axis_size(axis)
    leading, last = (max(0, -steps), min(count, count - steps))
    return lax.ppermute(value, axis, [(source, source + steps) for source in range(leading, last)])


def from_partner(block, axis, bit):
    count = lax.axis_size(axis)
    route = []
    for low in range(count):
        high = low | 1 << bit
        if high != low and high < count:
            route += [(low, high), (high, low)]
    return lax.ppermute(block, axis, route)


def apply_rotary(values, pos_rows, factor):
    half_dim = values.shape[-1] // 2
    speeds = THETA ** (-(jnp.arange(half_dim, dtype=jnp.float32) * 2.0 / values.shape[-1]))
    angles = (pos_rows.astype(jnp.float32) * factor)[:, None] * speeds[None, :]
    cosine = jnp.cos(angles)[:, None, :]
    sine_part = jnp.sin(angles)[:, None, :]
    front_half = values[..., :half_dim]
    back_half = values[..., half_dim:]
    return jnp.concatenate(
        [front_half * cosine - back_half * sine_part, back_half * cosine + front_half * sine_part],
        axis=-1,
    )


def lookup(position_table, tokens):
    return jnp.take(position_table, jnp.clip(tokens, 0, position_table.shape[0] - 1))


def zig_token(row_ids, tok_dev):
    half_rows = tok_dev // 2
    device_of = row_ids // tok_dev
    local_row = row_ids % tok_dev
    last_pair = 2 * lax.axis_size("ctx") - 1
    return jnp.where(
        local_row < half_rows,
        2 * device_of * half_rows + local_row,
        (last_pair - 2 * device_of) * half_rows + local_row - half_rows,
    )


def masked_attention(
    query_row_block,
    key_row_block,
    value_row_block,
    query_tok,
    key_tok,
    query_pos,
    key_pos,
    window_limits,
):
    scores = (
        jnp.einsum(
            "qagd,kad->qagk", query_row_block, key_row_block, preferred_element_type=jnp.float32
        )
        * SCALE
    )
    distance = query_tok[:, None] - key_tok[None, :]
    base_ok = (
        (distance >= 0)
        & (key_tok[None, :] >= 0)
        & (query_pos[:, None] - key_pos[None, :] == distance)
    )
    visible = base_ok[:, None, None, :] & (
        distance[:, None, None, :] < window_limits[None, :, :, None]
    )
    row_peak = jnp.max(jnp.where(visible, scores, -1e30), axis=-1, keepdims=True)
    lifted = jnp.where(visible, jnp.exp(scores - row_peak), 0.0)
    row_total = jnp.sum(lifted, axis=-1)
    mixed = jnp.einsum(
        "qagk,kad->qagd",
        lifted.astype(jnp.bfloat16),
        value_row_block,
        preferred_element_type=jnp.float32,
    )
    return (mixed / row_total[..., None]).astype(jnp.bfloat16)


def mirror(rows_block, mover):
    half_rows = rows_block.shape[0] // 2
    travel = rows_block[half_rows:]
    bit_count = lax.axis_size("ctx").bit_length() - 1
    for bit_index in range(bit_count):
        travel = mover(travel, bit_index)
    return jnp.concatenate([rows_block[:half_rows], travel], axis=0)


def project(residual_rows, pre_gain, proj_query, key_projection, value_projection, row_pos):
    row_count = residual_rows.shape[0]
    widened = residual_rows.astype(jnp.float32)
    normalized_rows = (
        pre_gain[None, :]
        * widened
        * lax.rsqrt(jnp.mean(widened * widened, axis=1, keepdims=True) + EPS)
    ).astype(jnp.bfloat16)
    query_heads = proj_query.shape[1] // HEAD_SIZE
    pair_heads = key_projection.shape[1] // HEAD_SIZE
    second_layer_query = (
        apply_rotary(
            jnp.dot(
                normalized_rows,
                lax.all_gather(proj_query, "ctx", axis=0, tiled=True),
                preferred_element_type=jnp.float32,
            ).reshape(row_count, query_heads, HEAD_SIZE),
            row_pos,
            POSITION_FACTOR,
        )
        .astype(jnp.bfloat16)
        .reshape(row_count, query_heads * HEAD_SIZE)
    )
    second_layer_key = (
        apply_rotary(
            jnp.dot(
                normalized_rows,
                lax.all_gather(key_projection, "ctx", axis=0, tiled=True),
                preferred_element_type=jnp.float32,
            ).reshape(row_count, pair_heads, HEAD_SIZE),
            row_pos,
            POSITION_FACTOR,
        )
        .astype(jnp.bfloat16)
        .reshape(row_count, pair_heads * HEAD_SIZE)
    )
    second_layer_value = jnp.dot(
        normalized_rows,
        lax.all_gather(value_projection, "ctx", axis=0, tiled=True),
        preferred_element_type=jnp.float32,
    ).astype(jnp.bfloat16)
    return (second_layer_query, second_layer_key, second_layer_value)


def attend_block(
    state, query_row_block, key_block, value_block, query_tok, query_pos, block_tok, block_pos
):
    row_peak, row_total, weighted = state
    scores = (
        jnp.einsum("qagd,kad->qagk", query_row_block, key_block, preferred_element_type=jnp.float32)
        * SCALE
    )
    distance = query_tok[:, None] - block_tok[None, :]
    visible = (distance >= 0) & (query_pos[:, None] - block_pos[None, :] == distance)
    visible = visible[:, None, None, :]
    new_peak = jnp.maximum(row_peak, jnp.max(jnp.where(visible, scores, -1e30), axis=-1))
    lifted = jnp.where(visible, jnp.exp(scores - new_peak[..., None]), 0.0)
    shrink = jnp.exp(row_peak - new_peak)
    row_total = row_total * shrink + jnp.sum(lifted, axis=-1)
    weighted = weighted * shrink[..., None] + jnp.einsum(
        "qagk,kad->qagd",
        lifted.astype(jnp.bfloat16),
        value_block,
        preferred_element_type=jnp.float32,
    )
    return (new_peak, row_total, weighted)


def keep_state(state):
    return state


def shards(
    resid_in,
    first_layer_queries,
    first_layer_keys,
    first_layer_values,
    out_one,
    post_gain,
    pre_gain,
    proj_query,
    key_projection,
    value_projection,
    window,
    positions,
):
    tok_dev = resid_in.shape[0]
    col_width = resid_in.shape[1]
    ctx_place = lax.axis_index("ctx")
    head_place = lax.axis_index("heads")
    query_heads = first_layer_queries.shape[1] // HEAD_SIZE
    pair_heads = first_layer_keys.shape[1] // HEAD_SIZE
    group_length = query_heads // pair_heads
    window_limits = window.reshape(pair_heads, group_length)
    own_pairs = jnp.stack([first_layer_keys, first_layer_values])
    reach_count = LONGEST_WINDOW // tok_dev
    pieces = [own_pairs]
    for section in range(reach_count):
        pieces = [shifted(own_pairs, "ctx", section + 1)] + pieces
    extended = jnp.concatenate(pieces, axis=1)
    key_span = extended.shape[1]
    local_tok = ctx_place * tok_dev + jnp.arange(tok_dev, dtype=jnp.int32)
    key_tok = (ctx_place - reach_count) * tok_dev + jnp.arange(key_span, dtype=jnp.int32)
    attend_one = masked_attention(
        first_layer_queries.reshape(tok_dev, pair_heads, group_length, HEAD_SIZE),
        extended[0].reshape(key_span, pair_heads, HEAD_SIZE),
        extended[1].reshape(key_span, pair_heads, HEAD_SIZE),
        local_tok,
        key_tok,
        lookup(positions, local_tok),
        lookup(positions, key_tok),
        window_limits,
    )
    attend_one = attend_one.reshape(tok_dev, query_heads * HEAD_SIZE)
    partial_rows = jnp.dot(attend_one, out_one, preferred_element_type=jnp.float32)
    mirror_tok = zig_token(ctx_place * tok_dev + jnp.arange(tok_dev, dtype=jnp.int32), tok_dev)
    mirror_pos = lookup(positions, mirror_tok)
    summed = lax.psum(partial_rows.astype(jnp.bfloat16), "heads").astype(jnp.float32)
    post_scaled = summed * lax.rsqrt(jnp.mean(summed * summed, axis=1, keepdims=True) + EPS)
    resid_full = lax.all_gather(resid_in, "heads", axis=1, tiled=True)
    residual_rows = (resid_full.astype(jnp.float32) + post_gain[None, :] * post_scaled).astype(
        jnp.bfloat16
    )
    resid_out = lax.dynamic_slice_in_dim(residual_rows, head_place * col_width, col_width, 1)
    second_layer_query, second_layer_key, second_layer_value = project(
        residual_rows,
        pre_gain,
        proj_query,
        key_projection,
        value_projection,
        lookup(positions, local_tok),
    )
    merged = jnp.concatenate([second_layer_query, second_layer_key, second_layer_value], axis=1)

    def move_proj(piece, bit_index):
        return from_partner(piece, "ctx", bit_index)

    merged = mirror(merged, move_proj)
    query_cols = query_heads * HEAD_SIZE
    pair_cols = pair_heads * HEAD_SIZE
    second_layer_query = merged[:, :query_cols]
    second_layer_key = merged[:, query_cols : query_cols + pair_cols]
    second_layer_value = merged[:, query_cols + pair_cols :]
    half_rows = tok_dev // 2
    queries = second_layer_query.reshape(tok_dev, pair_heads, group_length, HEAD_SIZE)
    query_parts = (queries[:half_rows], queries[half_rows:])
    tok_parts = (mirror_tok[:half_rows], mirror_tok[half_rows:])
    pos_parts = (mirror_pos[:half_rows], mirror_pos[half_rows:])
    pair_two = jnp.stack([second_layer_key, second_layer_value])

    def empty_state():
        return (
            jnp.full((half_rows, pair_heads, group_length), -1e30, jnp.float32),
            jnp.zeros((half_rows, pair_heads, group_length), jnp.float32),
            jnp.zeros((half_rows, pair_heads, group_length, HEAD_SIZE), jnp.float32),
        )

    start_state = (empty_state(), empty_state())
    piece = lax.all_gather(pair_two, "ctx", axis=1, tiled=True)
    piece_rows = piece.shape[1]
    unit_rows = 2 * tok_dev
    unit_count = piece_rows // unit_rows

    def one_unit(index, state):
        offset = index * unit_rows
        unit_block = lax.dynamic_slice_in_dim(piece, offset, unit_rows, 1)
        current = list(state)
        for key_half in range(unit_rows // half_rows):
            key_block = unit_block[0, key_half * half_rows : (key_half + 1) * half_rows].reshape(
                half_rows, pair_heads, HEAD_SIZE
            )
            value_block = unit_block[1, key_half * half_rows : (key_half + 1) * half_rows].reshape(
                half_rows, pair_heads, HEAD_SIZE
            )
            key_row_block = offset + key_half * half_rows + jnp.arange(half_rows, dtype=jnp.int32)
            block_tok = zig_token(key_row_block, tok_dev)
            block_pos = lookup(positions, block_tok)
            earliest = jnp.min(block_tok)
            for query_half in range(2):
                work = partial(
                    attend_block,
                    query_row_block=query_parts[query_half],
                    key_block=key_block,
                    value_block=value_block,
                    query_tok=tok_parts[query_half],
                    query_pos=pos_parts[query_half],
                    block_tok=block_tok,
                    block_pos=block_pos,
                )
                needed = earliest <= tok_parts[query_half][half_rows - 1]
                current[query_half] = lax.cond(needed, work, keep_state, current[query_half])
        return tuple(current)

    final_state = lax.fori_loop(0, unit_count, one_unit, start_state)
    front = final_state[0][2] / final_state[0][1][..., None]
    back = final_state[1][2] / final_state[1][1][..., None]
    attended = (
        jnp.concatenate([front, back], axis=0)
        .astype(jnp.bfloat16)
        .reshape(tok_dev, query_heads * HEAD_SIZE)
    )
    return (resid_out, attended)


def solution(mesh):
    placed = (
        P("ctx", "heads"),
        P("ctx", "heads"),
        P("ctx", "heads"),
        P("ctx", "heads"),
        P("heads", None),
        P(),
        P(),
        P("ctx", "heads"),
        P("ctx", "heads"),
        P("ctx", "heads"),
        P("heads"),
        P(),
    )
    return jax.shard_map(
        shards,
        mesh=mesh,
        in_specs=placed,
        out_specs=(P("ctx", "heads"), P("ctx", "heads")),
        check_vma=False,
    )
```

profile of v0, /device:TPU:2, one launch (start us, length us, event | category | flops | bytes accessed | tf_op | source)
XLA Modules:
  0.0 968.1 jit_solution(9957120319989894820)
XLA Ops:
  8.2 6.1 collective-permute-start
  14.3 8.0 collective-permute-start.1
  22.2 7.7 collective-permute-start.2
  30.0 5.4 collective-permute-start.3
  35.4 3.4 collective-permute-start.4
  40.6 6.5 gather_fusion.4
  50.8 6.6 collective-permute-start.6
  67.2 123.5 %all-reduce.2.cloned.1.call-done = bf16[128,5376]{1,0:T(8,128)(2,1)} async-done(((bf16[128,5376]{1,0:T(8,128)(2,1)}), bf16[128,5376]{1,0:T(8,128)(2,1)}) %all-reduce.2.cloned.1.call-update) | async-done | bytes 1376272 | tf_op jit(solution)/shard_map/psum | solution.py:227
  192.4 41.8 %all-gather.6.cloned.1.call-done = bf16[128,5376]{0,1:T(8,128)(2,1)} async-done(((bf16[128,336]{0,1:T(8,128)(2,1)}), bf16[128,5376]{0,1:T(8,128)(2,1)}) %all-gather.6.cloned.1.call-update) | async-done | bytes 1376272 | tf_op jit(solution)/shard_map/all_gather | solution.py:229
  236.8 3.8 fusion.130
  240.6 81.4 %all-gather.10.cloned.1.call-done = bf16[5376,128]{1,0:T(8,128)(2,1)} async-done(((bf16[168,128]{1,0:T(8,128)(2,1)}), bf16[5376,128]{1,0:T(8,128)(2,1)}) %all-gather.10.cloned.1.call-update) | async-done | bytes 1376272 | tf_op jit(solution)/shard_map/all_gather | solution.py:137
  324.7 80.3 %all-gather.12.cloned.1.call-done = bf16[5376,128]{1,0:T(8,128)(2,1)} async-done(((bf16[168,128]{1,0:T(8,128)(2,1)}), bf16[5376,128]{1,0:T(8,128)(2,1)}) %all-gather.12.cloned.1.call-update) | async-done | bytes 1376272 | tf_op jit(solution)/shard_map/all_gather | solution.py:148
  407.6 86.1 %all-gather.8.cloned.1.call-done = bf16[5376,256]{1,0:T(8,128)(2,1)} async-done(((bf16[168,256]{1,0:T(8,128)(2,1)}), bf16[5376,256]{1,0:T(8,128)(2,1)}) %all-gather.8.cloned.1.call-update) | async-done | bytes 2752528 | tf_op jit(solution)/shard_map/all_gather | solution.py:124
  493.7 3.4 fusion.164
  497.3 4.5 collective-permute-start.8
  501.9 4.6 collective-permute-done.8
  506.5 4.3 collective-permute-start.9
  510.8 7.9 collective-permute-done.9
  521.3 5.4 collective-permute-done.10
  528.6 10.0 %collective-permute-done.11 = bf16[64,512]{0,1:T(8,128)(2,1)S(1)} collective-permute-done((bf16[64,512]{0,1:T(8,128)(2,1)S(1)}, bf16[64,512]{0,1:T(8,128)(2,1)S(1)}, u32[]{:S(2)}, u32[]{:S(2)}) %collective-permute-start.11) | collective-permute-done | bytes 65568 | tf_op jit(solution)/shard_map/ppermute | solution.py:31
  538.6 4.0 collective-permute-start.12
  542.6 7.1 collective-permute-done.12
  553.8 75.9 %all-gather.14.cloned.1.call-done = bf16[2,4096,128]{1,2,0:T(8,128)(2,1)} async-done(((bf16[2,128,128]{1,2,0:T(8,128)(2,1)}), bf16[2,4096,128]{1,2,0:T(8,128)(2,1)}) %all-gather.14.cloned.1.call-update) | async-done | bytes 2097168 | tf_op jit(solution)/shard_map/all_gather | solution.py:268
  629.8 330.5 %while.26 = (s32[]{:T(128)}, f32[64,1,2]{0,2,1:T(2,128)S(1)}, f32[64,1,2]{0,2,1:T(2,128)S(1)}, f32[64,1,2,128]{3,0,2,1:T(8,128)S(1)}, f32[64,1,2]{0,2,1:T(2,128)...) while((s32[]{:T(128)}, f32[64,1,2]{0,2,1:T(2,128)S(1)}, ...), condition=%wide.region_42.45_spmd, body=%wide.region_5.44_spmd.sunk | while | flops 34610448 | bytes 3114491 | solution.py:303
  (1152 shorter events, 231.8 us)
Async XLA Ops:
  7.2 55.4 %copy-start = (bf16[256,5376]{1,0:T(8,128)(2,1)S(1)}, bf16[256,5376]{1,0:T(8,128)(2,1)}, u32[]{:S(2)}) copy-start(bf16[256,5376]{1,0:T(8,128)(2,1)} %param.38) | copy-start | bytes 8257540
  7.2 33.4 %copy-start.1 = (s32[4096]{0:T(1024)S(1)}, s32[4096]{0:T(1024)}, u32[]{:S(2)}) copy-start(s32[4096]{0:T(1024)} %param.45) | copy-start | bytes 49156
  7.2 183.5 %all-reduce.2.cloned.1.call-start = ((), (), s32[]{:S(2)}) async-start(), calls=%async_computation.1 | async-start | bytes 2752512 | tf_op jit(solution)/shard_map/psum | solution.py:227
  8.2 40.3 %collective-permute-start = (bf16[2,128,128]{2,1,0:T(8,128)(2,1)S(1)}, bf16[2,128,128]{2,1,0:T(8,128)(2,1)S(1)}, u32[]{:S(2)}, u32[]{:S(2)}) collective-permute-start(bf16[2,128,128]{2,1,0:T(8,128)(2,1)S(1)} %pad_maximum_fusion.2), channel_id=1, source_target_pairs={{0,128},{16,144},{32,160},{48,176},{64,192},{80,208},{96,224},{112... | collective-permute-start | bytes 196616 | tf_op jit(solution)/shard_map/ppermute | solution.py:21
  14.3 36.5 %collective-permute-start.1 = (bf16[2,128,128]{2,1,0:T(8,128)(2,1)S(1)}, bf16[2,128,128]{2,1,0:T(8,128)(2,1)S(1)}, u32[]{:S(2)}, u32[]{:S(2)}) collective-permute-start(bf16[2,128,128]{2,1,0:T(8,128)(2,1)S(1)} %pad_maximum_fusion.2), channel_id=1, source_target_pairs={{0,112},{16,128},{32,144},{48,160},{64,176},{80,192},{96,208},{112... | collective-permute-start | bytes 196616 | tf_op jit(solution)/shard_map/ppermute | solution.py:21
  22.2 35.1 %collective-permute-start.2 = (bf16[2,128,128]{2,1,0:T(8,128)(2,1)S(1)}, bf16[2,128,128]{2,1,0:T(8,128)(2,1)S(1)}, u32[]{:S(2)}, u32[]{:S(2)}) collective-permute-start(bf16[2,128,128]{2,1,0:T(8,128)(2,1)S(1)} %pad_maximum_fusion.2), channel_id=1, source_target_pairs={{0,96},{16,112},{32,128},{48,144},{64,160},{80,176},{96,192},{112,... | collective-permute-start | bytes 196616 | tf_op jit(solution)/shard_map/ppermute | solution.py:21
  30.0 28.7 %collective-permute-start.3 = (bf16[2,128,128]{2,1,0:T(8,128)(2,1)S(1)}, bf16[2,128,128]{2,1,0:T(8,128)(2,1)S(1)}, u32[]{:S(2)}, u32[]{:S(2)}) collective-permute-start(bf16[2,128,128]{2,1,0:T(8,128)(2,1)S(1)} %pad_maximum_fusion.2), channel_id=1, source_target_pairs={{0,80},{16,96},{32,112},{48,128},{64,144},{80,160},{96,176},{112,1... | collective-permute-start | bytes 196616 | tf_op jit(solution)/shard_map/ppermute | solution.py:21
  35.4 23.3 %collective-permute-start.4 = (bf16[2,128,128]{2,1,0:T(8,128)(2,1)S(1)}, bf16[2,128,128]{2,1,0:T(8,128)(2,1)S(1)}, u32[]{:S(2)}, u32[]{:S(2)}) collective-permute-start(bf16[2,128,128]{2,1,0:T(8,128)(2,1)S(1)} %pad_maximum_fusion.2), channel_id=1, source_target_pairs={{0,64},{16,80},{32,96},{48,112},{64,128},{80,144},{96,160},{112,17... | collective-permute-start | bytes 196616 | tf_op jit(solution)/shard_map/ppermute | solution.py:21
  47.1 14.0 %copy-start.5 = (s32[2]{0:T(128)S(1)}, s32[2]{0:T(128)}, u32[]{:S(2)}) copy-start(s32[2]{0:T(128)} %param.44) | copy-start | bytes 28
  48.5 10.3 %collective-permute-start.5 = (bf16[2,128,128]{2,1,0:T(8,128)(2,1)S(1)}, bf16[2,128,128]{2,1,0:T(8,128)(2,1)S(1)}, u32[]{:S(2)}, u32[]{:S(2)}) collective-permute-start(bf16[2,128,128]{2,1,0:T(8,128)(2,1)S(1)} %pad_maximum_fusion.2), channel_id=1, source_target_pairs={{0,48},{16,64},{32,80},{48,96},{64,112},{80,128},{96,144},{112,160... | collective-permute-start | bytes 196616 | tf_op jit(solution)/shard_map/ppermute | solution.py:21
  50.8 8.5 collective-permute-start.6
  57.4 3.7 collective-permute-start.7
  64.3 169.9 %all-gather.6.cloned.1.call-start = ((), (), s32[]{:S(2)}) async-start(), calls=%async_computation | async-start | bytes 1462272 | tf_op jit(solution)/shard_map/all_gather | solution.py:229
  65.1 256.9 %all-gather.10.cloned.1.call-start = ((), (), s32[]{:S(2)}) async-start(), calls=%async_computation.3 | async-start | bytes 1419264 | tf_op jit(solution)/shard_map/all_gather | solution.py:137
  65.8 339.2 %all-gather.12.cloned.1.call-start = ((), (), s32[]{:S(2)}) async-start(), calls=%async_computation.4 | async-start | bytes 1419264 | tf_op jit(solution)/shard_map/all_gather | solution.py:148
  66.4 427.3 %all-gather.8.cloned.1.call-start = ((), (), s32[]{:S(2)}) async-start(), calls=%async_computation.2 | async-start | bytes 2838528 | tf_op jit(solution)/shard_map/all_gather | solution.py:124
  67.0 562.7 %all-gather.14.cloned.1.call-start = ((), (), s32[]{:S(2)}) async-start(), calls=%async_computation.5 | async-start | bytes 2162688 | tf_op jit(solution)/shard_map/all_gather | solution.py:268
  192.4 44.4 %copy-start.4 = (f32[5376]{0:T(1024)S(1)}, f32[5376]{0:T(1024)}, u32[]{:S(2)}) copy-start(f32[5376]{0:T(1024)} %param.39) | copy-start | bytes 64516
  236.8 85.2 %copy-start.7 = (f32[5376]{0:T(1024)S(1)}, f32[5376]{0:T(1024)}, u32[]{:S(2)}) copy-start(f32[5376]{0:T(1024)} %param.40) | copy-start | bytes 64516
  497.3 9.2 collective-permute-start.8
  506.5 12.2 %collective-permute-start.9 = (bf16[64,512]{0,1:T(8,128)(2,1)S(1)}, bf16[64,512]{0,1:T(8,128)(2,1)S(1)}, u32[]{:S(2)}, u32[]{:S(2)}) collective-permute-start(bf16[64,512]{0,1:T(8,128)(2,1)S(1)} %collective-permute-done.8), channel_id=1, source_target_pairs={{0,32},{32,0},{16,48},{48,16},{64,96},{96,64},{80,112},{112,80},{1... | collective-permute-start | bytes 196616 | tf_op jit(solution)/shard_map/ppermute | solution.py:31
  518.7 8.0 collective-permute-start.10
  526.6 12.0 %collective-permute-start.11 = (bf16[64,512]{0,1:T(8,128)(2,1)S(1)}, bf16[64,512]{0,1:T(8,128)(2,1)S(1)}, u32[]{:S(2)}, u32[]{:S(2)}) collective-permute-start(bf16[64,512]{0,1:T(8,128)(2,1)S(1)} %collective-permute-done.10), channel_id=1, source_target_pairs={{0,128},{128,0},{16,144},{144,16},{32,160},{160,32},{48,176},{176,... | collective-permute-start | bytes 196616 | tf_op jit(solution)/shard_map/ppermute | solution.py:31
  538.6 11.1 %collective-permute-start.12 = (bf16[64,512]{0,1:T(8,128)(2,1)S(1)}, bf16[64,512]{0,1:T(8,128)(2,1)S(1)}, u32[]{:S(2)}, u32[]{:S(2)}) collective-permute-start(bf16[64,512]{0,1:T(8,128)(2,1)S(1)} %collective-permute-done.11), channel_id=1, source_target_pairs={{0,256},{256,0},{16,272},{272,16},{32,288},{288,32},{48,304},{304,... | collective-permute-start | bytes 196616 | tf_op jit(solution)/shard_map/ppermute | solution.py:31
  (3 other events, 42.0 us)
Sparse Core Ops, SparseCore 0:
  64.5 126.2 all-reduce.1
  192.9 41.3 all-gather.5
  237.5 84.5 all-gather.9
  325.1 79.9 all-gather.11
  408.1 85.5 all-gather.7
  550.6 79.0 all-gather.13
where the time goes:
time: 972 us; the launch traced here: 968 us
  waiting for transfers between devices  529 us (54%)
  loops' own time  173 us (18%)
  local copies, waits for them, and re-layouts  113 us (12%)
  starting transfers between devices  58.4 us (6%)
  other arithmetic  44 us (5%)
  matrix products  36.2 us (4%)
  between operations  14.7 us (2%)
    another operation x1, loops' own time, shards(): final_state = lax.fori_loop(0, unit_count, one_unit, start_state)  169 us
    psum x1, waiting for transfers between devices, shards(): lax.psum(partial_rows.astype(jnp.bfloat16), 'heads').astype(jnp.float32)  123 us
    all_gather x1, waiting for transfers between devices, project(): lax.all_gather(proj_query, 'ctx', axis=0, tiled=True)  86.1 us
    all_gather x1, waiting for transfers between devices, project(): lax.all_gather(key_projection, 'ctx', axis=0, tiled=True)  81.4 us
    all_gather x1, waiting for transfers between devices, project(): lax.all_gather(value_projection, 'ctx', axis=0, tiled=True)  80.3 us
    all_gather x1, waiting for transfers between devices, shards(): piece = lax.all_gather(pair_two, 'ctx', axis=1, tiled=True)  75.9 us
    gather x67, local copies, waits for them, and re-layouts, lookup(): jnp.take(position_table, jnp.clip(tokens, 0, position_table.shape[0] - 1))  58.9 us
    all_gather x1, waiting for transfers between devices, shards(): resid_full = lax.all_gather(resid_in, 'heads', axis=1, tiled=True)  41.8 us
  transfers between devices with their start and end apart: 19, of which 13 were waited for; matrix products, arithmetic and copies ran while one was open for 3% of the time, Pallas kernels for 0%

commit v1 on v0

v1 whole, which is shorter than its diff:
```python
from functools import partial

import jax
import jax.numpy as jnp
from jax import lax
from jax.experimental import pallas as pl
from jax.experimental.pallas import tpu as pltpu
from jax.sharding import PartitionSpec as P

HEAD_SIZE = 128
SCALE = 168.0 ** (-0.5)
EPS = 1e-06
THETA = 1000000.0
POSITION_FACTOR = 0.125
N_CTX = 32
N_HEADS = 16
Y_HI = 4
Z = 8
TOK = 128
HALF = 64
WIDTH = 5376
COLS = WIDTH // N_HEADS
SLAB = 5760
ROWS = TOK // N_HEADS
NEG = -1e30
Y_GROUPS = [[z * Y_HI + y for y in range(Y_HI)] for z in range(Z)]
Z_GROUPS = [[z * Y_HI + y for z in range(Z)] for y in range(Y_HI)]
VMEM_LIMIT = 48 * 1024 * 1024


def whole(memory_space=pltpu.VMEM):
    return pl.BlockSpec(memory_space=memory_space)


def fold_max(peak, part):
    for lane in range(0, part.shape[1], 128):
        peak = jnp.maximum(peak, part[:, lane : lane + 128])
    return peak


def fold_sum(total, part):
    for lane in range(0, part.shape[1], 128):
        total = total + part[:, lane : lane + 128]
    return total


def softmax_rows(query, chunks, low, high, scores):
    rows = query.shape[0]
    peak = jnp.full((rows, 128), NEG, jnp.float32)
    offset = 0
    for load, tokens in chunks:
        keys, _ = load()
        part = (
            lax.dot_general(
                query, keys, (((1,), (1,)), ((), ())), preferred_element_type=jnp.float32
            )
            * SCALE
        )
        width = part.shape[1]
        seen = (tokens >= low) & (tokens <= high)
        part = jnp.where(seen, part, NEG)
        scores[:, offset : offset + width] = part
        peak = fold_max(peak, part)
        offset += width
    top = jnp.max(peak, axis=1, keepdims=True)
    total = jnp.zeros((rows, 128), jnp.float32)
    mixed = jnp.zeros((rows, HEAD_SIZE), jnp.float32)
    offset = 0
    for load, tokens in chunks:
        _, values = load()
        width = values.shape[0]
        lifted = jnp.exp(scores[:, offset : offset + width] - top)
        total = fold_sum(total, lifted)
        mixed = mixed + jnp.dot(
            lifted.astype(jnp.bfloat16), values, preferred_element_type=jnp.float32
        )
        offset += width
    return mixed / jnp.sum(total, axis=1, keepdims=True)


def first_kernel(base, query, blocks, last, low, out_one, resid, sent, scores):
    place_z, place_y = base[0], base[1]
    start = (place_z * Y_HI + place_y) * TOK
    stacked = jnp.concatenate([query[:, :HEAD_SIZE], query[:, HEAD_SIZE:]], axis=0)
    lowest = low[...][:, :1]
    row = lax.broadcasted_iota(jnp.int32, (2 * TOK, 1), 0)
    high = start + lax.rem(row, TOK)
    lane = lax.broadcasted_iota(jnp.int32, (1, 2 * TOK), 1)
    pair = jnp.where(lane < TOK, lane, lane - (TOK + Y_HI * TOK))
    chunks = []
    for peer in range(Y_HI):
        newer = (place_z - jnp.where(peer > place_y, 1, 0)) * (Y_HI * TOK) + peer * TOK
        chunks.append(
            (
                lambda peer=peer: (
                    blocks[peer, :, :HEAD_SIZE],
                    blocks[peer, :, HEAD_SIZE:],
                ),
                newer + pair,
            )
        )
    chunks.append(
        (
            lambda: (last[:, :HEAD_SIZE], last[:, HEAD_SIZE:]),
            start - 2 * Y_HI * TOK + lane[:, :TOK],
        )
    )
    mixed = softmax_rows(stacked, chunks, lowest, high, scores).astype(jnp.bfloat16)
    attend = jnp.concatenate([mixed[:TOK], mixed[TOK:]], axis=1)
    step = 768
    for col in range(0, WIDTH, step):
        part = jnp.dot(attend, out_one[:, col : col + step], preferred_element_type=jnp.float32)
        sent[:, :, col : col + step] = part.reshape(N_HEADS, ROWS, step).astype(jnp.bfloat16)
    own = resid[...].astype(jnp.float32).reshape(N_HEADS, ROWS, COLS)
    sent[:, :, WIDTH : WIDTH + COLS] = own.astype(jnp.bfloat16)
    sent[:, :, WIDTH + COLS :] = jnp.zeros((N_HEADS, ROWS, SLAB - WIDTH - COLS), jnp.bfloat16)


def norm_kernel(got, post_gain, pre_gain, sent, rows, wide):
    combined = got[0, :, :WIDTH].astype(jnp.float32)
    for peer in range(1, N_HEADS):
        combined = combined + got[peer, :, :WIDTH].astype(jnp.float32)
    for peer in range(N_HEADS):
        rows[:, peer * COLS : (peer + 1) * COLS] = got[peer, :, WIDTH : WIDTH + COLS].astype(
            jnp.float32
        )
    scale = lax.rsqrt(jnp.mean(combined * combined, axis=1, keepdims=True) + EPS)
    resid = (rows[...] + post_gain[...] * (combined * scale)).astype(jnp.bfloat16)
    widened = resid.astype(jnp.float32)
    scale = lax.rsqrt(jnp.mean(widened * widened, axis=1, keepdims=True) + EPS)
    normed = (pre_gain[...] * widened * scale).astype(jnp.bfloat16)
    wide[...] = widened
    for peer in range(N_HEADS):
        sent[peer, :, :WIDTH] = normed
        sent[peer, :, WIDTH : WIDTH + COLS] = wide[:, peer * COLS : (peer + 1) * COLS].astype(
            jnp.bfloat16
        )
        sent[peer, :, WIDTH + COLS :] = jnp.zeros((ROWS, SLAB - WIDTH - COLS), jnp.bfloat16)


def project_kernel(got, weights, turn_cos, turn_sin, query, pair, total):
    step = pl.program_id(0)

    @pl.when(step == 0)
    def _():
        total[...] = jnp.zeros_like(total)

    rows = got[...].astype(jnp.float32).reshape(TOK, got.shape[2]).astype(jnp.bfloat16)
    total[...] += jnp.dot(rows, weights[...], preferred_element_type=jnp.float32)

    @pl.when(step == pl.num_programs(0) - 1)
    def _():
        for head in range(4):
            values = total[:, head * HEAD_SIZE : (head + 1) * HEAD_SIZE]
            if head < 3:
                values = values * turn_cos[...] + pltpu.roll(values, HALF, 1) * turn_sin[...]
            values = values.astype(jnp.bfloat16)
            if head < 2:
                query[:, head * HEAD_SIZE : (head + 1) * HEAD_SIZE] = values
            else:
                pair[:, (head - 2) * HEAD_SIZE : (head - 1) * HEAD_SIZE] = values


SPAN = 2304
CHUNK = 256


def second_kernel(base, query, pair, low, out, scores):
    for part in range(2):
        first = base[part]
        begin = jnp.clip(lax.div(first, TOK) * TOK + TOK - SPAN, 0, N_CTX * TOK - SPAN)
        begin = pl.multiple_of(begin, TOK)
        block = query[part * HALF : (part + 1) * HALF, :]
        stacked = jnp.concatenate([block[:, :HEAD_SIZE], block[:, HEAD_SIZE:]], axis=0)
        lowest = low[part * TOK : (part + 1) * TOK, :1]
        row = lax.broadcasted_iota(jnp.int32, (TOK, 1), 0)
        high = first + lax.rem(row, HALF)
        lane = lax.broadcasted_iota(jnp.int32, (1, CHUNK), 1)
        chunks = []
        for index in range(SPAN // CHUNK):
            at = pl.multiple_of(begin + index * CHUNK, TOK)
            chunks.append(
                (
                    lambda at=at: (
                        pair[pl.ds(at, CHUNK), :HEAD_SIZE],
                        pair[pl.ds(at, CHUNK), HEAD_SIZE:],
                    ),
                    at + lane,
                )
            )
        mixed = softmax_rows(stacked, chunks, lowest, high, scores).astype(jnp.bfloat16)
        out[part * HALF : (part + 1) * HALF, :] = jnp.concatenate(
            [mixed[:HALF], mixed[HALF:]], axis=1
        )


def exchange_heads(value):
    return lax.all_to_all(value, "heads", 0, 0, tiled=True)


def ctx_shift(value, steps):
    return lax.ppermute(value, "ctx", [(i, (i + steps) % N_CTX) for i in range(N_CTX)])


def shards(
    resid_in,
    first_layer_queries,
    first_layer_keys,
    first_layer_values,
    out_one,
    post_gain,
    pre_gain,
    proj_query,
    key_projection,
    value_projection,
    window,
    positions,
):
    ctx_place = lax.axis_index("ctx").astype(jnp.int32)
    place_z, place_y = ctx_place // Y_HI, ctx_place % Y_HI
    bf16, f32 = jnp.bfloat16, jnp.float32
    params = partial(pltpu.CompilerParams, vmem_limit_bytes=VMEM_LIMIT)

    weights = lax.all_gather(
        jnp.concatenate([proj_query, key_projection, value_projection], axis=1),
        "ctx",
        axis=0,
        tiled=True,
    )

    own = jnp.concatenate([first_layer_keys, first_layer_values], axis=1)
    back_one = ctx_shift(own, Y_HI)
    back_two = ctx_shift(own, 2 * Y_HI)
    later = jnp.concatenate([own, back_one], axis=0)
    earlier = jnp.concatenate([back_one, back_two], axis=0)
    peers = jnp.arange(Y_HI, dtype=jnp.int32)[:, None, None]
    blocks = lax.all_to_all(
        jnp.where(peers >= place_y, later[None], earlier[None]),
        "ctx",
        0,
        0,
        tiled=True,
        axis_index_groups=Y_GROUPS,
    )

    start = ctx_place * TOK
    tokens = start + jnp.arange(TOK, dtype=jnp.int32)
    local_pos = lax.dynamic_slice_in_dim(positions, start, TOK, 0)
    low_one = jnp.maximum((tokens - local_pos)[None, :], tokens[None, :] - window[:, None] + 1)
    low_one = jnp.broadcast_to(low_one.reshape(2 * TOK, 1), (2 * TOK, 128))
    sent = pl.pallas_call(
        first_kernel,
        out_shape=jax.ShapeDtypeStruct((N_HEADS, ROWS, SLAB), bf16),
        in_specs=[whole(pltpu.SMEM)] + [whole()] * 6,
        out_specs=whole(),
        scratch_shapes=[pltpu.VMEM((2 * TOK, 9 * TOK), f32)],
        compiler_params=params(),
        cost_estimate=pl.CostEstimate(
            flops=600_000_000, bytes_accessed=6_000_000, transcendentals=300_000
        ),
        name="first_layer",
    )(
        jnp.stack([place_z, place_y]),
        first_layer_queries,
        blocks,
        back_two,
        low_one,
        out_one,
        resid_in,
    )
    got = exchange_heads(sent)
    sent = pl.pallas_call(
        norm_kernel,
        out_shape=jax.ShapeDtypeStruct((N_HEADS, ROWS, SLAB), bf16),
        in_specs=[whole()] * 3,
        out_specs=whole(),
        scratch_shapes=[pltpu.VMEM((ROWS, WIDTH), f32)] * 2,
        compiler_params=params(),
        name="norms",
    )(got, post_gain[None, :], pre_gain[None, :])
    got = exchange_heads(sent)
    resid_out = got[:, :, WIDTH : WIDTH + COLS].reshape(TOK, COLS)

    speeds = THETA ** (-(jnp.arange(HALF, dtype=f32) * 2.0 / HEAD_SIZE))
    angles = (local_pos.astype(f32) * POSITION_FACTOR)[:, None] * speeds[None, :]
    cosine, sine = jnp.cos(angles), jnp.sin(angles)
    turn_cos = jnp.concatenate([cosine, cosine], axis=1)
    turn_sin = jnp.concatenate([-sine, sine], axis=1)
    depth = 896
    query, pair = pl.pallas_call(
        project_kernel,
        out_shape=(
            jax.ShapeDtypeStruct((TOK, 2 * HEAD_SIZE), bf16),
            jax.ShapeDtypeStruct((TOK, 2 * HEAD_SIZE), bf16),
        ),
        grid=(WIDTH // depth,),
        in_specs=[
            pl.BlockSpec((N_HEADS, ROWS, depth), lambda k: (0, 0, k)),
            pl.BlockSpec((depth, 4 * HEAD_SIZE), lambda k: (k, 0)),
            pl.BlockSpec((TOK, HEAD_SIZE), lambda k: (0, 0)),
            pl.BlockSpec((TOK, HEAD_SIZE), lambda k: (0, 0)),
        ],
        out_specs=(
            pl.BlockSpec((TOK, 2 * HEAD_SIZE), lambda k: (0, 0)),
            pl.BlockSpec((TOK, 2 * HEAD_SIZE), lambda k: (0, 0)),
        ),
        scratch_shapes=[pltpu.VMEM((TOK, 4 * HEAD_SIZE), f32)],
        compiler_params=params(),
        name="project",
    )(got, weights, turn_cos, turn_sin)

    row_pairs = lax.all_to_all(
        jnp.broadcast_to(pair[None], (Y_HI, TOK, 2 * HEAD_SIZE)),
        "ctx",
        0,
        0,
        tiled=True,
        axis_index_groups=Y_GROUPS,
    ).reshape(Y_HI * TOK, 2 * HEAD_SIZE)
    all_pairs = lax.all_gather(row_pairs, "ctx", axis=0, tiled=True, axis_index_groups=Z_GROUPS)
    moved = lax.ppermute(query[HALF:], "ctx", [(i, N_CTX - 1 - i) for i in range(N_CTX)])
    query = jnp.concatenate([query[:HALF], moved], axis=0)

    second = (2 * N_CTX - 1 - 2 * ctx_place) * HALF
    firsts = jnp.stack([start, second])
    both = (firsts[:, None] + jnp.arange(HALF, dtype=jnp.int32)[None, :])
    pos_both = jnp.stack(
        [
            lax.dynamic_slice_in_dim(positions, start, HALF, 0),
            lax.dynamic_slice_in_dim(positions, second, HALF, 0),
        ]
    )
    low_two = jnp.broadcast_to((both - pos_both)[:, None, :], (2, 2, HALF)).reshape(2 * TOK, 1)
    low_two = jnp.broadcast_to(low_two, (2 * TOK, 128))
    attended = pl.pallas_call(
        second_kernel,
        out_shape=jax.ShapeDtypeStruct((TOK, 2 * HEAD_SIZE), bf16),
        in_specs=[whole(pltpu.SMEM)] + [whole()] * 3,
        out_specs=whole(),
        scratch_shapes=[pltpu.VMEM((TOK, SPAN), f32)],
        compiler_params=params(),
        name="second_layer",
    )(firsts, query, all_pairs, low_two)
    return (resid_out, attended)


def solution(mesh):
    placed = (
        P("ctx", "heads"),
        P("ctx", "heads"),
        P("ctx", "heads"),
        P("ctx", "heads"),
        P("heads", None),
        P(),
        P(),
        P("ctx", "heads"),
        P("ctx", "heads"),
        P("ctx", "heads"),
        P("heads"),
        P(),
    )
    return jax.shard_map(
        shards,
        mesh=mesh,
        in_specs=placed,
        out_specs=(P("ctx", "heads"), P("ctx", "heads")),
        check_vma=False,
    )
```

time: 972 us -> 222 us (0.23)
  the two profiles are of different devices: /device:TPU:2 before, /device:TPU:8 now
where the time goes in v1:
time: 222 us; the launch traced here: 221 us
  waiting for transfers between devices  136 us (61%)
  starting transfers between devices  32.7 us (15%)
  blocking collectives  14.9 us (7%)
  between operations  14.2 us (6%)
  Pallas kernels  12.7 us (6%)
  local copies, waits for them, and re-layouts  6.15 us (3%)
  other arithmetic  4.79 us (2%)
    all_to_all x2, waiting for transfers between devices, exchange_heads(): return lax.all_to_all(value, 'heads', 0, 0, tiled=True)  73.3 us
    all_gather x1, waiting for transfers between devices, shards(): lax.all_gather(row_pairs, 'ctx', axis=0, tiled=True, axis_index_groups=Z_...  27.5 us
    all_to_all x1, waiting for transfers between devices, shards(): lax.all_to_all(jnp.where(peers >= place_y, later[None], earlier[None]), '...  14.9 us
    all_to_all x1, blocking collectives, shards(): lax.all_to_all(jnp.broadcast_to(pair[None], (Y_HI, TOK, 2 * HEAD_SIZE)),...  14.9 us
    all_to_all x2, starting transfers between devices, exchange_heads(): return lax.all_to_all(value, 'heads', 0, 0, tiled=True)  12.2 us
    ppermute x2, starting transfers between devices, ctx_shift(): lax.ppermute(value, 'ctx', [(i, (i + steps) % N_CTX) for i in range(N_CTX)])  10.4 us
    all_gather x1, waiting for transfers between devices, shards(): lax.all_gather(jnp.concatenate([proj_query, key_projection, value_project...  9.42 us
    all_to_all x1, starting transfers between devices, shards(): lax.all_to_all(jnp.where(peers >= place_y, later[None], earlier[None]), '...  6.19 us
  transfers between devices with their start and end apart: 8, of which 8 were waited for; matrix products, arithmetic and copies ran while one was open for 3% of the time, Pallas kernels for 2%

profile of v1, /device:TPU:8, one launch (start us, length us, event | category | flops | bytes accessed | tf_op | source)
XLA Modules:
  0.0 221.5 jit_solution(6846425375029391850)
XLA Ops:
  7.2 1.6 pad_maximum_fusion
  8.9 0.9 constant_dynamic-update-slice_fusion.1
  10.5 6.1 %collective-permute-start.1 = (bf16[128,256]{1,0:T(8,128)(2,1)S(1)}, bf16[128,256]{1,0:T(8,128)(2,1)S(1)}, u32[]{:S(2)}, u32[]{:S(2)}) collective-permute-start(bf16[128,256]{1,0:T(8,128)(2,1)S(1)} %constant_dynamic-update-slice_fusion), channel_id=1, source_target_pairs={{0,128},{16,144},{32,160},{48,176},{64,192},{80,208},{96,224},{112... | collective-permute-start | bytes 196616 | tf_op jit(solution)/shard_map/ppermute | solution.py:202
  16.6 4.3 %collective-permute-start = (bf16[128,256]{1,0:T(8,128)(2,1)S(1)}, bf16[128,256]{1,0:T(8,128)(2,1)S(1)}, u32[]{:S(2)}, u32[]{:S(2)}) collective-permute-start(bf16[128,256]{1,0:T(8,128)(2,1)S(1)} %constant_dynamic-update-slice_fusion), channel_id=1, source_target_pairs={{0,64},{16,80},{32,96},{48,112},{64,128},{80,144},{96,160},{112,17... | collective-permute-start | bytes 196616 | tf_op jit(solution)/shard_map/ppermute | solution.py:202
  21.0 2.8 %collective-permute-done.1.last = bf16[128,256]{1,0:T(8,128)(2,1)S(1)} collective-permute-done((bf16[128,256]{1,0:T(8,128)(2,1)S(1)}, bf16[128,256]{1,0:T(8,128)(2,1)S(1)}, u32[]{:S(2)}, u32[]{:S(2)}) %collective-permute-start.1) | collective-permute-done | bytes 65568 | tf_op jit(solution)/shard_map/ppermute | solution.py:202
  23.7 2.7 %collective-permute-done = bf16[128,256]{1,0:T(8,128)(2,1)S(1)} collective-permute-done((bf16[128,256]{1,0:T(8,128)(2,1)S(1)}, bf16[128,256]{1,0:T(8,128)(2,1)S(1)}, u32[]{:S(2)}, u32[]{:S(2)}) %collective-permute-start) | collective-permute-done | bytes 65568 | tf_op jit(solution)/shard_map/ppermute | solution.py:202
  26.4 0.9 broadcast_select_fusion
  27.3 6.2 %all-to-all-start = ((bf16[4,256,256]{2,1,0:T(8,128)(2,1)}), bf16[4,256,256]{2,1,0:T(8,128)(2,1)S(1)}, u32[]{:S(2)}, u32[]{:S(2)}) async-start(bf16[4,256,256]{2,1,0:T(8,128)(2,1)} %broadcast_select_fusion), calls=%async_computation | async-start | bytes 1048576 | tf_op jit(solution)/shard_map/all_to_all | solution.py:237
  33.5 1.0 copy.14.resid
  35.4 14.9 %all-to-all-done.blocks = bf16[4,256,256]{2,1,0:T(8,128)(2,1)S(1)} async-done(((bf16[4,256,256]{2,1,0:T(8,128)(2,1)}), bf16[4,256,256]{2,1,0:T(8,128)(2,1)S(1)}, u32[]{:S(2)}, u32[]{:S(2)}) %all-to-all-start) | async-done | bytes 524320 | tf_op jit(solution)/shard_map/all_to_all | solution.py:237
  50.4 3.1 %first_layer.1 = bf16[16,8,5760]{2,1,0:T(8,128)(2,1)} custom-call(s32[2]{0:T(128)S(1)} %pad_add_fusion.base, bf16[128,256]{1,0:T(8,128)(2,1)S(1)} %copy-done.2, bf16[4,256,256]{2,1,0:T(8,128)(2,1)S(1)} %all-to-all-done.blocks, bf16[128,256]{1,0:T(8,128)(2,1)S(1)} %collective-permute-done.1.last, s32[256,128]{1,0:T(8,128)S(1)} %broadcast_in_dim.41.low, ...), custom_call_target="tpu_custom_call" | custom-call | flops 600000000 | bytes 6000000 | tf_op jit(solution)/shard_map/first_layer/pallas_call | solution.py:251
  53.5 7.2 %all-to-all-start.1 = ((bf16[16,8,5760]{2,1,0:T(8,128)(2,1)}), bf16[16,8,5760]{2,1,0:T(8,128)(2,1)S(1)}, u32[]{:S(2)}, u32[]{:S(2)}) async-start(bf16[16,8,5760]{2,1,0:T(8,128)(2,1)} %first_layer.1), calls=%async_computation.1 | async-start | bytes 2949120 | tf_op jit(solution)/shard_map/all_to_all | solution.py:198
  60.7 19.7 %all-to-all-done.1.got = bf16[16,8,5760]{2,1,0:T(8,128)(2,1)S(1)} async-done(((bf16[16,8,5760]{2,1,0:T(8,128)(2,1)}), bf16[16,8,5760]{2,1,0:T(8,128)(2,1)S(1)}, u32[]{:S(2)}, u32[]{:S(2)}) %all-to-all-start.1) | async-done | bytes 1474592 | tf_op jit(solution)/shard_map/all_to_all | solution.py:198
  80.5 1.7 norms.1
  82.2 5.0 %all-to-all-start.2 = ((bf16[16,8,5760]{2,1,0:T(8,128)(2,1)}), bf16[16,8,5760]{2,1,0:T(8,128)(2,1)S(1)}, u32[]{:S(2)}, u32[]{:S(2)}) async-start(bf16[16,8,5760]{2,1,0:T(8,128)(2,1)} %norms.1), calls=%async_computation.2 | async-start | bytes 2949120 | tf_op jit(solution)/shard_map/all_to_all | solution.py:198
  88.4 53.6 %all-to-all-done.2.got = bf16[16,8,5760]{2,1,0:T(8,128)(2,1)S(1)} async-done(((bf16[16,8,5760]{2,1,0:T(8,128)(2,1)}), bf16[16,8,5760]{2,1,0:T(8,128)(2,1)S(1)}, u32[]{:S(2)}, u32[]{:S(2)}) %all-to-all-start.2) | async-done | bytes 1474592 | tf_op jit(solution)/shard_map/all_to_all | solution.py:198
  142.0 9.4 %all-gather.3.cloned.1.call-done.weights = bf16[5376,512]{1,0:T(8,128)(2,1)} async-done(((bf16[168,512]{1,0:T(8,128)(2,1)}), bf16[5376,512]{1,0:T(8,128)(2,1)}) %all-gather.3.cloned.1.call-update) | async-done | bytes 5505040 | tf_op jit(solution)/shard_map/all_gather | solution.py:224
  151.5 5.3 %project.1 = (bf16[128,256]{1,0:T(8,128)(2,1)S(1)}, bf16[128,256]{1,0:T(8,128)(2,1)S(1)}) custom-call(bf16[16,8,5760]{2,1,0:T(8,128)(2,1)S(1)} %all-to-all-done.2.got, bf16[5376,512]{1,0:T(8,128)(2,1)} %all-gather.3.cloned.1.call-done.weights, f32[128,128]{1,0:T(8,128)S(1)} %get-tuple-element.19.turn_cos, f32[128,128]{1,0:T(8,128)S(1)} %get-tuple-element.20.turn_sin), custom_call_target="tpu_custom_call" | custom-call | tf_op jit(solution)/shard_map/project/pallas_call | solution.py:290
  156.8 14.9 %all_to_all.20 = bf16[4,128,256]{2,1,0:T(8,128)(2,1)} all-to-all(bf16[4,128,256]{2,1,0:T(8,128)(2,1)S(1)} %broadcast_in_dim.70), channel_id=1, replica_groups={{0,16,32,48},{64,80,96,112},{128,144,160,176},{192,208,224,240},{256,27..., dimensions={0} | all-to-all | bytes 524288 | tf_op jit(solution)/shard_map/all_to_all | solution.py:312
  172.7 3.9 %collective-permute-start.2 = (bf16[64,256]{1,0:T(8,128)(2,1)S(1)}, bf16[64,256]{1,0:T(8,128)(2,1)S(1)}, u32[]{:S(2)}, u32[]{:S(2)}) collective-permute-start(bf16[64,256]{1,0:T(8,128)(2,1)S(1)} %get-tuple-element.9), channel_id=1, source_target_pairs={{0,496},{16,480},{32,464},{48,448},{64,432},{80,416},{96,400},{112... | collective-permute-start | bytes 98312 | tf_op jit(solution)/shard_map/ppermute | solution.py:321
  177.4 5.4 %collective-permute-done.2 = bf16[64,256]{1,0:T(8,128)(2,1)S(1)} collective-permute-done((bf16[64,256]{1,0:T(8,128)(2,1)S(1)}, bf16[64,256]{1,0:T(8,128)(2,1)S(1)}, u32[]{:S(2)}, u32[]{:S(2)}) %collective-permute-start.2) | collective-permute-done | bytes 32800 | tf_op jit(solution)/shard_map/ppermute | solution.py:321
  182.8 27.5 %all-gather.5.cloned.1.call-done.pair = bf16[4096,256]{1,0:T(8,128)(2,1)} async-done(((bf16[512,256]{1,0:T(8,128)(2,1)}), bf16[4096,256]{1,0:T(8,128)(2,1)}) %all-gather.5.cloned.1.call-update) | async-done | bytes 2097168 | tf_op jit(solution)/shard_map/all_gather | solution.py:320
  210.4 1.6 copy-done.1
  212.0 2.7 %second_layer.1 = bf16[128,256]{1,0:T(8,128)(2,1)} custom-call(s32[2]{0:T(128)S(1)} %pad_add_fusion.1.base, bf16[128,256]{1,0:T(8,128)(2,1)S(1)} %pad_maximum_fusion.5.query, bf16[4096,256]{1,0:T(8,128)(2,1)S(1)} %copy-done.1, s32[256,128]{1,0:T(8,128)S(1)} %broadcast_in_dim.73.low), custom_call_target="tpu_custom_call" | custom-call | tf_op jit(solution)/shard_map/second_layer/pallas_call | solution.py:335
  (39 shorter events, 5.0 us)
Async XLA Ops:
  7.2 144.3 %all-gather.3.cloned.1.call-start = ((), (), s32[]{:S(2)}) async-start(), calls=%async_computation.4 | async-start | bytes 5677056 | tf_op jit(solution)/shard_map/all_gather | solution.py:224
  8.8 26.5 %copy-start.5 = (s32[2]{0:T(128)S(1)}, s32[2]{0:T(128)}, u32[]{:S(2)}) copy-start(s32[2]{0:T(128)} %param.22) | copy-start | bytes 28
  8.8 41.5 %copy-start = (bf16[256,5376]{1,0:T(8,128)(2,1)S(1)}, bf16[256,5376]{1,0:T(8,128)(2,1)}, u32[]{:S(2)}) copy-start(bf16[256,5376]{1,0:T(8,128)(2,1)} %out_one.1) | copy-start | bytes 8257540
  8.8 41.6 %copy-start.2 = (bf16[128,256]{1,0:T(8,128)(2,1)S(1)}, bf16[128,256]{1,0:T(8,128)(2,1)}, u32[]{:S(2)}) copy-start(bf16[128,256]{1,0:T(8,128)(2,1)} %query.1) | copy-start | bytes 196612
  10.5 13.2 %collective-permute-start.1 = (bf16[128,256]{1,0:T(8,128)(2,1)S(1)}, bf16[128,256]{1,0:T(8,128)(2,1)S(1)}, u32[]{:S(2)}, u32[]{:S(2)}) collective-permute-start(bf16[128,256]{1,0:T(8,128)(2,1)S(1)} %constant_dynamic-update-slice_fusion), channel_id=1, source_target_pairs={{0,128},{16,144},{32,160},{48,176},{64,192},{80,208},{96,224},{112... | collective-permute-start | bytes 196616 | tf_op jit(solution)/shard_map/ppermute | solution.py:202
  16.6 9.7 %collective-permute-start = (bf16[128,256]{1,0:T(8,128)(2,1)S(1)}, bf16[128,256]{1,0:T(8,128)(2,1)S(1)}, u32[]{:S(2)}, u32[]{:S(2)}) collective-permute-start(bf16[128,256]{1,0:T(8,128)(2,1)S(1)} %constant_dynamic-update-slice_fusion), channel_id=1, source_target_pairs={{0,64},{16,80},{32,96},{48,112},{64,128},{80,144},{96,160},{112,17... | collective-permute-start | bytes 196616 | tf_op jit(solution)/shard_map/ppermute | solution.py:202
  27.3 23.0 %all-to-all-start = ((bf16[4,256,256]{2,1,0:T(8,128)(2,1)}), bf16[4,256,256]{2,1,0:T(8,128)(2,1)S(1)}, u32[]{:S(2)}, u32[]{:S(2)}) async-start(bf16[4,256,256]{2,1,0:T(8,128)(2,1)} %broadcast_select_fusion), calls=%async_computation | async-start | bytes 1048576 | tf_op jit(solution)/shard_map/all_to_all | solution.py:237
  53.5 7.2 %copy-start.3 = (f32[5376]{0:T(1024)S(1)}, f32[5376]{0:T(1024)}, u32[]{:S(2)}) copy-start(f32[5376]{0:T(1024)} %param.17) | copy-start | bytes 64516
  53.5 7.2 %copy-start.4 = (f32[5376]{0:T(1024)S(1)}, f32[5376]{0:T(1024)}, u32[]{:S(2)}) copy-start(f32[5376]{0:T(1024)} %param.18) | copy-start | bytes 64516
  53.5 27.0 %all-to-all-start.1 = ((bf16[16,8,5760]{2,1,0:T(8,128)(2,1)}), bf16[16,8,5760]{2,1,0:T(8,128)(2,1)S(1)}, u32[]{:S(2)}, u32[]{:S(2)}) async-start(bf16[16,8,5760]{2,1,0:T(8,128)(2,1)} %first_layer.1), calls=%async_computation.1 | async-start | bytes 2949120 | tf_op jit(solution)/shard_map/all_to_all | solution.py:198
  82.2 59.9 %all-to-all-start.2 = ((bf16[16,8,5760]{2,1,0:T(8,128)(2,1)}), bf16[16,8,5760]{2,1,0:T(8,128)(2,1)S(1)}, u32[]{:S(2)}, u32[]{:S(2)}) async-start(bf16[16,8,5760]{2,1,0:T(8,128)(2,1)} %norms.1), calls=%async_computation.2 | async-start | bytes 2949120 | tf_op jit(solution)/shard_map/all_to_all | solution.py:198
  87.2 123.1 %all-gather.5.cloned.1.call-start = ((), (), s32[]{:S(2)}) async-start(), calls=%async_computation.5 | async-start | bytes 2359296 | tf_op jit(solution)/shard_map/all_gather | solution.py:320
  172.7 10.0 %collective-permute-start.2 = (bf16[64,256]{1,0:T(8,128)(2,1)S(1)}, bf16[64,256]{1,0:T(8,128)(2,1)S(1)}, u32[]{:S(2)}, u32[]{:S(2)}) collective-permute-start(bf16[64,256]{1,0:T(8,128)(2,1)S(1)} %get-tuple-element.9), channel_id=1, source_target_pairs={{0,496},{16,480},{32,464},{48,448},{64,432},{80,416},{96,400},{112... | collective-permute-start | bytes 98312 | tf_op jit(solution)/shard_map/ppermute | solution.py:321
  210.4 1.6 copy-start.1
Sparse Core Ops, SparseCore 0:
  11.1 140.2 all-gather.2
  171.8 38.4 all-gather.4

commit v2 on v1

--- a/solution.py
+++ b/solution.py
@@ -6,6 +6,7 @@
 from jax.experimental import pallas as pl
 from jax.experimental.pallas import tpu as pltpu
 from jax.sharding import PartitionSpec as P
+
 
 HEAD_SIZE = 128
 SCALE = 168.0 ** (-0.5)
@@ -198,6 +199,18 @@
     return lax.all_to_all(value, "heads", 0, 0, tiled=True)
 
 
+def spread_rows(value):
+    rows, cols = value.shape
+    return lax.all_to_all(
+        jnp.broadcast_to(value[None], (Y_HI, rows, cols)),
+        "ctx",
+        0,
+        0,
+        tiled=True,
+        axis_index_groups=Y_GROUPS,
+    ).reshape(Y_HI * rows, cols)
+
+
 def ctx_shift(value, steps):
     return lax.ppermute(value, "ctx", [(i, (i + steps) % N_CTX) for i in range(N_CTX)])
 
@@ -221,26 +234,19 @@
     bf16, f32 = jnp.bfloat16, jnp.float32
     params = partial(pltpu.CompilerParams, vmem_limit_bytes=VMEM_LIMIT)
 
-    weights = lax.all_gather(
-        jnp.concatenate([proj_query, key_projection, value_projection], axis=1),
-        "ctx",
-        axis=0,
-        tiled=True,
-    )
-
     own = jnp.concatenate([first_layer_keys, first_layer_values], axis=1)
     back_one = ctx_shift(own, Y_HI)
     back_two = ctx_shift(own, 2 * Y_HI)
+    joined = jnp.concatenate([proj_query, key_projection, value_projection], axis=1)
+    weights = spread_rows(joined)
+    weights = lax.all_gather(weights, "ctx", axis=0, tiled=True, axis_index_groups=Z_GROUPS)
+
     later = jnp.concatenate([own, back_one], axis=0)
     earlier = jnp.concatenate([back_one, back_two], axis=0)
     peers = jnp.arange(Y_HI, dtype=jnp.int32)[:, None, None]
+    window_blocks = jnp.where(peers >= place_y, later[None], earlier[None])
     blocks = lax.all_to_all(
-        jnp.where(peers >= place_y, later[None], earlier[None]),
-        "ctx",
-        0,
-        0,
-        tiled=True,
-        axis_index_groups=Y_GROUPS,
+        window_blocks, "ctx", 0, 0, tiled=True, axis_index_groups=Y_GROUPS
     )
 
     start = ctx_place * TOK
@@ -309,14 +315,7 @@
         name="project",
     )(got, weights, turn_cos, turn_sin)
 
-    row_pairs = lax.all_to_all(
-        jnp.broadcast_to(pair[None], (Y_HI, TOK, 2 * HEAD_SIZE)),
-        "ctx",
-        0,
-        0,
-        tiled=True,
-        axis_index_groups=Y_GROUPS,
-    ).reshape(Y_HI * TOK, 2 * HEAD_SIZE)
+    row_pairs = spread_rows(pair)
     all_pairs = lax.all_gather(row_pairs, "ctx", axis=0, tiled=True, axis_index_groups=Z_GROUPS)
     moved = lax.ppermute(query[HALF:], "ctx", [(i, N_CTX - 1 - i) for i in range(N_CTX)])
     query = jnp.concatenate([query[:HALF], moved], axis=0)

time: 222 us -> 198 us (0.89)
  the two profiles are of different devices: /device:TPU:8 before, /device:TPU:2 now
where the time goes in v2:
time: 198 us; the launch traced here: 197 us
  waiting for transfers between devices  87.8 us (44%)
  blocking collectives  42.3 us (21%)
  starting transfers between devices  31.2 us (16%)
  between operations  14.3 us (7%)
  Pallas kernels  12.7 us (6%)
  local copies, waits for them, and re-layouts  4.55 us (2%)
  other arithmetic  4.14 us (2%)
    all_to_all x2, blocking collectives, spread_rows(): lax.all_to_all(jnp.broadcast_to(value[None], (Y_HI, rows, cols)), 'ctx',...  42.3 us
    all_to_all x2, waiting for transfers between devices, exchange_heads(): return lax.all_to_all(value, 'heads', 0, 0, tiled=True)  34.7 us
    all_gather x1, waiting for transfers between devices, shards(): lax.all_gather(row_pairs, 'ctx', axis=0, tiled=True, axis_index_groups=Z_...  31 us
    all_to_all x2, starting transfers between devices, exchange_heads(): return lax.all_to_all(value, 'heads', 0, 0, tiled=True)  13.2 us
    ppermute x2, starting transfers between devices, ctx_shift(): lax.ppermute(value, 'ctx', [(i, (i + steps) % N_CTX) for i in range(N_CTX)])  10.6 us
    all_to_all x1, waiting for transfers between devices, shards(): lax.all_to_all(window_blocks, 'ctx', 0, 0, tiled=True, axis_index_groups=...  10.3 us
    ppermute x2, waiting for transfers between devices, ctx_shift(): lax.ppermute(value, 'ctx', [(i, (i + steps) % N_CTX) for i in range(N_CTX)])  6.15 us
    ppermute x1, waiting for transfers between devices, shards(): lax.ppermute(query[HALF:], 'ctx', [(i, N_CTX - 1 - i) for i in range(N_CT...  5.54 us
  transfers between devices with their start and end apart: 8, of which 7 were waited for; matrix products, arithmetic and copies ran while one was open for 3% of the time, Pallas kernels for 2%

profile of v2, /device:TPU:2, one launch (start us, length us, event | category | flops | bytes accessed | tf_op | source)
XLA Modules:
  0.0 197.0 jit_solution(13650243598275666994)
XLA Ops:
  7.2 1.0 pad_maximum_fusion
  8.2 27.1 %all_to_all.25 = bf16[4,168,512]{2,1,0:T(8,128)(2,1)} all-to-all(bf16[4,168,512]{2,1,0:T(8,128)(2,1)S(1)} %broadcast_in_dim.46), channel_id=1, replica_groups={{0,16,32,48},{64,80,96,112},{128,144,160,176},{192,208,224,240},{256,27..., dimensions={0} | all-to-all | bytes 1376256 | tf_op jit(solution)/shard_map/all_to_all | solution.py:204
  35.4 4.5 %collective-permute-start = (bf16[128,256]{1,0:T(8,128)(2,1)S(1)}, bf16[128,256]{1,0:T(8,128)(2,1)S(1)}, u32[]{:S(2)}, u32[]{:S(2)}) collective-permute-start(bf16[128,256]{1,0:T(8,128)(2,1)S(1)} %constant_dynamic-update-slice_fusion), channel_id=1, source_target_pairs={{0,64},{16,80},{32,96},{48,112},{64,128},{80,144},{96,160},{112,17... | collective-permute-start | bytes 196616 | tf_op jit(solution)/shard_map/ppermute | solution.py:215
  40.0 6.1 %collective-permute-start.1 = (bf16[128,256]{1,0:T(8,128)(2,1)S(1)}, bf16[128,256]{1,0:T(8,128)(2,1)S(1)}, u32[]{:S(2)}, u32[]{:S(2)}) collective-permute-start(bf16[128,256]{1,0:T(8,128)(2,1)S(1)} %constant_dynamic-update-slice_fusion), channel_id=1, source_target_pairs={{0,128},{16,144},{32,160},{48,176},{64,192},{80,208},{96,224},{112... | collective-permute-start | bytes 196616 | tf_op jit(solution)/shard_map/ppermute | solution.py:215
  46.1 3.5 %collective-permute-done = bf16[128,256]{1,0:T(8,128)(2,1)S(1)} collective-permute-done((bf16[128,256]{1,0:T(8,128)(2,1)S(1)}, bf16[128,256]{1,0:T(8,128)(2,1)S(1)}, u32[]{:S(2)}, u32[]{:S(2)}) %collective-permute-start) | collective-permute-done | bytes 65568 | tf_op jit(solution)/shard_map/ppermute | solution.py:215
  49.6 2.7 %collective-permute-done.1.last = bf16[128,256]{1,0:T(8,128)(2,1)S(1)} collective-permute-done((bf16[128,256]{1,0:T(8,128)(2,1)S(1)}, bf16[128,256]{1,0:T(8,128)(2,1)S(1)}, u32[]{:S(2)}, u32[]{:S(2)}) %collective-permute-start.1) | collective-permute-done | bytes 65568 | tf_op jit(solution)/shard_map/ppermute | solution.py:215
  52.3 0.9 broadcast_select_fusion
  53.2 3.5 %all-to-all-start = ((bf16[4,256,256]{2,1,0:T(8,128)(2,1)}), bf16[4,256,256]{2,1,0:T(8,128)(2,1)S(1)}, u32[]{:S(2)}, u32[]{:S(2)}) async-start(bf16[4,256,256]{2,1,0:T(8,128)(2,1)} %broadcast_select_fusion), calls=%async_computation | async-start | bytes 1048576 | tf_op jit(solution)/shard_map/all_to_all | solution.py:248
  56.7 1.0 copy.14.resid
  58.6 10.3 %all-to-all-done.blocks = bf16[4,256,256]{2,1,0:T(8,128)(2,1)S(1)} async-done(((bf16[4,256,256]{2,1,0:T(8,128)(2,1)}), bf16[4,256,256]{2,1,0:T(8,128)(2,1)S(1)}, u32[]{:S(2)}, u32[]{:S(2)}) %all-to-all-start) | async-done | bytes 524320 | tf_op jit(solution)/shard_map/all_to_all | solution.py:248
  69.1 3.1 %first_layer.1 = bf16[16,8,5760]{2,1,0:T(8,128)(2,1)} custom-call(s32[2]{0:T(128)S(1)} %pad_add_fusion.base, bf16[128,256]{1,0:T(8,128)(2,1)S(1)} %copy-done.2, bf16[4,256,256]{2,1,0:T(8,128)(2,1)S(1)} %all-to-all-done.blocks, bf16[128,256]{1,0:T(8,128)(2,1)S(1)} %collective-permute-done.1.last, s32[256,128]{1,0:T(8,128)S(1)} %broadcast_in_dim.43.low, ...), custom_call_target="tpu_custom_call" | custom-call | flops 600000000 | bytes 6000000 | tf_op jit(solution)/shard_map/first_layer/pallas_call | solution.py:257
  72.1 6.4 %all-to-all-start.1 = ((bf16[16,8,5760]{2,1,0:T(8,128)(2,1)}), bf16[16,8,5760]{2,1,0:T(8,128)(2,1)S(1)}, u32[]{:S(2)}, u32[]{:S(2)}) async-start(bf16[16,8,5760]{2,1,0:T(8,128)(2,1)} %first_layer.1), calls=%async_computation.1 | async-start | bytes 2949120 | tf_op jit(solution)/shard_map/all_to_all | solution.py:199
  78.6 17.9 %all-to-all-done.1.got = bf16[16,8,5760]{2,1,0:T(8,128)(2,1)S(1)} async-done(((bf16[16,8,5760]{2,1,0:T(8,128)(2,1)}), bf16[16,8,5760]{2,1,0:T(8,128)(2,1)S(1)}, u32[]{:S(2)}, u32[]{:S(2)}) %all-to-all-start.1) | async-done | bytes 1474592 | tf_op jit(solution)/shard_map/all_to_all | solution.py:199
  96.5 1.7 norms.1
  98.2 6.8 %all-to-all-start.2 = ((bf16[16,8,5760]{2,1,0:T(8,128)(2,1)}), bf16[16,8,5760]{2,1,0:T(8,128)(2,1)S(1)}, u32[]{:S(2)}, u32[]{:S(2)}) async-start(bf16[16,8,5760]{2,1,0:T(8,128)(2,1)} %norms.1), calls=%async_computation.2 | async-start | bytes 2949120 | tf_op jit(solution)/shard_map/all_to_all | solution.py:199
  106.2 16.8 %all-to-all-done.2.got = bf16[16,8,5760]{2,1,0:T(8,128)(2,1)S(1)} async-done(((bf16[16,8,5760]{2,1,0:T(8,128)(2,1)}), bf16[16,8,5760]{2,1,0:T(8,128)(2,1)S(1)}, u32[]{:S(2)}, u32[]{:S(2)}) %all-to-all-start.2) | async-done | bytes 1474592 | tf_op jit(solution)/shard_map/all_to_all | solution.py:199
  123.0 5.3 %project.1 = (bf16[128,256]{1,0:T(8,128)(2,1)S(1)}, bf16[128,256]{1,0:T(8,128)(2,1)S(1)}) custom-call(bf16[16,8,5760]{2,1,0:T(8,128)(2,1)S(1)} %all-to-all-done.2.got, bf16[5376,512]{1,0:T(8,128)(2,1)} %all-gather.3.cloned.1.call-done.weights, f32[128,128]{1,0:T(8,128)S(1)} %get-tuple-element.19.turn_cos, f32[128,128]{1,0:T(8,128)S(1)} %get-tuple-element.20.turn_sin), custom_call_target="tpu_custom_call" | custom-call | tf_op jit(solution)/shard_map/project/pallas_call | solution.py:296
  128.3 15.3 %all_to_all.26 = bf16[4,128,256]{2,1,0:T(8,128)(2,1)} all-to-all(bf16[4,128,256]{2,1,0:T(8,128)(2,1)S(1)} %broadcast_in_dim.47), channel_id=1, replica_groups={{0,16,32,48},{64,80,96,112},{128,144,160,176},{192,208,224,240},{256,27..., dimensions={0} | all-to-all | bytes 524288 | tf_op jit(solution)/shard_map/all_to_all | solution.py:204
  143.7 0.8 dynamic-slice_bitcast_fusion.1
  144.6 3.8 %collective-permute-start.2 = (bf16[64,256]{1,0:T(8,128)(2,1)S(1)}, bf16[64,256]{1,0:T(8,128)(2,1)S(1)}, u32[]{:S(2)}, u32[]{:S(2)}) collective-permute-start(bf16[64,256]{1,0:T(8,128)(2,1)S(1)} %get-tuple-element.9), channel_id=1, source_target_pairs={{0,496},{16,480},{32,464},{48,448},{64,432},{80,416},{96,400},{112... | collective-permute-start | bytes 98312 | tf_op jit(solution)/shard_map/ppermute | solution.py:320
  149.2 5.5 %collective-permute-done.2 = bf16[64,256]{1,0:T(8,128)(2,1)S(1)} collective-permute-done((bf16[64,256]{1,0:T(8,128)(2,1)S(1)}, bf16[64,256]{1,0:T(8,128)(2,1)S(1)}, u32[]{:S(2)}, u32[]{:S(2)}) %collective-permute-start.2) | collective-permute-done | bytes 32800 | tf_op jit(solution)/shard_map/ppermute | solution.py:320
  154.8 31.0 %all-gather.5.cloned.1.call-done.pair = bf16[4096,256]{1,0:T(8,128)(2,1)} async-done(((bf16[512,256]{1,0:T(8,128)(2,1)}), bf16[4096,256]{1,0:T(8,128)(2,1)}) %all-gather.5.cloned.1.call-update) | async-done | bytes 2097168 | tf_op jit(solution)/shard_map/all_gather | solution.py:319
  185.9 1.6 copy-done.1
  187.5 2.7 %second_layer.1 = bf16[128,256]{1,0:T(8,128)(2,1)} custom-call(s32[2]{0:T(128)S(1)} %pad_add_fusion.1.base, bf16[128,256]{1,0:T(8,128)(2,1)S(1)} %pad_maximum_fusion.5.query, bf16[4096,256]{1,0:T(8,128)(2,1)S(1)} %copy-done.1, s32[256,128]{1,0:T(8,128)S(1)} %broadcast_in_dim.80.low), custom_call_target="tpu_custom_call" | custom-call | tf_op jit(solution)/shard_map/second_layer/pallas_call | solution.py:334
  (45 shorter events, 3.6 us)
Async XLA Ops:
  7.2 115.8 %all-gather.3.cloned.1.call-start = ((), (), s32[]{:S(2)}) async-start(), calls=%async_computation.5 | async-start | bytes 6193152 | tf_op jit(solution)/shard_map/all_gather | solution.py:242
  8.2 27.2 %copy-start.3 = (bf16[128,128]{1,0:T(8,128)(2,1)S(1)}, bf16[128,128]{1,0:T(8,128)(2,1)}, u32[]{:S(2)}) copy-start(bf16[128,128]{1,0:T(8,128)(2,1)} %param.14) | copy-start | bytes 98308
  8.2 27.2 %copy-start.4 = (bf16[128,128]{1,0:T(8,128)(2,1)S(1)}, bf16[128,128]{1,0:T(8,128)(2,1)}, u32[]{:S(2)}) copy-start(bf16[128,128]{1,0:T(8,128)(2,1)} %param.15) | copy-start | bytes 98308
  35.3 23.2 %copy-start.7 = (s32[2]{0:T(128)S(1)}, s32[2]{0:T(128)}, u32[]{:S(2)}) copy-start(s32[2]{0:T(128)} %param.22) | copy-start | bytes 28
  35.3 33.7 %copy-start.2 = (bf16[128,256]{1,0:T(8,128)(2,1)S(1)}, bf16[128,256]{1,0:T(8,128)(2,1)}, u32[]{:S(2)}) copy-start(bf16[128,256]{1,0:T(8,128)(2,1)} %query.1) | copy-start | bytes 196612
  35.4 33.7 %copy-start = (bf16[256,5376]{1,0:T(8,128)(2,1)S(1)}, bf16[256,5376]{1,0:T(8,128)(2,1)}, u32[]{:S(2)}) copy-start(bf16[256,5376]{1,0:T(8,128)(2,1)} %out_one.1) | copy-start | bytes 8257540
  35.4 14.2 %collective-permute-start = (bf16[128,256]{1,0:T(8,128)(2,1)S(1)}, bf16[128,256]{1,0:T(8,128)(2,1)S(1)}, u32[]{:S(2)}, u32[]{:S(2)}) collective-permute-start(bf16[128,256]{1,0:T(8,128)(2,1)S(1)} %constant_dynamic-update-slice_fusion), channel_id=1, source_target_pairs={{0,64},{16,80},{32,96},{48,112},{64,128},{80,144},{96,160},{112,17... | collective-permute-start | bytes 196616 | tf_op jit(solution)/shard_map/ppermute | solution.py:215
  40.0 12.3 %collective-permute-start.1 = (bf16[128,256]{1,0:T(8,128)(2,1)S(1)}, bf16[128,256]{1,0:T(8,128)(2,1)S(1)}, u32[]{:S(2)}, u32[]{:S(2)}) collective-permute-start(bf16[128,256]{1,0:T(8,128)(2,1)S(1)} %constant_dynamic-update-slice_fusion), channel_id=1, source_target_pairs={{0,128},{16,144},{32,160},{48,176},{64,192},{80,208},{96,224},{112... | collective-permute-start | bytes 196616 | tf_op jit(solution)/shard_map/ppermute | solution.py:215
  53.2 15.8 %all-to-all-start = ((bf16[4,256,256]{2,1,0:T(8,128)(2,1)}), bf16[4,256,256]{2,1,0:T(8,128)(2,1)S(1)}, u32[]{:S(2)}, u32[]{:S(2)}) async-start(bf16[4,256,256]{2,1,0:T(8,128)(2,1)} %broadcast_select_fusion), calls=%async_computation | async-start | bytes 1048576 | tf_op jit(solution)/shard_map/all_to_all | solution.py:248
  72.1 6.4 %copy-start.5 = (f32[5376]{0:T(1024)S(1)}, f32[5376]{0:T(1024)}, u32[]{:S(2)}) copy-start(f32[5376]{0:T(1024)} %param.17) | copy-start | bytes 64516
  72.1 6.4 %copy-start.6 = (f32[5376]{0:T(1024)S(1)}, f32[5376]{0:T(1024)}, u32[]{:S(2)}) copy-start(f32[5376]{0:T(1024)} %param.18) | copy-start | bytes 64516
  72.1 24.4 %all-to-all-start.1 = ((bf16[16,8,5760]{2,1,0:T(8,128)(2,1)}), bf16[16,8,5760]{2,1,0:T(8,128)(2,1)S(1)}, u32[]{:S(2)}, u32[]{:S(2)}) async-start(bf16[16,8,5760]{2,1,0:T(8,128)(2,1)} %first_layer.1), calls=%async_computation.1 | async-start | bytes 2949120 | tf_op jit(solution)/shard_map/all_to_all | solution.py:199
  98.2 24.8 %all-to-all-start.2 = ((bf16[16,8,5760]{2,1,0:T(8,128)(2,1)}), bf16[16,8,5760]{2,1,0:T(8,128)(2,1)S(1)}, u32[]{:S(2)}, u32[]{:S(2)}) async-start(bf16[16,8,5760]{2,1,0:T(8,128)(2,1)} %norms.1), calls=%async_computation.2 | async-start | bytes 2949120 | tf_op jit(solution)/shard_map/all_to_all | solution.py:199
  105.0 80.8 %all-gather.5.cloned.1.call-start = ((), (), s32[]{:S(2)}) async-start(), calls=%async_computation.6 | async-start | bytes 2359296 | tf_op jit(solution)/shard_map/all_gather | solution.py:319
  144.6 10.1 %collective-permute-start.2 = (bf16[64,256]{1,0:T(8,128)(2,1)S(1)}, bf16[64,256]{1,0:T(8,128)(2,1)S(1)}, u32[]{:S(2)}, u32[]{:S(2)}) collective-permute-start(bf16[64,256]{1,0:T(8,128)(2,1)S(1)} %get-tuple-element.9), channel_id=1, source_target_pairs={{0,496},{16,480},{32,464},{48,448},{64,432},{80,416},{96,400},{112... | collective-permute-start | bytes 98312 | tf_op jit(solution)/shard_map/ppermute | solution.py:320
  185.9 1.6 copy-start.1
Sparse Core Ops, SparseCore 0:
  35.5 70.8 all-gather.2
  143.7 42.0 all-gather.4

commit v3 on v2

--- a/solution.py
+++ b/solution.py
@@ -25,8 +25,10 @@
 ROWS = TOK // N_HEADS
 NEG = -1e30
 Y_GROUPS = [[z * Y_HI + y for y in range(Y_HI)] for z in range(Z)]
+GROUP = 16
+HALF_GROUPS = [list(range(GROUP)), list(range(GROUP, N_CTX))]
 Z_GROUPS = [[z * Y_HI + y for z in range(Z)] for y in range(Y_HI)]
-VMEM_LIMIT = 48 * 1024 * 1024
+VMEM_LIMIT = 24 * 1024 * 1024
 
 
 def whole(memory_space=pltpu.VMEM):
@@ -76,7 +78,8 @@
             lifted.astype(jnp.bfloat16), values, preferred_element_type=jnp.float32
         )
         offset += width
-    return mixed / jnp.sum(total, axis=1, keepdims=True)
+    total = jnp.sum(total, axis=1, keepdims=True)
+    return mixed / total, top + jnp.log(total)
 
 
 def first_kernel(base, query, blocks, last, low, out_one, resid, sent, scores):
@@ -106,7 +109,8 @@
             start - 2 * Y_HI * TOK + lane[:, :TOK],
         )
     )
-    mixed = softmax_rows(stacked, chunks, lowest, high, scores).astype(jnp.bfloat16)
+    mixed, _ = softmax_rows(stacked, chunks, lowest, high, scores)
+    mixed = mixed.astype(jnp.bfloat16)
     attend = jnp.concatenate([mixed[:TOK], mixed[TOK:]], axis=1)
     step = 768
     for col in range(0, WIDTH, step):
@@ -139,76 +143,143 @@
         sent[peer, :, WIDTH + COLS :] = jnp.zeros((ROWS, SLAB - WIDTH - COLS), jnp.bfloat16)
 
 
-def project_kernel(got, weights, turn_cos, turn_sin, query, pair, total):
-    step = pl.program_id(0)
-
-    @pl.when(step == 0)
-    def _():
-        total[...] = jnp.zeros_like(total)
-
-    rows = got[...].astype(jnp.float32).reshape(TOK, got.shape[2]).astype(jnp.bfloat16)
-    total[...] += jnp.dot(rows, weights[...], preferred_element_type=jnp.float32)
-
-    @pl.when(step == pl.num_programs(0) - 1)
-    def _():
-        for head in range(4):
-            values = total[:, head * HEAD_SIZE : (head + 1) * HEAD_SIZE]
-            if head < 3:
-                values = values * turn_cos[...] + pltpu.roll(values, HALF, 1) * turn_sin[...]
-            values = values.astype(jnp.bfloat16)
-            if head < 2:
-                query[:, head * HEAD_SIZE : (head + 1) * HEAD_SIZE] = values
-            else:
-                pair[:, (head - 2) * HEAD_SIZE : (head - 1) * HEAD_SIZE] = values
-
-
-SPAN = 2304
+def prepare_kernel(
+    keys, values, proj_query, key_projection, value_projection, own, spread, joined, in_sem, out_sem
+):
+    width = HEAD_SIZE
+    moves = [
+        pltpu.make_async_copy(source, target, in_sem.at[index])
+        for index, (source, target) in enumerate(
+            (
+                (proj_query, joined.at[:, : 2 * width]),
+                (key_projection, joined.at[:, 2 * width : 3 * width]),
+                (value_projection, joined.at[:, 3 * width :]),
+                (keys, own.at[:, :width]),
+                (values, own.at[:, width:]),
+            )
+        )
+    ]
+    for move in moves:
+        move.start()
+    for move in moves[:3]:
+        move.wait()
+    copies = [
+        pltpu.make_async_copy(joined, spread.at[peer], out_sem.at[peer]) for peer in range(Y_HI)
+    ]
+    for move in copies:
+        move.start()
+    for move in moves[3:] + copies:
+        move.wait()
+
+
+def project_kernel(
+    got, weights, turn_cos, turn_sin, query, pair, held, block, in_sem, out_sem
+):
+    depth = WIDTH // PARTS
+    spans = [slice(part * depth, (part + 1) * depth) for part in range(PARTS)]
+    moves = [
+        pltpu.make_async_copy(weights.at[span], held.at[span], in_sem.at[part])
+        for part, span in enumerate(spans)
+    ]
+    for move in moves:
+        move.start()
+    total = jnp.zeros((TOK, 4 * HEAD_SIZE), jnp.float32)
+    for move, span in zip(moves, spans):
+        rows = got[:, :, span].astype(jnp.float32).reshape(TOK, depth).astype(jnp.bfloat16)
+        move.wait()
+        total = total + jnp.dot(rows, held[span, :], preferred_element_type=jnp.float32)
+    for head in range(4):
+        values = total[:, head * HEAD_SIZE : (head + 1) * HEAD_SIZE]
+        if head < 3:
+            values = values * turn_cos[...] + pltpu.roll(values, HALF, 1) * turn_sin[...]
+        values = values.astype(jnp.bfloat16)
+        if head < 2:
+            query[:, head * HEAD_SIZE : (head + 1) * HEAD_SIZE] = values
+        else:
+            block[:, (head - 2) * HEAD_SIZE : (head - 1) * HEAD_SIZE] = values
+    moves = [pltpu.make_async_copy(block, pair.at[peer], out_sem.at[peer]) for peer in range(GROUP)]
+    for move in moves:
+        move.start()
+    for move in moves:
+        move.wait()
+
+
 CHUNK = 256
-
-
-def second_kernel(base, query, pair, low, out, scores):
-    for part in range(2):
-        first = base[part]
-        begin = jnp.clip(lax.div(first, TOK) * TOK + TOK - SPAN, 0, N_CTX * TOK - SPAN)
-        begin = pl.multiple_of(begin, TOK)
-        block = query[part * HALF : (part + 1) * HALF, :]
-        stacked = jnp.concatenate([block[:, :HEAD_SIZE], block[:, HEAD_SIZE:]], axis=0)
-        lowest = low[part * TOK : (part + 1) * TOK, :1]
-        row = lax.broadcasted_iota(jnp.int32, (TOK, 1), 0)
-        high = first + lax.rem(row, HALF)
-        lane = lax.broadcasted_iota(jnp.int32, (1, CHUNK), 1)
+PARTS = 7
+
+
+def three_terms(values):
+    terms = []
+    for _ in range(3):
+        term = values.astype(jnp.bfloat16).astype(jnp.float32)
+        terms.append(term)
+        values = values - term
+    return terms
+
+
+def second_kernel(base, own_query, other_query, pair, low, kept, kept_log, sent, scores):
+    lane = lax.broadcasted_iota(jnp.int32, (1, CHUNK), 1)
+    row = lax.broadcasted_iota(jnp.int32, (2 * TOK, 1), 0)
+    slot = lax.broadcasted_iota(jnp.int32, (HALF, HEAD_SIZE), 1)
+    for index, query in enumerate((own_query, other_query)):
+        stacked = jnp.concatenate([query[:, :HEAD_SIZE], query[:, HEAD_SIZE:]], axis=0)
+        lowest = low[index * TOK : (index + 1) * TOK, :1]
+        lowest = jnp.concatenate([lowest, lowest], axis=0)
+        high = base[1 + index] + lax.rem(row, TOK)
         chunks = []
-        for index in range(SPAN // CHUNK):
-            at = pl.multiple_of(begin + index * CHUNK, TOK)
+        for at in range(0, GROUP * TOK, CHUNK):
             chunks.append(
                 (
                     lambda at=at: (
-                        pair[pl.ds(at, CHUNK), :HEAD_SIZE],
-                        pair[pl.ds(at, CHUNK), HEAD_SIZE:],
+                        pair[at : at + CHUNK, :HEAD_SIZE],
+                        pair[at : at + CHUNK, HEAD_SIZE:],
                     ),
-                    at + lane,
+                    base[0] + at + lane,
                 )
             )
-        mixed = softmax_rows(stacked, chunks, lowest, high, scores).astype(jnp.bfloat16)
-        out[part * HALF : (part + 1) * HALF, :] = jnp.concatenate(
-            [mixed[:HALF], mixed[HALF:]], axis=1
-        )
+        mixed, logs = softmax_rows(stacked, chunks, lowest, high, scores)
+        for half in range(2):
+            rows = slice(half * HALF, (half + 1) * HALF)
+            pieces = [slice(half * HALF + head * TOK, (half + 1) * HALF + head * TOK) for head in range(2)]
+            if half == index:
+                for head in range(2):
+                    kept[rows, head * HEAD_SIZE : (head + 1) * HEAD_SIZE] = mixed[pieces[head]]
+                kept_log[rows, :] = jnp.where(slot < 3, logs[pieces[0]], logs[pieces[1]])
+            else:
+                packed = jnp.zeros((HALF, HEAD_SIZE), jnp.float32)
+                for head in range(2):
+                    sent[rows, head * HEAD_SIZE : (head + 1) * HEAD_SIZE] = mixed[
+                        pieces[head]
+                    ].astype(jnp.bfloat16)
+                    for place, term in enumerate(three_terms(logs[pieces[head]])):
+                        packed = jnp.where(slot == 3 * head + place, term, packed)
+                sent[rows, 2 * HEAD_SIZE :] = packed.astype(jnp.bfloat16)
+
+
+def combine_kernel(kept, kept_log, got, out):
+    packed = got[:, 2 * HEAD_SIZE :].astype(jnp.float32)
+    for head in range(2):
+        cols = slice(head * HEAD_SIZE, (head + 1) * HEAD_SIZE)
+        mine = kept_log[:, 3 * head : 3 * head + 1]
+        at = 3 * head
+        theirs = packed[:, at : at + 1] + packed[:, at + 1 : at + 2] + packed[:, at + 2 : at + 3]
+        top = jnp.maximum(mine, theirs)
+        mine = jnp.exp(mine - top)
+        theirs = jnp.exp(theirs - top)
+        mixed = kept[:, cols] * mine + got[:, cols].astype(jnp.float32) * theirs
+        out[:, cols] = (mixed / (mine + theirs)).astype(jnp.bfloat16)
 
 
 def exchange_heads(value):
     return lax.all_to_all(value, "heads", 0, 0, tiled=True)
 
 
-def spread_rows(value):
-    rows, cols = value.shape
-    return lax.all_to_all(
-        jnp.broadcast_to(value[None], (Y_HI, rows, cols)),
-        "ctx",
-        0,
-        0,
-        tiled=True,
-        axis_index_groups=Y_GROUPS,
-    ).reshape(Y_HI * rows, cols)
+def exchange_y(value):
+    return lax.all_to_all(value, "ctx", 0, 0, tiled=True, axis_index_groups=Y_GROUPS)
+
+
+def mirror(value):
+    return lax.ppermute(value, "ctx", [(i, N_CTX - 1 - i) for i in range(N_CTX)])
 
 
 def ctx_shift(value, steps):
@@ -234,20 +305,31 @@
     bf16, f32 = jnp.bfloat16, jnp.float32
     params = partial(pltpu.CompilerParams, vmem_limit_bytes=VMEM_LIMIT)
 
-    own = jnp.concatenate([first_layer_keys, first_layer_values], axis=1)
+    own, spread = pl.pallas_call(
+        prepare_kernel,
+        out_shape=(
+            jax.ShapeDtypeStruct((TOK, 2 * HEAD_SIZE), bf16),
+            jax.ShapeDtypeStruct((Y_HI, proj_query.shape[0], 4 * HEAD_SIZE), bf16),
+        ),
+        in_specs=[whole(pltpu.HBM)] * 5,
+        out_specs=(whole(), whole(pltpu.HBM)),
+        scratch_shapes=[
+            pltpu.VMEM((proj_query.shape[0], 4 * HEAD_SIZE), bf16),
+            pltpu.SemaphoreType.DMA((5,)),
+            pltpu.SemaphoreType.DMA((Y_HI,)),
+        ],
+        name="prepare",
+    )(first_layer_keys, first_layer_values, proj_query, key_projection, value_projection)
     back_one = ctx_shift(own, Y_HI)
     back_two = ctx_shift(own, 2 * Y_HI)
-    joined = jnp.concatenate([proj_query, key_projection, value_projection], axis=1)
-    weights = spread_rows(joined)
+    weights = exchange_y(spread).reshape(-1, 4 * HEAD_SIZE)
     weights = lax.all_gather(weights, "ctx", axis=0, tiled=True, axis_index_groups=Z_GROUPS)
 
     later = jnp.concatenate([own, back_one], axis=0)
     earlier = jnp.concatenate([back_one, back_two], axis=0)
     peers = jnp.arange(Y_HI, dtype=jnp.int32)[:, None, None]
     window_blocks = jnp.where(peers >= place_y, later[None], earlier[None])
-    blocks = lax.all_to_all(
-        window_blocks, "ctx", 0, 0, tiled=True, axis_index_groups=Y_GROUPS
-    )
+    blocks = exchange_y(window_blocks)
 
     start = ctx_place * TOK
     tokens = start + jnp.arange(TOK, dtype=jnp.int32)
@@ -292,54 +374,57 @@
     cosine, sine = jnp.cos(angles), jnp.sin(angles)
     turn_cos = jnp.concatenate([cosine, cosine], axis=1)
     turn_sin = jnp.concatenate([-sine, sine], axis=1)
-    depth = 896
     query, pair = pl.pallas_call(
         project_kernel,
         out_shape=(
             jax.ShapeDtypeStruct((TOK, 2 * HEAD_SIZE), bf16),
-            jax.ShapeDtypeStruct((TOK, 2 * HEAD_SIZE), bf16),
+            jax.ShapeDtypeStruct((GROUP, TOK, 2 * HEAD_SIZE), bf16),
         ),
-        grid=(WIDTH // depth,),
-        in_specs=[
-            pl.BlockSpec((N_HEADS, ROWS, depth), lambda k: (0, 0, k)),
-            pl.BlockSpec((depth, 4 * HEAD_SIZE), lambda k: (k, 0)),
-            pl.BlockSpec((TOK, HEAD_SIZE), lambda k: (0, 0)),
-            pl.BlockSpec((TOK, HEAD_SIZE), lambda k: (0, 0)),
+        in_specs=[whole(), whole(pltpu.HBM), whole(), whole()],
+        out_specs=(whole(), whole(pltpu.HBM)),
+        scratch_shapes=[
+            pltpu.VMEM((WIDTH, 4 * HEAD_SIZE), bf16),
+            pltpu.VMEM((TOK, 2 * HEAD_SIZE), bf16),
+            pltpu.SemaphoreType.DMA((PARTS,)),
+            pltpu.SemaphoreType.DMA((GROUP,)),
         ],
-        out_specs=(
-            pl.BlockSpec((TOK, 2 * HEAD_SIZE), lambda k: (0, 0)),
-            pl.BlockSpec((TOK, 2 * HEAD_SIZE), lambda k: (0, 0)),
-        ),
-        scratch_shapes=[pltpu.VMEM((TOK, 4 * HEAD_SIZE), f32)],
-        compiler_params=params(),
+        compiler_params=pltpu.CompilerParams(vmem_limit_bytes=52 * 1024 * 1024),
         name="project",
     )(got, weights, turn_cos, turn_sin)
 
-    row_pairs = spread_rows(pair)
-    all_pairs = lax.all_gather(row_pairs, "ctx", axis=0, tiled=True, axis_index_groups=Z_GROUPS)
-    moved = lax.ppermute(query[HALF:], "ctx", [(i, N_CTX - 1 - i) for i in range(N_CTX)])
-    query = jnp.concatenate([query[:HALF], moved], axis=0)
-
-    second = (2 * N_CTX - 1 - 2 * ctx_place) * HALF
-    firsts = jnp.stack([start, second])
-    both = (firsts[:, None] + jnp.arange(HALF, dtype=jnp.int32)[None, :])
-    pos_both = jnp.stack(
-        [
-            lax.dynamic_slice_in_dim(positions, start, HALF, 0),
-            lax.dynamic_slice_in_dim(positions, second, HALF, 0),
-        ]
-    )
-    low_two = jnp.broadcast_to((both - pos_both)[:, None, :], (2, 2, HALF)).reshape(2 * TOK, 1)
-    low_two = jnp.broadcast_to(low_two, (2 * TOK, 128))
-    attended = pl.pallas_call(
+    pairs = lax.all_to_all(
+        pair, "ctx", 0, 0, tiled=True, axis_index_groups=HALF_GROUPS
+    ).reshape(GROUP * TOK, 2 * HEAD_SIZE)
+    other_query = mirror(query)
+
+    other_start = (N_CTX - 1 - ctx_place) * TOK
+    other_pos = lax.dynamic_slice_in_dim(positions, other_start, TOK, 0)
+    other_tokens = other_start + jnp.arange(TOK, dtype=jnp.int32)
+    low_two = jnp.concatenate([tokens - local_pos, other_tokens - other_pos])
+    low_two = jnp.broadcast_to(low_two[:, None], (2 * TOK, 128))
+    bases = jnp.stack([(ctx_place // GROUP) * (GROUP * TOK), start, other_start])
+    kept, kept_log, sent = pl.pallas_call(
         second_kernel,
-        out_shape=jax.ShapeDtypeStruct((TOK, 2 * HEAD_SIZE), bf16),
-        in_specs=[whole(pltpu.SMEM)] + [whole()] * 3,
-        out_specs=whole(),
-        scratch_shapes=[pltpu.VMEM((TOK, SPAN), f32)],
+        out_shape=(
+            jax.ShapeDtypeStruct((TOK, 2 * HEAD_SIZE), f32),
+            jax.ShapeDtypeStruct((TOK, HEAD_SIZE), f32),
+            jax.ShapeDtypeStruct((TOK, 3 * HEAD_SIZE), bf16),
+        ),
+        in_specs=[whole(pltpu.SMEM)] + [whole()] * 4,
+        out_specs=(whole(), whole(), whole()),
+        scratch_shapes=[pltpu.VMEM((2 * TOK, GROUP * TOK), f32)],
         compiler_params=params(),
         name="second_layer",
-    )(firsts, query, all_pairs, low_two)
+    )(bases, query, other_query, pairs, low_two)
+    got = mirror(sent)
+    attended = pl.pallas_call(
+        combine_kernel,
+        out_shape=jax.ShapeDtypeStruct((TOK, 2 * HEAD_SIZE), bf16),
+        in_specs=[whole()] * 3,
+        out_specs=whole(),
+        compiler_params=params(),
+        name="combine",
+    )(kept, kept_log, got)
     return (resid_out, attended)
 
 

time: 198 us -> 196 us (0.990)
  the two profiles are of different devices: /device:TPU:2 before, /device:TPU:22 now
where the time goes in v3:
time: 196 us; the launch traced here: 195 us
  waiting for transfers between devices  89 us (45%)
  starting transfers between devices  42.2 us (22%)
  blocking collectives  26.1 us (13%)
  Pallas kernels  16.4 us (8%)
  between operations  14.2 us (7%)
  local copies, waits for them, and re-layouts  4.03 us (2%)
  other arithmetic  3.13 us (2%)
    all_to_all x2, waiting for transfers between devices, exchange_heads(): return lax.all_to_all(value, 'heads', 0, 0, tiled=True)  38.7 us
    ppermute x2, waiting for transfers between devices, mirror(): lax.ppermute(value, 'ctx', [(i, N_CTX - 1 - i) for i in range(N_CTX)])  34.1 us
    all_to_all x1, blocking collectives, exchange_y(): lax.all_to_all(value, 'ctx', 0, 0, tiled=True, axis_index_groups=Y_GROUPS)  26.1 us
    ppermute x2, starting transfers between devices, mirror(): lax.ppermute(value, 'ctx', [(i, N_CTX - 1 - i) for i in range(N_CTX)])  10.9 us
    all_to_all x1, waiting for transfers between devices, exchange_y(): lax.all_to_all(value, 'ctx', 0, 0, tiled=True, axis_index_groups=Y_GROUPS)  10.8 us
    ppermute x2, starting transfers between devices, ctx_shift(): lax.ppermute(value, 'ctx', [(i, (i + steps) % N_CTX) for i in range(N_CTX)])  10.6 us
    all_to_all x2, starting transfers between devices, exchange_heads(): return lax.all_to_all(value, 'heads', 0, 0, tiled=True)  9.77 us
    all_to_all x1, starting transfers between devices, shards(): lax.all_to_all(pair, 'ctx', 0, 0, tiled=True, axis_index_groups=HALF_GROUPS)  6.58 us
  transfers between devices with their start and end apart: 9, of which 7 were waited for; matrix products, arithmetic and copies ran while one was open for 3% of the time, Pallas kernels for 2%

profile of v3, /device:TPU:22, one launch (start us, length us, event | category | flops | bytes accessed | tf_op | source)
XLA Modules:
  0.0 195.1 jit_solution(10618528753286690919)
XLA Ops:
  7.2 2.5 %prepare.1 = (bf16[128,256]{1,0:T(8,128)(2,1)}, bf16[4,168,512]{2,1,0:T(8,128)(2,1)}) custom-call(bf16[128,128]{1,0:T(8,128)(2,1)} %keys.1, bf16[128,128]{1,0:T(8,128)(2,1)} %values.1, bf16[168,256]{1,0:T(8,128)(2,1)} %proj_query.1, bf16[168,128]{1,0:T(8,128)(2,1)} %key_projection.1, bf16[168,128]{1,0:T(8,128)(2,1)} %value_projection.1), custom_call_target="tpu_custom_call" | custom-call | tf_op jit(solution)/shard_map/prepare/pallas_call | solution.py:308
  9.7 26.1 %all_to_all.25 = bf16[4,168,512]{2,1,0:T(8,128)(2,1)} all-to-all(bf16[4,168,512]{2,1,0:T(8,128)(2,1)} %get-tuple-element.10), channel_id=1, replica_groups={{0,16,32,48},{64,80,96,112},{128,144,160,176},{192,208,224,240},{256,27..., dimensions={0} | all-to-all | bytes 1376256 | tf_op jit(solution)/shard_map/all_to_all | solution.py:278
  35.9 6.4 %collective-permute-start.1 = (bf16[128,256]{1,0:T(8,128)(2,1)S(1)}, bf16[128,256]{1,0:T(8,128)(2,1)S(1)}, u32[]{:S(2)}, u32[]{:S(2)}) collective-permute-start(bf16[128,256]{1,0:T(8,128)(2,1)S(1)} %copy-done.3), channel_id=1, source_target_pairs={{0,128},{16,144},{32,160},{48,176},{64,192},{80,208},{96,224},{112... | collective-permute-start | bytes 196616 | tf_op jit(solution)/shard_map/ppermute | solution.py:286
  42.2 4.3 %collective-permute-start = (bf16[128,256]{1,0:T(8,128)(2,1)S(1)}, bf16[128,256]{1,0:T(8,128)(2,1)S(1)}, u32[]{:S(2)}, u32[]{:S(2)}) collective-permute-start(bf16[128,256]{1,0:T(8,128)(2,1)S(1)} %copy-done.3), channel_id=1, source_target_pairs={{0,64},{16,80},{32,96},{48,112},{64,128},{80,144},{96,160},{112,17... | collective-permute-start | bytes 196616 | tf_op jit(solution)/shard_map/ppermute | solution.py:286
  46.5 2.8 %collective-permute-done.1.last = bf16[128,256]{1,0:T(8,128)(2,1)S(1)} collective-permute-done((bf16[128,256]{1,0:T(8,128)(2,1)S(1)}, bf16[128,256]{1,0:T(8,128)(2,1)S(1)}, u32[]{:S(2)}, u32[]{:S(2)}) %collective-permute-start.1) | collective-permute-done | bytes 65568 | tf_op jit(solution)/shard_map/ppermute | solution.py:286
  49.3 2.7 %collective-permute-done = bf16[128,256]{1,0:T(8,128)(2,1)S(1)} collective-permute-done((bf16[128,256]{1,0:T(8,128)(2,1)S(1)}, bf16[128,256]{1,0:T(8,128)(2,1)S(1)}, u32[]{:S(2)}, u32[]{:S(2)}) %collective-permute-start) | collective-permute-done | bytes 65568 | tf_op jit(solution)/shard_map/ppermute | solution.py:286
  52.9 4.3 %all-to-all-start = ((bf16[4,256,256]{2,1,0:T(8,128)(2,1)}), bf16[4,256,256]{2,1,0:T(8,128)(2,1)S(1)}, u32[]{:S(2)}, u32[]{:S(2)}) async-start(bf16[4,256,256]{2,1,0:T(8,128)(2,1)} %broadcast_select_fusion), calls=%async_computation | async-start | bytes 1048576 | tf_op jit(solution)/shard_map/all_to_all | solution.py:278
  57.2 1.0 copy.14.resid
  59.2 10.8 %all-to-all-done.blocks = bf16[4,256,256]{2,1,0:T(8,128)(2,1)S(1)} async-done(((bf16[4,256,256]{2,1,0:T(8,128)(2,1)}), bf16[4,256,256]{2,1,0:T(8,128)(2,1)S(1)}, u32[]{:S(2)}, u32[]{:S(2)}) %all-to-all-start) | async-done | bytes 524320 | tf_op jit(solution)/shard_map/all_to_all | solution.py:278
  70.1 3.1 %first_layer.1 = bf16[16,8,5760]{2,1,0:T(8,128)(2,1)} custom-call(s32[2]{0:T(128)S(1)} %pad_add_fusion.1.base, bf16[128,256]{1,0:T(8,128)(2,1)S(1)} %copy-done.1, bf16[4,256,256]{2,1,0:T(8,128)(2,1)S(1)} %all-to-all-done.blocks, bf16[128,256]{1,0:T(8,128)(2,1)S(1)} %collective-permute-done.1.last, s32[256,128]{1,0:T(8,128)S(1)} %broadcast_in_dim.52.low, ...), custom_call_target="tpu_custom_call" | custom-call | flops 600000000 | bytes 6000000 | tf_op jit(solution)/shard_map/first_layer/pallas_call | solution.py:339
  73.2 4.9 %all-to-all-start.1 = ((bf16[16,8,5760]{2,1,0:T(8,128)(2,1)}), bf16[16,8,5760]{2,1,0:T(8,128)(2,1)S(1)}, u32[]{:S(2)}, u32[]{:S(2)}) async-start(bf16[16,8,5760]{2,1,0:T(8,128)(2,1)} %first_layer.1), calls=%async_computation.1 | async-start | bytes 2949120 | tf_op jit(solution)/shard_map/all_to_all | solution.py:274
  78.1 19.9 %all-to-all-done.1.got = bf16[16,8,5760]{2,1,0:T(8,128)(2,1)S(1)} async-done(((bf16[16,8,5760]{2,1,0:T(8,128)(2,1)}), bf16[16,8,5760]{2,1,0:T(8,128)(2,1)S(1)}, u32[]{:S(2)}, u32[]{:S(2)}) %all-to-all-start.1) | async-done | bytes 1474592 | tf_op jit(solution)/shard_map/all_to_all | solution.py:274
  98.0 1.7 norms.1
  99.7 4.9 %all-to-all-start.2 = ((bf16[16,8,5760]{2,1,0:T(8,128)(2,1)}), bf16[16,8,5760]{2,1,0:T(8,128)(2,1)S(1)}, u32[]{:S(2)}, u32[]{:S(2)}) async-start(bf16[16,8,5760]{2,1,0:T(8,128)(2,1)} %norms.1), calls=%async_computation.2 | async-start | bytes 2949120 | tf_op jit(solution)/shard_map/all_to_all | solution.py:274
  105.7 18.8 %all-to-all-done.2.got = bf16[16,8,5760]{2,1,0:T(8,128)(2,1)S(1)} async-done(((bf16[16,8,5760]{2,1,0:T(8,128)(2,1)}), bf16[16,8,5760]{2,1,0:T(8,128)(2,1)S(1)}, u32[]{:S(2)}, u32[]{:S(2)}) %all-to-all-start.2) | async-done | bytes 1474592 | tf_op jit(solution)/shard_map/all_to_all | solution.py:274
  124.5 1.1 copy-done.2
  125.7 5.5 %project.1 = (bf16[128,256]{1,0:T(8,128)(2,1)S(1)}, bf16[16,128,256]{2,1,0:T(8,128)(2,1)}) custom-call(bf16[16,8,5760]{2,1,0:T(8,128)(2,1)} %copy-done.2, bf16[5376,512]{1,0:T(8,128)(2,1)} %all-gather.2.cloned.1.call-done.weights, f32[128,128]{1,0:T(8,128)S(1)} %get-tuple-element.26.turn_cos, f32[128,128]{1,0:T(8,128)S(1)} %get-tuple-element.27.turn_sin), custom_call_target="tpu_custom_call" | custom-call | tf_op jit(solution)/shard_map/project/pallas_call | solution.py:377
  131.2 6.6 %all-to-all-start.4 = ((bf16[16,128,256]{2,1,0:T(8,128)(2,1)}), bf16[16,128,256]{2,1,0:T(8,128)(2,1)S(1)}, u32[]{:S(2)}, u32[]{:S(2)}) async-start(bf16[16,128,256]{2,1,0:T(8,128)(2,1)} %get-tuple-element.12), calls=%async_computation.4 | async-start | bytes 2097152 | tf_op jit(solution)/shard_map/all_to_all | solution.py:395
  137.8 8.9 %collective-permute-start.2 = (bf16[128,256]{1,0:T(8,128)(2,1)S(1)}, bf16[128,256]{1,0:T(8,128)(2,1)S(1)}, u32[]{:S(2)}, u32[]{:S(2)}) collective-permute-start(bf16[128,256]{1,0:T(8,128)(2,1)S(1)} %get-tuple-element.11.own_query), channel_id=1, source_target_pairs={{0,496},{16,480},{32,464},{48,448},{64,432},{80,416},{96,400},{112... | collective-permute-start | bytes 196616 | tf_op jit(solution)/shard_map/ppermute | solution.py:282
  146.8 24.8 %collective-permute-done.2.other_query = bf16[128,256]{1,0:T(8,128)(2,1)S(1)} collective-permute-done((bf16[128,256]{1,0:T(8,128)(2,1)S(1)}, bf16[128,256]{1,0:T(8,128)(2,1)S(1)}, u32[]{:S(2)}, u32[]{:S(2)}) %collective-permute-start.2) | collective-permute-done | bytes 65568 | tf_op jit(solution)/shard_map/ppermute | solution.py:282
  171.7 2.8 %second_layer.1 = (f32[128,256]{1,0:T(8,128)S(1)}, f32[128,128]{1,0:T(8,128)S(1)}, bf16[128,384]{1,0:T(8,128)(2,1)S(1)}) custom-call(s32[3]{0:T(128)S(1)} %pad_add_fusion.2.base, bf16[128,256]{1,0:T(8,128)(2,1)S(1)} %get-tuple-element.11.own_query, bf16[128,256]{1,0:T(8,128)(2,1)S(1)} %collective-permute-done.2.other_query, bf16[2048,256]{1,0:T(8,128)(2,1)S(1)} %bitcast.11, ...), custom_call_target="tpu_custom_call" | custom-call | tf_op jit(solution)/shard_map/second_layer/pallas_call | solution.py:406
  174.5 1.9 collective-permute-start.3
  176.4 0.9 slice_bitcast_fusion
  178.0 9.3 %collective-permute-done.3.got = bf16[128,384]{1,0:T(8,128)(2,1)S(1)} collective-permute-done((bf16[128,384]{1,0:T(8,128)(2,1)S(1)}, bf16[128,384]{1,0:T(8,128)(2,1)S(1)}, u32[]{:S(2)}, u32[]{:S(2)}) %collective-permute-start.3) | collective-permute-done | bytes 98336 | tf_op jit(solution)/shard_map/ppermute | solution.py:282
  (35 shorter events, 5.1 us)
Async XLA Ops:
  7.2 117.4 %all-gather.2.cloned.1.call-start = ((), (), s32[]{:S(2)}) async-start(), calls=%async_computation.5 | async-start | bytes 6193152 | tf_op jit(solution)/shard_map/all_gather | solution.py:326
  9.7 26.2 %copy-start.3 = (bf16[128,256]{1,0:T(8,128)(2,1)S(1)}, bf16[128,256]{1,0:T(8,128)(2,1)}, u32[]{:S(2)}) copy-start(bf16[128,256]{1,0:T(8,128)(2,1)} %get-tuple-element.9) | copy-start | bytes 196612
  35.8 23.3 %copy-start.6 = (s32[2]{0:T(128)S(1)}, s32[2]{0:T(128)}, u32[]{:S(2)}) copy-start(s32[2]{0:T(128)} %param.22) | copy-start | bytes 28
  35.8 34.3 %copy-start = (bf16[256,5376]{1,0:T(8,128)(2,1)S(1)}, bf16[256,5376]{1,0:T(8,128)(2,1)}, u32[]{:S(2)}) copy-start(bf16[256,5376]{1,0:T(8,128)(2,1)} %out_one.1) | copy-start | bytes 8257540
  35.8 34.2 %copy-start.1 = (bf16[128,256]{1,0:T(8,128)(2,1)S(1)}, bf16[128,256]{1,0:T(8,128)(2,1)}, u32[]{:S(2)}) copy-start(bf16[128,256]{1,0:T(8,128)(2,1)} %query.1) | copy-start | bytes 196612
  35.9 13.4 %collective-permute-start.1 = (bf16[128,256]{1,0:T(8,128)(2,1)S(1)}, bf16[128,256]{1,0:T(8,128)(2,1)S(1)}, u32[]{:S(2)}, u32[]{:S(2)}) collective-permute-start(bf16[128,256]{1,0:T(8,128)(2,1)S(1)} %copy-done.3), channel_id=1, source_target_pairs={{0,128},{16,144},{32,160},{48,176},{64,192},{80,208},{96,224},{112... | collective-permute-start | bytes 196616 | tf_op jit(solution)/shard_map/ppermute | solution.py:286
  42.2 9.8 %collective-permute-start = (bf16[128,256]{1,0:T(8,128)(2,1)S(1)}, bf16[128,256]{1,0:T(8,128)(2,1)S(1)}, u32[]{:S(2)}, u32[]{:S(2)}) collective-permute-start(bf16[128,256]{1,0:T(8,128)(2,1)S(1)} %copy-done.3), channel_id=1, source_target_pairs={{0,64},{16,80},{32,96},{48,112},{64,128},{80,144},{96,160},{112,17... | collective-permute-start | bytes 196616 | tf_op jit(solution)/shard_map/ppermute | solution.py:286
  52.9 17.0 %all-to-all-start = ((bf16[4,256,256]{2,1,0:T(8,128)(2,1)}), bf16[4,256,256]{2,1,0:T(8,128)(2,1)S(1)}, u32[]{:S(2)}, u32[]{:S(2)}) async-start(bf16[4,256,256]{2,1,0:T(8,128)(2,1)} %broadcast_select_fusion), calls=%async_computation | async-start | bytes 1048576 | tf_op jit(solution)/shard_map/all_to_all | solution.py:278
  73.1 4.9 %copy-start.4 = (f32[5376]{0:T(1024)S(1)}, f32[5376]{0:T(1024)}, u32[]{:S(2)}) copy-start(f32[5376]{0:T(1024)} %param.17) | copy-start | bytes 64516
  73.2 5.0 %copy-start.5 = (f32[5376]{0:T(1024)S(1)}, f32[5376]{0:T(1024)}, u32[]{:S(2)}) copy-start(f32[5376]{0:T(1024)} %param.18) | copy-start | bytes 64516
  73.2 24.8 %all-to-all-start.1 = ((bf16[16,8,5760]{2,1,0:T(8,128)(2,1)}), bf16[16,8,5760]{2,1,0:T(8,128)(2,1)S(1)}, u32[]{:S(2)}, u32[]{:S(2)}) async-start(bf16[16,8,5760]{2,1,0:T(8,128)(2,1)} %first_layer.1), calls=%async_computation.1 | async-start | bytes 2949120 | tf_op jit(solution)/shard_map/all_to_all | solution.py:274
  99.7 24.9 %all-to-all-start.2 = ((bf16[16,8,5760]{2,1,0:T(8,128)(2,1)}), bf16[16,8,5760]{2,1,0:T(8,128)(2,1)S(1)}, u32[]{:S(2)}, u32[]{:S(2)}) async-start(bf16[16,8,5760]{2,1,0:T(8,128)(2,1)} %norms.1), calls=%async_computation.2 | async-start | bytes 2949120 | tf_op jit(solution)/shard_map/all_to_all | solution.py:274
  124.5 1.1 copy-start.2
  131.2 40.4 %all-to-all-start.4 = ((bf16[16,128,256]{2,1,0:T(8,128)(2,1)}), bf16[16,128,256]{2,1,0:T(8,128)(2,1)S(1)}, u32[]{:S(2)}, u32[]{:S(2)}) async-start(bf16[16,128,256]{2,1,0:T(8,128)(2,1)} %get-tuple-element.12), calls=%async_computation.4 | async-start | bytes 2097152 | tf_op jit(solution)/shard_map/all_to_all | solution.py:395
  137.8 33.8 %collective-permute-start.2 = (bf16[128,256]{1,0:T(8,128)(2,1)S(1)}, bf16[128,256]{1,0:T(8,128)(2,1)S(1)}, u32[]{:S(2)}, u32[]{:S(2)}) collective-permute-start(bf16[128,256]{1,0:T(8,128)(2,1)S(1)} %get-tuple-element.11.own_query), channel_id=1, source_target_pairs={{0,496},{16,480},{32,464},{48,448},{64,432},{80,416},{96,400},{112... | collective-permute-start | bytes 196616 | tf_op jit(solution)/shard_map/ppermute | solution.py:282
  174.5 12.9 %collective-permute-start.3 = (bf16[128,384]{1,0:T(8,128)(2,1)S(1)}, bf16[128,384]{1,0:T(8,128)(2,1)S(1)}, u32[]{:S(2)}, u32[]{:S(2)}) collective-permute-start(bf16[128,384]{1,0:T(8,128)(2,1)S(1)} %get-tuple-element.15), channel_id=1, source_target_pairs={{0,496},{16,480},{32,464},{48,448},{64,432},{80,416},{96,400},{112... | collective-permute-start | bytes 294920 | tf_op jit(solution)/shard_map/ppermute | solution.py:282
Sparse Core Ops, SparseCore 0:
  36.0 71.8 all-gather.1

commit v4 on v3

--- a/solution.py
+++ b/solution.py
@@ -25,8 +25,6 @@
 ROWS = TOK // N_HEADS
 NEG = -1e30
 Y_GROUPS = [[z * Y_HI + y for y in range(Y_HI)] for z in range(Z)]
-GROUP = 16
-HALF_GROUPS = [list(range(GROUP)), list(range(GROUP, N_CTX))]
 Z_GROUPS = [[z * Y_HI + y for z in range(Z)] for y in range(Y_HI)]
 VMEM_LIMIT = 24 * 1024 * 1024
 
@@ -82,7 +80,24 @@
     return mixed / total, top + jnp.log(total)
 
 
-def first_kernel(base, query, blocks, last, low, out_one, resid, sent, scores):
+def select_kernel(base, own, back_one, back_two, *shifted):
+    for steps, out in enumerate(shifted, start=1):
+        onward = base[1] + steps < Y_HI
+
+        @pl.when(onward)
+        def _(out=out):
+            out[:TOK] = own[...]
+            out[TOK:] = back_one[...]
+
+        @pl.when(jnp.logical_not(onward))
+        def _(out=out):
+            out[:TOK] = back_one[...]
+            out[TOK:] = back_two[...]
+
+
+def first_kernel(
+    base, query, own, back_one, back_two, near, middle, far, low, out_one, resid, sent, scores
+):
     place_z, place_y = base[0], base[1]
     start = (place_z * Y_HI + place_y) * TOK
     stacked = jnp.concatenate([query[:, :HEAD_SIZE], query[:, HEAD_SIZE:]], axis=0)
@@ -92,23 +107,14 @@
     lane = lax.broadcasted_iota(jnp.int32, (1, 2 * TOK), 1)
     pair = jnp.where(lane < TOK, lane, lane - (TOK + Y_HI * TOK))
     chunks = []
-    for peer in range(Y_HI):
-        newer = (place_z - jnp.where(peer > place_y, 1, 0)) * (Y_HI * TOK) + peer * TOK
-        chunks.append(
-            (
-                lambda peer=peer: (
-                    blocks[peer, :, :HEAD_SIZE],
-                    blocks[peer, :, HEAD_SIZE:],
-                ),
-                newer + pair,
-            )
-        )
-    chunks.append(
-        (
-            lambda: (last[:, :HEAD_SIZE], last[:, HEAD_SIZE:]),
-            start - 2 * Y_HI * TOK + lane[:, :TOK],
-        )
-    )
+
+    def add(block, tokens):
+        chunks.append((lambda: (block[:, :HEAD_SIZE], block[:, HEAD_SIZE:]), tokens))
+
+    for steps, block in enumerate((near, middle, far), start=1):
+        add(block, start - steps * TOK + pair)
+    for level, block in enumerate((own, back_one, back_two)):
+        add(block, start - level * Y_HI * TOK + lane[:, :TOK])
     mixed, _ = softmax_rows(stacked, chunks, lowest, high, scores)
     mixed = mixed.astype(jnp.bfloat16)
     attend = jnp.concatenate([mixed[:TOK], mixed[TOK:]], axis=1)
@@ -173,7 +179,7 @@
 
 
 def project_kernel(
-    got, weights, turn_cos, turn_sin, query, pair, held, block, in_sem, out_sem
+    got, weights, turn_cos, turn_sin, front, back, pair, held, block, in_sem, out_sem
 ):
     depth = WIDTH // PARTS
     spans = [slice(part * depth, (part + 1) * depth) for part in range(PARTS)]
@@ -194,10 +200,11 @@
             values = values * turn_cos[...] + pltpu.roll(values, HALF, 1) * turn_sin[...]
         values = values.astype(jnp.bfloat16)
         if head < 2:
-            query[:, head * HEAD_SIZE : (head + 1) * HEAD_SIZE] = values
+            front[:, head * HEAD_SIZE : (head + 1) * HEAD_SIZE] = values[:HALF]
+            back[:, head * HEAD_SIZE : (head + 1) * HEAD_SIZE] = values[HALF:]
         else:
             block[:, (head - 2) * HEAD_SIZE : (head - 1) * HEAD_SIZE] = values
-    moves = [pltpu.make_async_copy(block, pair.at[peer], out_sem.at[peer]) for peer in range(GROUP)]
+    moves = [pltpu.make_async_copy(block, pair.at[member], out_sem.at[member]) for member in range(Z)]
     for move in moves:
         move.start()
     for move in moves:
@@ -217,57 +224,59 @@
     return terms
 
 
-def second_kernel(base, own_query, other_query, pair, low, kept, kept_log, sent, scores):
+def second_kernel(base, queries, pair, low, sent, scores):
+    place_z, place_y = base[0], base[1]
     lane = lax.broadcasted_iota(jnp.int32, (1, CHUNK), 1)
+    lane = jnp.where(lane < TOK, lane, lane + (Y_HI - 1) * TOK)
     row = lax.broadcasted_iota(jnp.int32, (2 * TOK, 1), 0)
-    slot = lax.broadcasted_iota(jnp.int32, (HALF, HEAD_SIZE), 1)
-    for index, query in enumerate((own_query, other_query)):
-        stacked = jnp.concatenate([query[:, :HEAD_SIZE], query[:, HEAD_SIZE:]], axis=0)
-        lowest = low[index * TOK : (index + 1) * TOK, :1]
+    slot = lax.broadcasted_iota(jnp.int32, (TOK, HEAD_SIZE), 1)
+    chunks = []
+    for at in range(0, Z * TOK, CHUNK):
+        chunks.append(
+            (
+                lambda at=at: (pair[at : at + CHUNK, :HEAD_SIZE], pair[at : at + CHUNK, HEAD_SIZE:]),
+                at * Y_HI + place_y * TOK + lane,
+            )
+        )
+    for peer in range(Y_HI):
+        block = queries[peer * TOK : (peer + 1) * TOK, :]
+        stacked = jnp.concatenate([block[:, :HEAD_SIZE], block[:, HEAD_SIZE:]], axis=0)
+        lowest = low[peer * TOK : (peer + 1) * TOK, :1]
         lowest = jnp.concatenate([lowest, lowest], axis=0)
-        high = base[1 + index] + lax.rem(row, TOK)
-        chunks = []
-        for at in range(0, GROUP * TOK, CHUNK):
-            chunks.append(
-                (
-                    lambda at=at: (
-                        pair[at : at + CHUNK, :HEAD_SIZE],
-                        pair[at : at + CHUNK, HEAD_SIZE:],
-                    ),
-                    base[0] + at + lane,
-                )
+        front_first = (place_z * Y_HI + peer) * TOK
+        back_first = ((Z - place_z) * Y_HI - 1 - peer) * TOK
+        within = lax.rem(row, TOK)
+        high = within + jnp.where(within < HALF, front_first, back_first)
+        mixed, logs = softmax_rows(stacked, chunks, lowest, high, scores)
+        packed = jnp.zeros((TOK, HEAD_SIZE), jnp.float32)
+        for head in range(2):
+            rows = slice(head * TOK, (head + 1) * TOK)
+            sent[peer, :, head * HEAD_SIZE : (head + 1) * HEAD_SIZE] = mixed[rows].astype(
+                jnp.bfloat16
             )
-        mixed, logs = softmax_rows(stacked, chunks, lowest, high, scores)
-        for half in range(2):
-            rows = slice(half * HALF, (half + 1) * HALF)
-            pieces = [slice(half * HALF + head * TOK, (half + 1) * HALF + head * TOK) for head in range(2)]
-            if half == index:
-                for head in range(2):
-                    kept[rows, head * HEAD_SIZE : (head + 1) * HEAD_SIZE] = mixed[pieces[head]]
-                kept_log[rows, :] = jnp.where(slot < 3, logs[pieces[0]], logs[pieces[1]])
-            else:
-                packed = jnp.zeros((HALF, HEAD_SIZE), jnp.float32)
-                for head in range(2):
-                    sent[rows, head * HEAD_SIZE : (head + 1) * HEAD_SIZE] = mixed[
-                        pieces[head]
-                    ].astype(jnp.bfloat16)
-                    for place, term in enumerate(three_terms(logs[pieces[head]])):
-                        packed = jnp.where(slot == 3 * head + place, term, packed)
-                sent[rows, 2 * HEAD_SIZE :] = packed.astype(jnp.bfloat16)
-
-
-def combine_kernel(kept, kept_log, got, out):
-    packed = got[:, 2 * HEAD_SIZE :].astype(jnp.float32)
+            for place, term in enumerate(three_terms(logs[rows])):
+                packed = jnp.where(slot == 3 * head + place, term, packed)
+        sent[peer, :, 2 * HEAD_SIZE :] = packed.astype(jnp.bfloat16)
+
+
+def combine_kernel(got, out):
     for head in range(2):
+        logs = []
+        for peer in range(Y_HI):
+            packed = got[peer, :, 2 * HEAD_SIZE :].astype(jnp.float32)
+            at = 3 * head
+            logs.append(
+                packed[:, at : at + 1] + packed[:, at + 1 : at + 2] + packed[:, at + 2 : at + 3]
+            )
+        top = jnp.maximum(jnp.maximum(logs[0], logs[1]), jnp.maximum(logs[2], logs[3]))
         cols = slice(head * HEAD_SIZE, (head + 1) * HEAD_SIZE)
-        mine = kept_log[:, 3 * head : 3 * head + 1]
-        at = 3 * head
-        theirs = packed[:, at : at + 1] + packed[:, at + 1 : at + 2] + packed[:, at + 2 : at + 3]
-        top = jnp.maximum(mine, theirs)
-        mine = jnp.exp(mine - top)
-        theirs = jnp.exp(theirs - top)
-        mixed = kept[:, cols] * mine + got[:, cols].astype(jnp.float32) * theirs
-        out[:, cols] = (mixed / (mine + theirs)).astype(jnp.bfloat16)
+        mixed = jnp.zeros((TOK, HEAD_SIZE), jnp.float32)
+        total = jnp.zeros((TOK, 1), jnp.float32)
+        for peer in range(Y_HI):
+            weight = jnp.exp(logs[peer] - top)
+            mixed = mixed + weight * got[peer, :, cols].astype(jnp.float32)
+            total = total + weight
+        out[:, cols] = (mixed / total).astype(jnp.bfloat16)
 
 
 def exchange_heads(value):
@@ -276,6 +285,11 @@
 
 def exchange_y(value):
     return lax.all_to_all(value, "ctx", 0, 0, tiled=True, axis_index_groups=Y_GROUPS)
+
+
+def y_shift(value, steps):
+    pairs = [(z * Y_HI + y, z * Y_HI + (y + steps) % Y_HI) for z in range(Z) for y in range(Y_HI)]
+    return lax.ppermute(value, "ctx", pairs)
 
 
 def mirror(value):
@@ -325,11 +339,18 @@
     weights = exchange_y(spread).reshape(-1, 4 * HEAD_SIZE)
     weights = lax.all_gather(weights, "ctx", axis=0, tiled=True, axis_index_groups=Z_GROUPS)
 
-    later = jnp.concatenate([own, back_one], axis=0)
-    earlier = jnp.concatenate([back_one, back_two], axis=0)
-    peers = jnp.arange(Y_HI, dtype=jnp.int32)[:, None, None]
-    window_blocks = jnp.where(peers >= place_y, later[None], earlier[None])
-    blocks = exchange_y(window_blocks)
+    bases = jnp.stack([place_z, place_y])
+    outgoing = pl.pallas_call(
+        select_kernel,
+        out_shape=[jax.ShapeDtypeStruct((2 * TOK, 2 * HEAD_SIZE), bf16)] * (Y_HI - 1),
+        in_specs=[whole(pltpu.SMEM)] + [whole()] * 3,
+        out_specs=[whole()] * (Y_HI - 1),
+        compiler_params=params(),
+        name="window_select",
+    )(bases, own, back_one, back_two)
+    incoming = []
+    for steps, block in enumerate(outgoing, start=1):
+        incoming.append(y_shift(block, steps))
 
     start = ctx_place * TOK
     tokens = start + jnp.arange(TOK, dtype=jnp.int32)
@@ -339,7 +360,7 @@
     sent = pl.pallas_call(
         first_kernel,
         out_shape=jax.ShapeDtypeStruct((N_HEADS, ROWS, SLAB), bf16),
-        in_specs=[whole(pltpu.SMEM)] + [whole()] * 6,
+        in_specs=[whole(pltpu.SMEM)] + [whole()] * 10,
         out_specs=whole(),
         scratch_shapes=[pltpu.VMEM((2 * TOK, 9 * TOK), f32)],
         compiler_params=params(),
@@ -348,10 +369,12 @@
         ),
         name="first_layer",
     )(
-        jnp.stack([place_z, place_y]),
+        bases,
         first_layer_queries,
-        blocks,
+        own,
+        back_one,
         back_two,
+        *incoming,
         low_one,
         out_one,
         resid_in,
@@ -374,57 +397,62 @@
     cosine, sine = jnp.cos(angles), jnp.sin(angles)
     turn_cos = jnp.concatenate([cosine, cosine], axis=1)
     turn_sin = jnp.concatenate([-sine, sine], axis=1)
-    query, pair = pl.pallas_call(
+    front, back, pair = pl.pallas_call(
         project_kernel,
         out_shape=(
-            jax.ShapeDtypeStruct((TOK, 2 * HEAD_SIZE), bf16),
-            jax.ShapeDtypeStruct((GROUP, TOK, 2 * HEAD_SIZE), bf16),
+            jax.ShapeDtypeStruct((HALF, 2 * HEAD_SIZE), bf16),
+            jax.ShapeDtypeStruct((HALF, 2 * HEAD_SIZE), bf16),
+            jax.ShapeDtypeStruct((Z, TOK, 2 * HEAD_SIZE), bf16),
         ),
         in_specs=[whole(), whole(pltpu.HBM), whole(), whole()],
-        out_specs=(whole(), whole(pltpu.HBM)),
+        out_specs=(whole(), whole(), whole(pltpu.HBM)),
         scratch_shapes=[
             pltpu.VMEM((WIDTH, 4 * HEAD_SIZE), bf16),
             pltpu.VMEM((TOK, 2 * HEAD_SIZE), bf16),
             pltpu.SemaphoreType.DMA((PARTS,)),
-            pltpu.SemaphoreType.DMA((GROUP,)),
+            pltpu.SemaphoreType.DMA((Z,)),
         ],
-        compiler_params=pltpu.CompilerParams(vmem_limit_bytes=52 * 1024 * 1024),
+        compiler_params=pltpu.CompilerParams(vmem_limit_bytes=50 * 1024 * 1024),
         name="project",
     )(got, weights, turn_cos, turn_sin)
 
-    pairs = lax.all_to_all(
-        pair, "ctx", 0, 0, tiled=True, axis_index_groups=HALF_GROUPS
-    ).reshape(GROUP * TOK, 2 * HEAD_SIZE)
-    other_query = mirror(query)
-
-    other_start = (N_CTX - 1 - ctx_place) * TOK
-    other_pos = lax.dynamic_slice_in_dim(positions, other_start, TOK, 0)
-    other_tokens = other_start + jnp.arange(TOK, dtype=jnp.int32)
-    low_two = jnp.concatenate([tokens - local_pos, other_tokens - other_pos])
-    low_two = jnp.broadcast_to(low_two[:, None], (2 * TOK, 128))
-    bases = jnp.stack([(ctx_place // GROUP) * (GROUP * TOK), start, other_start])
-    kept, kept_log, sent = pl.pallas_call(
+    pairs = lax.all_to_all(pair, "ctx", 0, 0, tiled=True, axis_index_groups=Z_GROUPS)
+    pairs = pairs.reshape(Z * TOK, 2 * HEAD_SIZE)
+    back = mirror(back)
+    queries = lax.all_gather(
+        jnp.concatenate([front, back], axis=0),
+        "ctx",
+        axis=0,
+        tiled=True,
+        axis_index_groups=Y_GROUPS,
+    )
+
+    level = Y_HI * TOK
+    halves = (Y_HI, 2, HALF)
+    order = jnp.arange(level, dtype=jnp.int32).reshape(halves)
+    near, far = place_z * level, (Z - 1 - place_z) * level
+    near_low = near + order - lax.dynamic_slice_in_dim(positions, near, level, 0).reshape(halves)
+    far_low = far + order - lax.dynamic_slice_in_dim(positions, far, level, 0).reshape(halves)
+    low_two = jnp.stack([near_low[:, 0], far_low[::-1, 1]], axis=1).reshape(level, 1)
+    low_two = jnp.broadcast_to(low_two, (level, 128))
+    sent = pl.pallas_call(
         second_kernel,
-        out_shape=(
-            jax.ShapeDtypeStruct((TOK, 2 * HEAD_SIZE), f32),
-            jax.ShapeDtypeStruct((TOK, HEAD_SIZE), f32),
-            jax.ShapeDtypeStruct((TOK, 3 * HEAD_SIZE), bf16),
-        ),
-        in_specs=[whole(pltpu.SMEM)] + [whole()] * 4,
-        out_specs=(whole(), whole(), whole()),
-        scratch_shapes=[pltpu.VMEM((2 * TOK, GROUP * TOK), f32)],
+        out_shape=jax.ShapeDtypeStruct((Y_HI, TOK, 3 * HEAD_SIZE), bf16),
+        in_specs=[whole(pltpu.SMEM)] + [whole()] * 3,
+        out_specs=whole(),
+        scratch_shapes=[pltpu.VMEM((2 * TOK, Z * TOK), f32)],
         compiler_params=params(),
         name="second_layer",
-    )(bases, query, other_query, pairs, low_two)
-    got = mirror(sent)
+    )(bases, queries, pairs, low_two)
+    got = exchange_y(sent)
     attended = pl.pallas_call(
         combine_kernel,
         out_shape=jax.ShapeDtypeStruct((TOK, 2 * HEAD_SIZE), bf16),
-        in_specs=[whole()] * 3,
+        in_specs=[whole()],
         out_specs=whole(),
         compiler_params=params(),
         name="combine",
-    )(kept, kept_log, got)
+    )(got)
     return (resid_out, attended)
 
 

time: 196 us -> 196 us (level)
  the two profiles are of different devices: /device:TPU:22 before, /device:TPU:64 now
where the time goes in v4:
time: 196 us; the launch traced here: 195 us
  waiting for transfers between devices  60.7 us (31%)
  starting transfers between devices  53.5 us (27%)
  blocking collectives  42 us (21%)
  Pallas kernels  16.7 us (9%)
  between operations  14.3 us (7%)
  local copies, waits for them, and re-layouts  4.72 us (2%)
  other arithmetic  2.79 us (1%)
    all_to_all x2, waiting for transfers between devices, exchange_heads(): return lax.all_to_all(value, 'heads', 0, 0, tiled=True)  41 us
    all_to_all x1, blocking collectives, exchange_y(): lax.all_to_all(value, 'ctx', 0, 0, tiled=True, axis_index_groups=Y_GROUPS)  27.3 us
    all_gather x1, blocking collectives, shards(): lax.all_gather(jnp.concatenate([front, back], axis=0), 'ctx', axis=0, til...  14.7 us
    ppermute x3, starting transfers between devices, y_shift(): return lax.ppermute(value, 'ctx', pairs)  11.8 us
    ppermute x2, starting transfers between devices, ctx_shift(): lax.ppermute(value, 'ctx', [(i, (i + steps) % N_CTX) for i in range(N_CTX)])  11.6 us
    all_to_all x2, starting transfers between devices, exchange_heads(): return lax.all_to_all(value, 'heads', 0, 0, tiled=True)  11.3 us
    all_to_all x1, waiting for transfers between devices, exchange_y(): lax.all_to_all(value, 'ctx', 0, 0, tiled=True, axis_index_groups=Y_GROUPS)  10.1 us
    all_to_all x1, starting transfers between devices, shards(): lax.all_to_all(pair, 'ctx', 0, 0, tiled=True, axis_index_groups=Z_GROUPS)  7.94 us
  transfers between devices with their start and end apart: 11, of which 7 were waited for; matrix products, arithmetic and copies ran while one was open for 3% of the time, Pallas kernels for 3%

profile of v4, /device:TPU:64, one launch (start us, length us, event | category | flops | bytes accessed | tf_op | source)
XLA Modules:
  0.0 194.6 jit_solution(6885416074639506992)
XLA Ops:
  7.2 2.6 %prepare.1 = (bf16[128,256]{1,0:T(8,128)(2,1)}, bf16[4,168,512]{2,1,0:T(8,128)(2,1)}) custom-call(bf16[128,128]{1,0:T(8,128)(2,1)} %keys.1, bf16[128,128]{1,0:T(8,128)(2,1)} %values.1, bf16[168,256]{1,0:T(8,128)(2,1)} %proj_query.1, bf16[168,128]{1,0:T(8,128)(2,1)} %key_projection.1, bf16[168,128]{1,0:T(8,128)(2,1)} %value_projection.1), custom_call_target="tpu_custom_call" | custom-call | tf_op jit(solution)/shard_map/prepare/pallas_call | solution.py:322
  9.8 27.3 %all_to_all.25 = bf16[4,168,512]{2,1,0:T(8,128)(2,1)} all-to-all(bf16[4,168,512]{2,1,0:T(8,128)(2,1)} %get-tuple-element.14), channel_id=1, replica_groups={{0,16,32,48},{64,80,96,112},{128,144,160,176},{192,208,224,240},{256,27..., dimensions={0} | all-to-all | bytes 1376256 | tf_op jit(solution)/shard_map/all_to_all | solution.py:287
  37.1 4.3 %collective-permute-start = (bf16[128,256]{1,0:T(8,128)(2,1)}, bf16[128,256]{1,0:T(8,128)(2,1)S(1)}, u32[]{:S(2)}, u32[]{:S(2)}) collective-permute-start(bf16[128,256]{1,0:T(8,128)(2,1)} %get-tuple-element.10.own), channel_id=1, source_target_pairs={{0,64},{16,80},{32,96},{48,112},{64,128},{80,144},{96,160},{112,17... | collective-permute-start | bytes 196616 | tf_op jit(solution)/shard_map/ppermute | solution.py:300
  41.4 7.3 %collective-permute-start.1 = (bf16[128,256]{1,0:T(8,128)(2,1)}, bf16[128,256]{1,0:T(8,128)(2,1)S(1)}, u32[]{:S(2)}, u32[]{:S(2)}) collective-permute-start(bf16[128,256]{1,0:T(8,128)(2,1)} %get-tuple-element.10.own), channel_id=1, source_target_pairs={{0,128},{16,144},{32,160},{48,176},{64,192},{80,208},{96,224},{112... | collective-permute-start | bytes 196616 | tf_op jit(solution)/shard_map/ppermute | solution.py:300
  48.8 1.0 copy.14.resid
  53.0 3.9 %collective-permute-start.2 = (bf16[256,256]{1,0:T(8,128)(2,1)S(1)}, bf16[256,256]{1,0:T(8,128)(2,1)S(1)}, u32[]{:S(2)}, u32[]{:S(2)}) collective-permute-start(bf16[256,256]{1,0:T(8,128)(2,1)S(1)} %get-tuple-element.11), channel_id=1, source_target_pairs={{0,16},{16,32},{32,48},{48,0},{64,80},{80,96},{96,112},{112,64},{1... | collective-permute-start | bytes 393224 | tf_op jit(solution)/shard_map/ppermute | solution.py:292
  56.9 3.2 %collective-permute-start.3 = (bf16[256,256]{1,0:T(8,128)(2,1)S(1)}, bf16[256,256]{1,0:T(8,128)(2,1)S(1)}, u32[]{:S(2)}, u32[]{:S(2)}) collective-permute-start(bf16[256,256]{1,0:T(8,128)(2,1)S(1)} %get-tuple-element.12), channel_id=1, source_target_pairs={{0,32},{16,48},{32,0},{48,16},{64,96},{80,112},{96,64},{112,80},{1... | collective-permute-start | bytes 393224 | tf_op jit(solution)/shard_map/ppermute | solution.py:292
  60.1 4.7 %collective-permute-start.4 = (bf16[256,256]{1,0:T(8,128)(2,1)S(1)}, bf16[256,256]{1,0:T(8,128)(2,1)S(1)}, u32[]{:S(2)}, u32[]{:S(2)}) collective-permute-start(bf16[256,256]{1,0:T(8,128)(2,1)S(1)} %get-tuple-element.13), channel_id=1, source_target_pairs={{0,48},{16,0},{32,16},{48,32},{64,112},{80,64},{96,80},{112,96},{1... | collective-permute-start | bytes 393224 | tf_op jit(solution)/shard_map/ppermute | solution.py:292
  65.6 3.1 %collective-permute-done.3.middle = bf16[256,256]{1,0:T(8,128)(2,1)S(1)} collective-permute-done((bf16[256,256]{1,0:T(8,128)(2,1)S(1)}, bf16[256,256]{1,0:T(8,128)(2,1)S(1)}, u32[]{:S(2)}, u32[]{:S(2)}) %collective-permute-start.3) | collective-permute-done | bytes 131104 | tf_op jit(solution)/shard_map/ppermute | solution.py:292
  70.3 3.1 %first_layer.1 = bf16[16,8,5760]{2,1,0:T(8,128)(2,1)} custom-call(s32[2]{0:T(128)S(1)} %pad_add_fusion.1.base, bf16[128,256]{1,0:T(8,128)(2,1)S(1)} %copy-done.2, bf16[128,256]{1,0:T(8,128)(2,1)S(1)} %copy-done.1, bf16[128,256]{1,0:T(8,128)(2,1)S(1)} %collective-permute-done.back_one, bf16[128,256]{1,0:T(8,128)(2,1)S(1)} %collective-permute-done.1.back_two, ...), custom_call_target="tpu_custom_call" | custom-call | flops 600000000 | bytes 6000000 | tf_op jit(solution)/shard_map/first_layer/pallas_call | solution.py:360
  73.3 7.5 %all-to-all-start = ((bf16[16,8,5760]{2,1,0:T(8,128)(2,1)}), bf16[16,8,5760]{2,1,0:T(8,128)(2,1)S(1)}, u32[]{:S(2)}, u32[]{:S(2)}) async-start(bf16[16,8,5760]{2,1,0:T(8,128)(2,1)} %first_layer.1), calls=%async_computation | async-start | bytes 2949120 | tf_op jit(solution)/shard_map/all_to_all | solution.py:283
  81.0 21.1 %all-to-all-done.got = bf16[16,8,5760]{2,1,0:T(8,128)(2,1)S(1)} async-done(((bf16[16,8,5760]{2,1,0:T(8,128)(2,1)}), bf16[16,8,5760]{2,1,0:T(8,128)(2,1)S(1)}, u32[]{:S(2)}, u32[]{:S(2)}) %all-to-all-start) | async-done | bytes 1474592 | tf_op jit(solution)/shard_map/all_to_all | solution.py:283
  102.0 1.7 norms.1
  103.7 3.7 %all-to-all-start.1 = ((bf16[16,8,5760]{2,1,0:T(8,128)(2,1)}), bf16[16,8,5760]{2,1,0:T(8,128)(2,1)S(1)}, u32[]{:S(2)}, u32[]{:S(2)}) async-start(bf16[16,8,5760]{2,1,0:T(8,128)(2,1)} %norms.1), calls=%async_computation.1 | async-start | bytes 2949120 | tf_op jit(solution)/shard_map/all_to_all | solution.py:283
  108.6 19.9 %all-to-all-done.1.got = bf16[16,8,5760]{2,1,0:T(8,128)(2,1)S(1)} async-done(((bf16[16,8,5760]{2,1,0:T(8,128)(2,1)}), bf16[16,8,5760]{2,1,0:T(8,128)(2,1)S(1)}, u32[]{:S(2)}, u32[]{:S(2)}) %all-to-all-start.1) | async-done | bytes 1474592 | tf_op jit(solution)/shard_map/all_to_all | solution.py:283
  128.6 3.8 %project.1 = (bf16[64,256]{1,0:T(8,128)(2,1)S(1)}, bf16[64,256]{1,0:T(8,128)(2,1)S(1)}, bf16[8,128,256]{2,1,0:T(8,128)(2,1)}) custom-call(bf16[16,8,5760]{2,1,0:T(8,128)(2,1)S(1)} %all-to-all-done.1.got, bf16[5376,512]{1,0:T(8,128)(2,1)} %all-gather.2.cloned.1.call-done.weights, f32[128,128]{1,0:T(8,128)S(1)} %get-tuple-element.29.turn_cos, ...), custom_call_target="tpu_custom_call" | custom-call | tf_op jit(solution)/shard_map/project/pallas_call | solution.py:400
  132.4 7.9 %all-to-all-start.3 = ((bf16[8,128,256]{2,1,0:T(8,128)(2,1)}), bf16[8,128,256]{2,1,0:T(8,128)(2,1)S(1)}, u32[]{:S(2)}, u32[]{:S(2)}) async-start(bf16[8,128,256]{2,1,0:T(8,128)(2,1)} %get-tuple-element.17), calls=%async_computation.3 | async-start | bytes 1048576 | tf_op jit(solution)/shard_map/all_to_all | solution.py:419
  141.3 6.8 %collective-permute-start.5 = (bf16[64,256]{1,0:T(8,128)(2,1)S(1)}, bf16[64,256]{1,0:T(8,128)(2,1)S(1)}, u32[]{:S(2)}, u32[]{:S(2)}) collective-permute-start(bf16[64,256]{1,0:T(8,128)(2,1)S(1)} %get-tuple-element.16), channel_id=1, source_target_pairs={{0,496},{16,480},{32,464},{48,448},{64,432},{80,416},{96,400},{112... | collective-permute-start | bytes 98312 | tf_op jit(solution)/shard_map/ppermute | solution.py:296
  148.2 4.9 %collective-permute-done.5 = bf16[64,256]{1,0:T(8,128)(2,1)S(1)} collective-permute-done((bf16[64,256]{1,0:T(8,128)(2,1)S(1)}, bf16[64,256]{1,0:T(8,128)(2,1)S(1)}, u32[]{:S(2)}, u32[]{:S(2)}) %collective-permute-start.5) | collective-permute-done | bytes 32800 | tf_op jit(solution)/shard_map/ppermute | solution.py:296
  153.1 14.7 %all_gather.7.queries = bf16[512,256]{1,0:T(8,128)(2,1)S(1)} all-gather(bf16[128,256]{1,0:T(8,128)(2,1)S(1)} %pad_maximum_fusion.2), channel_id=1, replica_groups={{0,16,32,48},{64,80,96,112},{128,144,160,176},{192,208,224,240},{256,27..., dimensions={0}, use_global_device_ids=true | all-gather | bytes 327680 | tf_op jit(solution)/shard_map/all_gather | solution.py:422
  168.0 3.8 %second_layer.1 = bf16[4,128,384]{2,1,0:T(8,128)(2,1)} custom-call(s32[2]{0:T(128)S(1)} %pad_add_fusion.1.base, bf16[512,256]{1,0:T(8,128)(2,1)S(1)} %all_gather.7.queries, bf16[1024,256]{1,0:T(8,128)(2,1)S(1)} %bitcast.8, s32[512,128]{1,0:T(8,128)S(1)} %broadcast_in_dim.27.low), custom_call_target="tpu_custom_call" | custom-call | tf_op jit(solution)/shard_map/second_layer/pallas_call | solution.py:438
  171.7 4.0 %all-to-all-start.4 = ((bf16[4,128,384]{2,1,0:T(8,128)(2,1)}), bf16[4,128,384]{2,1,0:T(8,128)(2,1)S(1)}, u32[]{:S(2)}, u32[]{:S(2)}) async-start(bf16[4,128,384]{2,1,0:T(8,128)(2,1)} %second_layer.1), calls=%async_computation.4 | async-start | bytes 786432 | tf_op jit(solution)/shard_map/all_to_all | solution.py:287
  176.5 10.1 %all-to-all-done.4.got = bf16[4,128,384]{2,1,0:T(8,128)(2,1)S(1)} async-done(((bf16[4,128,384]{2,1,0:T(8,128)(2,1)}), bf16[4,128,384]{2,1,0:T(8,128)(2,1)S(1)}, u32[]{:S(2)}, u32[]{:S(2)}) %all-to-all-start.4) | async-done | bytes 393248 | tf_op jit(solution)/shard_map/all_to_all | solution.py:287
  186.6 1.2 combine.1
  (41 shorter events, 8.8 us)
Async XLA Ops:
  7.2 62.2 %copy-start = (bf16[256,5376]{1,0:T(8,128)(2,1)S(1)}, bf16[256,5376]{1,0:T(8,128)(2,1)}, u32[]{:S(2)}) copy-start(bf16[256,5376]{1,0:T(8,128)(2,1)} %out_one.1) | copy-start | bytes 8257540
  7.2 121.4 %all-gather.2.cloned.1.call-start = ((), (), s32[]{:S(2)}) async-start(), calls=%async_computation.5 | async-start | bytes 6193152 | tf_op jit(solution)/shard_map/all_gather | solution.py:340
  37.1 13.5 %collective-permute-start = (bf16[128,256]{1,0:T(8,128)(2,1)}, bf16[128,256]{1,0:T(8,128)(2,1)S(1)}, u32[]{:S(2)}, u32[]{:S(2)}) collective-permute-start(bf16[128,256]{1,0:T(8,128)(2,1)} %get-tuple-element.10.own), channel_id=1, source_target_pairs={{0,64},{16,80},{32,96},{48,112},{64,128},{80,144},{96,160},{112,17... | collective-permute-start | bytes 196616 | tf_op jit(solution)/shard_map/ppermute | solution.py:300
  41.4 10.1 %collective-permute-start.1 = (bf16[128,256]{1,0:T(8,128)(2,1)}, bf16[128,256]{1,0:T(8,128)(2,1)S(1)}, u32[]{:S(2)}, u32[]{:S(2)}) collective-permute-start(bf16[128,256]{1,0:T(8,128)(2,1)} %get-tuple-element.10.own), channel_id=1, source_target_pairs={{0,128},{16,144},{32,160},{48,176},{64,192},{80,208},{96,224},{112... | collective-permute-start | bytes 196616 | tf_op jit(solution)/shard_map/ppermute | solution.py:300
  51.6 0.8 copy-start.1
  53.0 12.6 %collective-permute-start.2 = (bf16[256,256]{1,0:T(8,128)(2,1)S(1)}, bf16[256,256]{1,0:T(8,128)(2,1)S(1)}, u32[]{:S(2)}, u32[]{:S(2)}) collective-permute-start(bf16[256,256]{1,0:T(8,128)(2,1)S(1)} %get-tuple-element.11), channel_id=1, source_target_pairs={{0,16},{16,32},{32,48},{48,0},{64,80},{80,96},{96,112},{112,64},{1... | collective-permute-start | bytes 393224 | tf_op jit(solution)/shard_map/ppermute | solution.py:292
  56.9 11.8 %collective-permute-start.3 = (bf16[256,256]{1,0:T(8,128)(2,1)S(1)}, bf16[256,256]{1,0:T(8,128)(2,1)S(1)}, u32[]{:S(2)}, u32[]{:S(2)}) collective-permute-start(bf16[256,256]{1,0:T(8,128)(2,1)S(1)} %get-tuple-element.12), channel_id=1, source_target_pairs={{0,32},{16,48},{32,0},{48,16},{64,96},{80,112},{96,64},{112,80},{1... | collective-permute-start | bytes 393224 | tf_op jit(solution)/shard_map/ppermute | solution.py:292
  60.1 9.2 %collective-permute-start.4 = (bf16[256,256]{1,0:T(8,128)(2,1)S(1)}, bf16[256,256]{1,0:T(8,128)(2,1)S(1)}, u32[]{:S(2)}, u32[]{:S(2)}) collective-permute-start(bf16[256,256]{1,0:T(8,128)(2,1)S(1)} %get-tuple-element.13), channel_id=1, source_target_pairs={{0,48},{16,0},{32,16},{48,32},{64,112},{80,64},{96,80},{112,96},{1... | collective-permute-start | bytes 393224 | tf_op jit(solution)/shard_map/ppermute | solution.py:292
  69.4 0.8 copy-start.2
  73.3 7.6 %copy-start.3 = (f32[5376]{0:T(1024)S(1)}, f32[5376]{0:T(1024)}, u32[]{:S(2)}) copy-start(f32[5376]{0:T(1024)} %param.17) | copy-start | bytes 64516
  73.3 7.6 %copy-start.4 = (f32[5376]{0:T(1024)S(1)}, f32[5376]{0:T(1024)}, u32[]{:S(2)}) copy-start(f32[5376]{0:T(1024)} %param.18) | copy-start | bytes 64516
  73.3 28.7 %all-to-all-start = ((bf16[16,8,5760]{2,1,0:T(8,128)(2,1)}), bf16[16,8,5760]{2,1,0:T(8,128)(2,1)S(1)}, u32[]{:S(2)}, u32[]{:S(2)}) async-start(bf16[16,8,5760]{2,1,0:T(8,128)(2,1)} %first_layer.1), calls=%async_computation | async-start | bytes 2949120 | tf_op jit(solution)/shard_map/all_to_all | solution.py:283
  103.7 24.8 %all-to-all-start.1 = ((bf16[16,8,5760]{2,1,0:T(8,128)(2,1)}), bf16[16,8,5760]{2,1,0:T(8,128)(2,1)S(1)}, u32[]{:S(2)}, u32[]{:S(2)}) async-start(bf16[16,8,5760]{2,1,0:T(8,128)(2,1)} %norms.1), calls=%async_computation.1 | async-start | bytes 2949120 | tf_op jit(solution)/shard_map/all_to_all | solution.py:283
  132.4 35.5 %all-to-all-start.3 = ((bf16[8,128,256]{2,1,0:T(8,128)(2,1)}), bf16[8,128,256]{2,1,0:T(8,128)(2,1)S(1)}, u32[]{:S(2)}, u32[]{:S(2)}) async-start(bf16[8,128,256]{2,1,0:T(8,128)(2,1)} %get-tuple-element.17), calls=%async_computation.3 | async-start | bytes 1048576 | tf_op jit(solution)/shard_map/all_to_all | solution.py:419
  141.3 11.8 %collective-permute-start.5 = (bf16[64,256]{1,0:T(8,128)(2,1)S(1)}, bf16[64,256]{1,0:T(8,128)(2,1)S(1)}, u32[]{:S(2)}, u32[]{:S(2)}) collective-permute-start(bf16[64,256]{1,0:T(8,128)(2,1)S(1)} %get-tuple-element.16), channel_id=1, source_target_pairs={{0,496},{16,480},{32,464},{48,448},{64,432},{80,416},{96,400},{112... | collective-permute-start | bytes 98312 | tf_op jit(solution)/shard_map/ppermute | solution.py:296
  171.7 14.9 %all-to-all-start.4 = ((bf16[4,128,384]{2,1,0:T(8,128)(2,1)}), bf16[4,128,384]{2,1,0:T(8,128)(2,1)S(1)}, u32[]{:S(2)}, u32[]{:S(2)}) async-start(bf16[4,128,384]{2,1,0:T(8,128)(2,1)} %second_layer.1), calls=%async_computation.4 | async-start | bytes 786432 | tf_op jit(solution)/shard_map/all_to_all | solution.py:287
Sparse Core Ops, SparseCore 0:
  37.3 67.7 all-gather.1

commit v5 on v3

--- a/solution.py
+++ b/solution.py
@@ -25,8 +25,10 @@
 ROWS = TOK // N_HEADS
 NEG = -1e30
 Y_GROUPS = [[z * Y_HI + y for y in range(Y_HI)] for z in range(Z)]
-GROUP = 16
-HALF_GROUPS = [list(range(GROUP)), list(range(GROUP, N_CTX))]
+LEVEL_PAIRS = [
+    [z * Y_HI + y for y in range(Y_HI)] + [(Z - 1 - z) * Y_HI + y for y in range(Y_HI)]
+    for z in range(Z // 2)
+]
 Z_GROUPS = [[z * Y_HI + y for z in range(Z)] for y in range(Y_HI)]
 VMEM_LIMIT = 24 * 1024 * 1024
 
@@ -197,7 +199,7 @@
             query[:, head * HEAD_SIZE : (head + 1) * HEAD_SIZE] = values
         else:
             block[:, (head - 2) * HEAD_SIZE : (head - 1) * HEAD_SIZE] = values
-    moves = [pltpu.make_async_copy(block, pair.at[peer], out_sem.at[peer]) for peer in range(GROUP)]
+    moves = [pltpu.make_async_copy(block, pair.at[member], out_sem.at[member]) for member in range(Z)]
     for move in moves:
         move.start()
     for move in moves:
@@ -217,57 +219,58 @@
     return terms
 
 
-def second_kernel(base, own_query, other_query, pair, low, kept, kept_log, sent, scores):
+def second_kernel(base, queries, pair, low, sent, scores):
+    place_z, place_y, upper = base[0], base[1], base[2]
     lane = lax.broadcasted_iota(jnp.int32, (1, CHUNK), 1)
+    lane = jnp.where(lane < TOK, lane, lane + (Y_HI - 1) * TOK)
     row = lax.broadcasted_iota(jnp.int32, (2 * TOK, 1), 0)
-    slot = lax.broadcasted_iota(jnp.int32, (HALF, HEAD_SIZE), 1)
-    for index, query in enumerate((own_query, other_query)):
-        stacked = jnp.concatenate([query[:, :HEAD_SIZE], query[:, HEAD_SIZE:]], axis=0)
-        lowest = low[index * TOK : (index + 1) * TOK, :1]
+    slot = lax.broadcasted_iota(jnp.int32, (TOK, HEAD_SIZE), 1)
+    chunks = []
+    for at in range(0, Z * TOK, CHUNK):
+        chunks.append(
+            (
+                lambda at=at: (pair[at : at + CHUNK, :HEAD_SIZE], pair[at : at + CHUNK, HEAD_SIZE:]),
+                at * Y_HI + place_y * TOK + lane,
+            )
+        )
+    for peer in range(Y_HI):
+        block = queries[peer * TOK : (peer + 1) * TOK, :]
+        stacked = jnp.concatenate([block[:, :HEAD_SIZE], block[:, HEAD_SIZE:]], axis=0)
+        lowest = low[peer * TOK : (peer + 1) * TOK, :1]
         lowest = jnp.concatenate([lowest, lowest], axis=0)
-        high = base[1 + index] + lax.rem(row, TOK)
-        chunks = []
-        for at in range(0, GROUP * TOK, CHUNK):
-            chunks.append(
-                (
-                    lambda at=at: (
-                        pair[at : at + CHUNK, :HEAD_SIZE],
-                        pair[at : at + CHUNK, HEAD_SIZE:],
-                    ),
-                    base[0] + at + lane,
-                )
-            )
+        high = (place_z * Y_HI + peer) * TOK + lax.rem(row, TOK)
         mixed, logs = softmax_rows(stacked, chunks, lowest, high, scores)
-        for half in range(2):
-            rows = slice(half * HALF, (half + 1) * HALF)
-            pieces = [slice(half * HALF + head * TOK, (half + 1) * HALF + head * TOK) for head in range(2)]
-            if half == index:
-                for head in range(2):
-                    kept[rows, head * HEAD_SIZE : (head + 1) * HEAD_SIZE] = mixed[pieces[head]]
-                kept_log[rows, :] = jnp.where(slot < 3, logs[pieces[0]], logs[pieces[1]])
-            else:
-                packed = jnp.zeros((HALF, HEAD_SIZE), jnp.float32)
-                for head in range(2):
-                    sent[rows, head * HEAD_SIZE : (head + 1) * HEAD_SIZE] = mixed[
-                        pieces[head]
-                    ].astype(jnp.bfloat16)
-                    for place, term in enumerate(three_terms(logs[pieces[head]])):
-                        packed = jnp.where(slot == 3 * head + place, term, packed)
-                sent[rows, 2 * HEAD_SIZE :] = packed.astype(jnp.bfloat16)
-
-
-def combine_kernel(kept, kept_log, got, out):
-    packed = got[:, 2 * HEAD_SIZE :].astype(jnp.float32)
-    for head in range(2):
-        cols = slice(head * HEAD_SIZE, (head + 1) * HEAD_SIZE)
-        mine = kept_log[:, 3 * head : 3 * head + 1]
-        at = 3 * head
-        theirs = packed[:, at : at + 1] + packed[:, at + 1 : at + 2] + packed[:, at + 2 : at + 3]
-        top = jnp.maximum(mine, theirs)
-        mine = jnp.exp(mine - top)
-        theirs = jnp.exp(theirs - top)
-        mixed = kept[:, cols] * mine + got[:, cols].astype(jnp.float32) * theirs
-        out[:, cols] = (mixed / (mine + theirs)).astype(jnp.bfloat16)
+        packed = jnp.zeros((TOK, HEAD_SIZE), jnp.float32)
+        pieces = []
+        for head in range(2):
+            rows = slice(head * TOK, (head + 1) * TOK)
+            pieces.append(mixed[rows])
+            for place, term in enumerate(three_terms(logs[rows])):
+                packed = jnp.where(slot == 3 * head + place, term, packed)
+        whole_rows = jnp.concatenate(pieces + [packed], axis=1).astype(jnp.bfloat16)
+        sent[peer + Y_HI * upper] = whole_rows[:HALF]
+        sent[Y_HI - 1 - peer + Y_HI * (1 - upper)] = whole_rows[HALF:]
+
+
+def combine_kernel(base, got, out):
+    for half in range(2):
+        upper = base[2] if half == 0 else 1 - base[2]
+        parts = [got[peer + Y_HI * upper].astype(jnp.float32) for peer in range(Y_HI)]
+        for head in range(2):
+            at = 2 * HEAD_SIZE + 3 * head
+            logs = [
+                part[:, at : at + 1] + part[:, at + 1 : at + 2] + part[:, at + 2 : at + 3]
+                for part in parts
+            ]
+            top = jnp.maximum(jnp.maximum(logs[0], logs[1]), jnp.maximum(logs[2], logs[3]))
+            cols = slice(head * HEAD_SIZE, (head + 1) * HEAD_SIZE)
+            mixed = jnp.zeros((HALF, HEAD_SIZE), jnp.float32)
+            total = jnp.zeros((HALF, 1), jnp.float32)
+            for part, log in zip(parts, logs):
+                weight = jnp.exp(log - top)
+                mixed = mixed + weight * part[:, cols]
+                total = total + weight
+            out[half * HALF : (half + 1) * HALF, cols] = (mixed / total).astype(jnp.bfloat16)
 
 
 def exchange_heads(value):
@@ -276,10 +279,6 @@
 
 def exchange_y(value):
     return lax.all_to_all(value, "ctx", 0, 0, tiled=True, axis_index_groups=Y_GROUPS)
-
-
-def mirror(value):
-    return lax.ppermute(value, "ctx", [(i, N_CTX - 1 - i) for i in range(N_CTX)])
 
 
 def ctx_shift(value, steps):
@@ -325,6 +324,7 @@
     weights = exchange_y(spread).reshape(-1, 4 * HEAD_SIZE)
     weights = lax.all_gather(weights, "ctx", axis=0, tiled=True, axis_index_groups=Z_GROUPS)
 
+    bases = jnp.stack([place_z, place_y, place_z // (Z // 2)])
     later = jnp.concatenate([own, back_one], axis=0)
     earlier = jnp.concatenate([back_one, back_two], axis=0)
     peers = jnp.arange(Y_HI, dtype=jnp.int32)[:, None, None]
@@ -348,7 +348,7 @@
         ),
         name="first_layer",
     )(
-        jnp.stack([place_z, place_y]),
+        bases,
         first_layer_queries,
         blocks,
         back_two,
@@ -378,7 +378,7 @@
         project_kernel,
         out_shape=(
             jax.ShapeDtypeStruct((TOK, 2 * HEAD_SIZE), bf16),
-            jax.ShapeDtypeStruct((GROUP, TOK, 2 * HEAD_SIZE), bf16),
+            jax.ShapeDtypeStruct((Z, TOK, 2 * HEAD_SIZE), bf16),
         ),
         in_specs=[whole(), whole(pltpu.HBM), whole(), whole()],
         out_specs=(whole(), whole(pltpu.HBM)),
@@ -386,45 +386,41 @@
             pltpu.VMEM((WIDTH, 4 * HEAD_SIZE), bf16),
             pltpu.VMEM((TOK, 2 * HEAD_SIZE), bf16),
             pltpu.SemaphoreType.DMA((PARTS,)),
-            pltpu.SemaphoreType.DMA((GROUP,)),
+            pltpu.SemaphoreType.DMA((Z,)),
         ],
-        compiler_params=pltpu.CompilerParams(vmem_limit_bytes=52 * 1024 * 1024),
+        compiler_params=pltpu.CompilerParams(vmem_limit_bytes=50 * 1024 * 1024),
         name="project",
     )(got, weights, turn_cos, turn_sin)
 
-    pairs = lax.all_to_all(
-        pair, "ctx", 0, 0, tiled=True, axis_index_groups=HALF_GROUPS
-    ).reshape(GROUP * TOK, 2 * HEAD_SIZE)
-    other_query = mirror(query)
-
-    other_start = (N_CTX - 1 - ctx_place) * TOK
-    other_pos = lax.dynamic_slice_in_dim(positions, other_start, TOK, 0)
-    other_tokens = other_start + jnp.arange(TOK, dtype=jnp.int32)
-    low_two = jnp.concatenate([tokens - local_pos, other_tokens - other_pos])
-    low_two = jnp.broadcast_to(low_two[:, None], (2 * TOK, 128))
-    bases = jnp.stack([(ctx_place // GROUP) * (GROUP * TOK), start, other_start])
-    kept, kept_log, sent = pl.pallas_call(
+    pairs = lax.all_to_all(pair, "ctx", 0, 0, tiled=True, axis_index_groups=Z_GROUPS)
+    pairs = pairs.reshape(Z * TOK, 2 * HEAD_SIZE)
+    queries = lax.all_gather(
+        query, "ctx", axis=0, tiled=True, axis_index_groups=Y_GROUPS
+    )
+
+    level = Y_HI * TOK
+    first = place_z * level
+    low_two = first + jnp.arange(level, dtype=jnp.int32)
+    low_two = low_two - lax.dynamic_slice_in_dim(positions, first, level, 0)
+    low_two = jnp.broadcast_to(low_two[:, None], (level, 128))
+    sent = pl.pallas_call(
         second_kernel,
-        out_shape=(
-            jax.ShapeDtypeStruct((TOK, 2 * HEAD_SIZE), f32),
-            jax.ShapeDtypeStruct((TOK, HEAD_SIZE), f32),
-            jax.ShapeDtypeStruct((TOK, 3 * HEAD_SIZE), bf16),
-        ),
-        in_specs=[whole(pltpu.SMEM)] + [whole()] * 4,
-        out_specs=(whole(), whole(), whole()),
-        scratch_shapes=[pltpu.VMEM((2 * TOK, GROUP * TOK), f32)],
+        out_shape=jax.ShapeDtypeStruct((2 * Y_HI, HALF, 3 * HEAD_SIZE), bf16),
+        in_specs=[whole(pltpu.SMEM)] + [whole()] * 3,
+        out_specs=whole(),
+        scratch_shapes=[pltpu.VMEM((2 * TOK, Z * TOK), f32)],
         compiler_params=params(),
         name="second_layer",
-    )(bases, query, other_query, pairs, low_two)
-    got = mirror(sent)
+    )(bases, queries, pairs, low_two)
+    got = lax.all_to_all(sent, "ctx", 0, 0, tiled=True, axis_index_groups=LEVEL_PAIRS)
     attended = pl.pallas_call(
         combine_kernel,
         out_shape=jax.ShapeDtypeStruct((TOK, 2 * HEAD_SIZE), bf16),
-        in_specs=[whole()] * 3,
+        in_specs=[whole(pltpu.SMEM), whole()],
         out_specs=whole(),
         compiler_params=params(),
         name="combine",
-    )(kept, kept_log, got)
+    )(bases, got)
     return (resid_out, attended)
 
 

time: 196 us -> 188 us (0.959)
  the two profiles are of different devices: /device:TPU:22 before, /device:TPU:6 now
where the time goes in v5:
time: 188 us; the launch traced here: 187 us
  waiting for transfers between devices  72.4 us (39%)
  blocking collectives  42 us (22%)
  starting transfers between devices  36.3 us (19%)
  Pallas kernels  16.5 us (9%)
  between operations  14.3 us (8%)
  other arithmetic  3.79 us (2%)
  local copies, waits for them, and re-layouts  2.03 us (1%)
    all_to_all x2, waiting for transfers between devices, exchange_heads(): return lax.all_to_all(value, 'heads', 0, 0, tiled=True)  38.7 us
    all_to_all x1, blocking collectives, exchange_y(): lax.all_to_all(value, 'ctx', 0, 0, tiled=True, axis_index_groups=Y_GROUPS)  27.4 us
    all_gather x1, blocking collectives, shards(): lax.all_gather(query, 'ctx', axis=0, tiled=True, axis_index_groups=Y_GROUPS)  14.6 us
    all_to_all x1, waiting for transfers between devices, shards(): lax.all_to_all(sent, 'ctx', 0, 0, tiled=True, axis_index_groups=LEVEL_PAIRS)  14.6 us
    all_to_all x2, starting transfers between devices, exchange_heads(): return lax.all_to_all(value, 'heads', 0, 0, tiled=True)  11.2 us
    ppermute x2, starting transfers between devices, ctx_shift(): lax.ppermute(value, 'ctx', [(i, (i + steps) % N_CTX) for i in range(N_CTX)])  10.6 us
    all_to_all x1, waiting for transfers between devices, exchange_y(): lax.all_to_all(value, 'ctx', 0, 0, tiled=True, axis_index_groups=Y_GROUPS)  10.3 us
    all_to_all x1, starting transfers between devices, shards(): lax.all_to_all(pair, 'ctx', 0, 0, tiled=True, axis_index_groups=Z_GROUPS)  6.87 us
  transfers between devices with their start and end apart: 8, of which 7 were waited for; matrix products, arithmetic and copies ran while one was open for 3% of the time, Pallas kernels for 3%

profile of v5, /device:TPU:6, one launch (start us, length us, event | category | flops | bytes accessed | tf_op | source)
XLA Modules:
  0.0 187.3 jit_solution(8950216302360251514)
XLA Ops:
  7.2 2.5 %prepare.1 = (bf16[128,256]{1,0:T(8,128)(2,1)}, bf16[4,168,512]{2,1,0:T(8,128)(2,1)}) custom-call(bf16[128,128]{1,0:T(8,128)(2,1)} %keys.1, bf16[128,128]{1,0:T(8,128)(2,1)} %values.1, bf16[168,256]{1,0:T(8,128)(2,1)} %proj_query.1, bf16[168,128]{1,0:T(8,128)(2,1)} %key_projection.1, bf16[168,128]{1,0:T(8,128)(2,1)} %value_projection.1), custom_call_target="tpu_custom_call" | custom-call | tf_op jit(solution)/shard_map/prepare/pallas_call | solution.py:307
  9.7 27.4 %all_to_all.30 = bf16[4,168,512]{2,1,0:T(8,128)(2,1)} all-to-all(bf16[4,168,512]{2,1,0:T(8,128)(2,1)} %get-tuple-element.7), channel_id=1, replica_groups={{0,16,32,48},{64,80,96,112},{128,144,160,176},{192,208,224,240},{256,27..., dimensions={0} | all-to-all | bytes 1376256 | tf_op jit(solution)/shard_map/all_to_all | solution.py:281
  37.2 4.5 %collective-permute-start = (bf16[128,256]{1,0:T(8,128)(2,1)S(1)}, bf16[128,256]{1,0:T(8,128)(2,1)S(1)}, u32[]{:S(2)}, u32[]{:S(2)}) collective-permute-start(bf16[128,256]{1,0:T(8,128)(2,1)S(1)} %copy-done.2), channel_id=1, source_target_pairs={{0,64},{16,80},{32,96},{48,112},{64,128},{80,144},{96,160},{112,17... | collective-permute-start | bytes 196616 | tf_op jit(solution)/shard_map/ppermute | solution.py:285
  41.7 6.1 %collective-permute-start.1 = (bf16[128,256]{1,0:T(8,128)(2,1)S(1)}, bf16[128,256]{1,0:T(8,128)(2,1)S(1)}, u32[]{:S(2)}, u32[]{:S(2)}) collective-permute-start(bf16[128,256]{1,0:T(8,128)(2,1)S(1)} %copy-done.2), channel_id=1, source_target_pairs={{0,128},{16,144},{32,160},{48,176},{64,192},{80,208},{96,224},{112... | collective-permute-start | bytes 196616 | tf_op jit(solution)/shard_map/ppermute | solution.py:285
  47.8 3.5 %collective-permute-done = bf16[128,256]{1,0:T(8,128)(2,1)S(1)} collective-permute-done((bf16[128,256]{1,0:T(8,128)(2,1)S(1)}, bf16[128,256]{1,0:T(8,128)(2,1)S(1)}, u32[]{:S(2)}, u32[]{:S(2)}) %collective-permute-start) | collective-permute-done | bytes 65568 | tf_op jit(solution)/shard_map/ppermute | solution.py:285
  51.3 2.7 %collective-permute-done.1.last = bf16[128,256]{1,0:T(8,128)(2,1)S(1)} collective-permute-done((bf16[128,256]{1,0:T(8,128)(2,1)S(1)}, bf16[128,256]{1,0:T(8,128)(2,1)S(1)}, u32[]{:S(2)}, u32[]{:S(2)}) %collective-permute-start.1) | collective-permute-done | bytes 65568 | tf_op jit(solution)/shard_map/ppermute | solution.py:285
  54.0 0.9 broadcast_select_fusion
  54.9 3.5 %all-to-all-start = ((bf16[4,256,256]{2,1,0:T(8,128)(2,1)}), bf16[4,256,256]{2,1,0:T(8,128)(2,1)S(1)}, u32[]{:S(2)}, u32[]{:S(2)}) async-start(bf16[4,256,256]{2,1,0:T(8,128)(2,1)} %broadcast_select_fusion), calls=%async_computation | async-start | bytes 1048576 | tf_op jit(solution)/shard_map/all_to_all | solution.py:281
  58.4 1.0 copy.14.resid
  60.4 10.3 %all-to-all-done.blocks = bf16[4,256,256]{2,1,0:T(8,128)(2,1)S(1)} async-done(((bf16[4,256,256]{2,1,0:T(8,128)(2,1)}), bf16[4,256,256]{2,1,0:T(8,128)(2,1)S(1)}, u32[]{:S(2)}, u32[]{:S(2)}) %all-to-all-start) | async-done | bytes 524320 | tf_op jit(solution)/shard_map/all_to_all | solution.py:281
  70.8 3.1 %first_layer.1 = bf16[16,8,5760]{2,1,0:T(8,128)(2,1)} custom-call(s32[3]{0:T(128)S(1)} %pad_add_fusion.base, bf16[128,256]{1,0:T(8,128)(2,1)S(1)} %copy-done.1, bf16[4,256,256]{2,1,0:T(8,128)(2,1)S(1)} %all-to-all-done.blocks, bf16[128,256]{1,0:T(8,128)(2,1)S(1)} %collective-permute-done.1.last, s32[256,128]{1,0:T(8,128)S(1)} %broadcast_in_dim.52.low, ...), custom_call_target="tpu_custom_call" | custom-call | flops 600000000 | bytes 6000000 | tf_op jit(solution)/shard_map/first_layer/pallas_call | solution.py:339
  73.9 6.4 %all-to-all-start.1 = ((bf16[16,8,5760]{2,1,0:T(8,128)(2,1)}), bf16[16,8,5760]{2,1,0:T(8,128)(2,1)S(1)}, u32[]{:S(2)}, u32[]{:S(2)}) async-start(bf16[16,8,5760]{2,1,0:T(8,128)(2,1)} %first_layer.1), calls=%async_computation.1 | async-start | bytes 2949120 | tf_op jit(solution)/shard_map/all_to_all | solution.py:277
  80.3 19.9 %all-to-all-done.1.got = bf16[16,8,5760]{2,1,0:T(8,128)(2,1)S(1)} async-done(((bf16[16,8,5760]{2,1,0:T(8,128)(2,1)}), bf16[16,8,5760]{2,1,0:T(8,128)(2,1)S(1)}, u32[]{:S(2)}, u32[]{:S(2)}) %all-to-all-start.1) | async-done | bytes 1474592 | tf_op jit(solution)/shard_map/all_to_all | solution.py:277
  100.1 1.7 norms.1
  101.9 4.9 %all-to-all-start.2 = ((bf16[16,8,5760]{2,1,0:T(8,128)(2,1)}), bf16[16,8,5760]{2,1,0:T(8,128)(2,1)S(1)}, u32[]{:S(2)}, u32[]{:S(2)}) async-start(bf16[16,8,5760]{2,1,0:T(8,128)(2,1)} %norms.1), calls=%async_computation.2 | async-start | bytes 2949120 | tf_op jit(solution)/shard_map/all_to_all | solution.py:277
  107.9 18.8 %all-to-all-done.2.got = bf16[16,8,5760]{2,1,0:T(8,128)(2,1)S(1)} async-done(((bf16[16,8,5760]{2,1,0:T(8,128)(2,1)}), bf16[16,8,5760]{2,1,0:T(8,128)(2,1)S(1)}, u32[]{:S(2)}, u32[]{:S(2)}) %all-to-all-start.2) | async-done | bytes 1474592 | tf_op jit(solution)/shard_map/all_to_all | solution.py:277
  126.7 3.8 %project.1 = (bf16[128,256]{1,0:T(8,128)(2,1)S(1)}, bf16[8,128,256]{2,1,0:T(8,128)(2,1)}) custom-call(bf16[16,8,5760]{2,1,0:T(8,128)(2,1)S(1)} %all-to-all-done.2.got, bf16[5376,512]{1,0:T(8,128)(2,1)} %all-gather.2.cloned.1.call-done.weights, f32[128,128]{1,0:T(8,128)S(1)} %get-tuple-element.19.turn_cos, f32[128,128]{1,0:T(8,128)S(1)} %get-tuple-element.20.turn_sin), custom_call_target="tpu_custom_call" | custom-call | tf_op jit(solution)/shard_map/project/pallas_call | solution.py:377
  130.6 6.9 %all-to-all-start.4 = ((bf16[8,128,256]{2,1,0:T(8,128)(2,1)}), bf16[8,128,256]{2,1,0:T(8,128)(2,1)S(1)}, u32[]{:S(2)}, u32[]{:S(2)}) async-start(bf16[8,128,256]{2,1,0:T(8,128)(2,1)} %get-tuple-element.9), calls=%async_computation.4 | async-start | bytes 1048576 | tf_op jit(solution)/shard_map/all_to_all | solution.py:395
  138.2 14.6 %all_gather.7.queries = bf16[512,256]{1,0:T(8,128)(2,1)S(1)} all-gather(bf16[128,256]{1,0:T(8,128)(2,1)S(1)} %get-tuple-element.8), channel_id=1, replica_groups={{0,16,32,48},{64,80,96,112},{128,144,160,176},{192,208,224,240},{256,27..., dimensions={0}, use_global_device_ids=true | all-gather | bytes 327680 | tf_op jit(solution)/shard_map/all_gather | solution.py:397
  152.8 2.7 %all-to-all-done.4 = bf16[8,128,256]{2,1,0:T(8,128)(2,1)S(1)} async-done(((bf16[8,128,256]{2,1,0:T(8,128)(2,1)}), bf16[8,128,256]{2,1,0:T(8,128)(2,1)S(1)}, u32[]{:S(2)}, u32[]{:S(2)}) %all-to-all-start.4) | async-done | bytes 524320 | tf_op jit(solution)/shard_map/all_to_all | solution.py:395
  155.6 3.7 %second_layer.1 = bf16[8,64,384]{2,1,0:T(8,128)(2,1)} custom-call(s32[3]{0:T(128)S(1)} %pad_add_fusion.base, bf16[512,256]{1,0:T(8,128)(2,1)S(1)} %all_gather.7.queries, bf16[1024,256]{1,0:T(8,128)(2,1)S(1)} %bitcast.9, s32[512,128]{1,0:T(8,128)S(1)} %broadcast_in_dim.55.low), custom_call_target="tpu_custom_call" | custom-call | tf_op jit(solution)/shard_map/second_layer/pallas_call | solution.py:406
  159.3 4.1 %all-to-all-start.5 = ((bf16[8,64,384]{2,1,0:T(8,128)(2,1)}), bf16[8,64,384]{2,1,0:T(8,128)(2,1)S(1)}, u32[]{:S(2)}, u32[]{:S(2)}) async-start(bf16[8,64,384]{2,1,0:T(8,128)(2,1)} %second_layer.1), calls=%async_computation.5 | async-start | bytes 786432 | tf_op jit(solution)/shard_map/all_to_all | solution.py:415
  164.2 14.6 %all-to-all-done.5.got = bf16[8,64,384]{2,1,0:T(8,128)(2,1)S(1)} async-done(((bf16[8,64,384]{2,1,0:T(8,128)(2,1)}), bf16[8,64,384]{2,1,0:T(8,128)(2,1)S(1)}, u32[]{:S(2)}, u32[]{:S(2)}) %all-to-all-start.5) | async-done | bytes 393248 | tf_op jit(solution)/shard_map/all_to_all | solution.py:415
  178.8 1.7 combine.1
  (31 shorter events, 4.0 us)
Async XLA Ops:
  7.2 119.5 %all-gather.2.cloned.1.call-start = ((), (), s32[]{:S(2)}) async-start(), calls=%async_computation.6 | async-start | bytes 6193152 | tf_op jit(solution)/shard_map/all_gather | solution.py:325
  9.7 27.5 %copy-start.2 = (bf16[128,256]{1,0:T(8,128)(2,1)S(1)}, bf16[128,256]{1,0:T(8,128)(2,1)}, u32[]{:S(2)}) copy-start(bf16[128,256]{1,0:T(8,128)(2,1)} %get-tuple-element.6) | copy-start | bytes 196612
  37.1 23.2 %copy-start.5 = (s32[2]{0:T(128)S(1)}, s32[2]{0:T(128)}, u32[]{:S(2)}) copy-start(s32[2]{0:T(128)} %param.22) | copy-start | bytes 28
  37.1 33.7 %copy-start = (bf16[256,5376]{1,0:T(8,128)(2,1)S(1)}, bf16[256,5376]{1,0:T(8,128)(2,1)}, u32[]{:S(2)}) copy-start(bf16[256,5376]{1,0:T(8,128)(2,1)} %out_one.1) | copy-start | bytes 8257540
  37.1 33.6 %copy-start.1 = (bf16[128,256]{1,0:T(8,128)(2,1)S(1)}, bf16[128,256]{1,0:T(8,128)(2,1)}, u32[]{:S(2)}) copy-start(bf16[128,256]{1,0:T(8,128)(2,1)} %query.1) | copy-start | bytes 196612
  37.2 14.2 %collective-permute-start = (bf16[128,256]{1,0:T(8,128)(2,1)S(1)}, bf16[128,256]{1,0:T(8,128)(2,1)S(1)}, u32[]{:S(2)}, u32[]{:S(2)}) collective-permute-start(bf16[128,256]{1,0:T(8,128)(2,1)S(1)} %copy-done.2), channel_id=1, source_target_pairs={{0,64},{16,80},{32,96},{48,112},{64,128},{80,144},{96,160},{112,17... | collective-permute-start | bytes 196616 | tf_op jit(solution)/shard_map/ppermute | solution.py:285
  41.7 12.3 %collective-permute-start.1 = (bf16[128,256]{1,0:T(8,128)(2,1)S(1)}, bf16[128,256]{1,0:T(8,128)(2,1)S(1)}, u32[]{:S(2)}, u32[]{:S(2)}) collective-permute-start(bf16[128,256]{1,0:T(8,128)(2,1)S(1)} %copy-done.2), channel_id=1, source_target_pairs={{0,128},{16,144},{32,160},{48,176},{64,192},{80,208},{96,224},{112... | collective-permute-start | bytes 196616 | tf_op jit(solution)/shard_map/ppermute | solution.py:285
  54.9 15.8 %all-to-all-start = ((bf16[4,256,256]{2,1,0:T(8,128)(2,1)}), bf16[4,256,256]{2,1,0:T(8,128)(2,1)S(1)}, u32[]{:S(2)}, u32[]{:S(2)}) async-start(bf16[4,256,256]{2,1,0:T(8,128)(2,1)} %broadcast_select_fusion), calls=%async_computation | async-start | bytes 1048576 | tf_op jit(solution)/shard_map/all_to_all | solution.py:281
  73.9 6.4 %copy-start.3 = (f32[5376]{0:T(1024)S(1)}, f32[5376]{0:T(1024)}, u32[]{:S(2)}) copy-start(f32[5376]{0:T(1024)} %param.17) | copy-start | bytes 64516
  73.9 6.4 %copy-start.4 = (f32[5376]{0:T(1024)S(1)}, f32[5376]{0:T(1024)}, u32[]{:S(2)}) copy-start(f32[5376]{0:T(1024)} %param.18) | copy-start | bytes 64516
  73.9 26.3 %all-to-all-start.1 = ((bf16[16,8,5760]{2,1,0:T(8,128)(2,1)}), bf16[16,8,5760]{2,1,0:T(8,128)(2,1)S(1)}, u32[]{:S(2)}, u32[]{:S(2)}) async-start(bf16[16,8,5760]{2,1,0:T(8,128)(2,1)} %first_layer.1), calls=%async_computation.1 | async-start | bytes 2949120 | tf_op jit(solution)/shard_map/all_to_all | solution.py:277
  101.9 24.9 %all-to-all-start.2 = ((bf16[16,8,5760]{2,1,0:T(8,128)(2,1)}), bf16[16,8,5760]{2,1,0:T(8,128)(2,1)S(1)}, u32[]{:S(2)}, u32[]{:S(2)}) async-start(bf16[16,8,5760]{2,1,0:T(8,128)(2,1)} %norms.1), calls=%async_computation.2 | async-start | bytes 2949120 | tf_op jit(solution)/shard_map/all_to_all | solution.py:277
  130.6 24.9 %all-to-all-start.4 = ((bf16[8,128,256]{2,1,0:T(8,128)(2,1)}), bf16[8,128,256]{2,1,0:T(8,128)(2,1)S(1)}, u32[]{:S(2)}, u32[]{:S(2)}) async-start(bf16[8,128,256]{2,1,0:T(8,128)(2,1)} %get-tuple-element.9), calls=%async_computation.4 | async-start | bytes 1048576 | tf_op jit(solution)/shard_map/all_to_all | solution.py:395
  159.3 19.5 %all-to-all-start.5 = ((bf16[8,64,384]{2,1,0:T(8,128)(2,1)}), bf16[8,64,384]{2,1,0:T(8,128)(2,1)S(1)}, u32[]{:S(2)}, u32[]{:S(2)}) async-start(bf16[8,64,384]{2,1,0:T(8,128)(2,1)} %second_layer.1), calls=%async_computation.5 | async-start | bytes 786432 | tf_op jit(solution)/shard_map/all_to_all | solution.py:415
Sparse Core Ops, SparseCore 0:
  37.3 70.7 all-gather.1

commit v6 on v5

--- a/solution.py
+++ b/solution.py
@@ -174,21 +174,26 @@
         move.wait()
 
 
-def project_kernel(
-    got, weights, turn_cos, turn_sin, query, pair, held, block, in_sem, out_sem
-):
+def project_kernel(base, got, *refs):
+    pieces, refs = refs[: Z + 1], refs[Z + 1 :]
+    turn_cos, turn_sin, query, pair, held, block, in_sem, out_sem = refs
+    level_rows = WIDTH // Z
+    offsets = [0, -1, 1, -2, 2, -3, 3, 4, 4]
+    for index, (piece, offset) in enumerate(zip(pieces, offsets)):
+        level = lax.rem(base[0] + (offset + Z), Z)
+        at = level * level_rows + (level_rows // 2 if index == Z else 0)
+        target = held.at[pl.ds(pl.multiple_of(at, 16), piece.shape[0])]
+        pltpu.make_async_copy(piece, target, in_sem.at[level]).start()
     depth = WIDTH // PARTS
-    spans = [slice(part * depth, (part + 1) * depth) for part in range(PARTS)]
-    moves = [
-        pltpu.make_async_copy(weights.at[span], held.at[span], in_sem.at[part])
-        for part, span in enumerate(spans)
-    ]
-    for move in moves:
-        move.start()
     total = jnp.zeros((TOK, 4 * HEAD_SIZE), jnp.float32)
-    for move, span in zip(moves, spans):
+    arrived = 0
+    for part in range(PARTS):
+        span = slice(part * depth, (part + 1) * depth)
         rows = got[:, :, span].astype(jnp.float32).reshape(TOK, depth).astype(jnp.bfloat16)
-        move.wait()
+        while arrived * level_rows < (part + 1) * depth:
+            rows_of = slice(arrived * level_rows, (arrived + 1) * level_rows)
+            pltpu.make_async_copy(pieces[0], held.at[rows_of], in_sem.at[arrived]).wait()
+            arrived += 1
         total = total + jnp.dot(rows, held[span, :], preferred_element_type=jnp.float32)
     for head in range(4):
         values = total[:, head * HEAD_SIZE : (head + 1) * HEAD_SIZE]
@@ -322,9 +327,19 @@
     back_one = ctx_shift(own, Y_HI)
     back_two = ctx_shift(own, 2 * Y_HI)
     weights = exchange_y(spread).reshape(-1, 4 * HEAD_SIZE)
-    weights = lax.all_gather(weights, "ctx", axis=0, tiled=True, axis_index_groups=Z_GROUPS)
-
     bases = jnp.stack([place_z, place_y, place_z // (Z // 2)])
+    pieces = [weights]
+    upward, downward = weights, weights
+    for _ in range(1, Z // 2):
+        upward = ctx_shift(upward, Y_HI)
+        downward = ctx_shift(downward, -Y_HI)
+        pieces += [upward, downward]
+    half_rows = weights.shape[0] // 2
+    upward, downward = upward[:half_rows], downward[half_rows:]
+    upward = ctx_shift(upward, Y_HI)
+    downward = ctx_shift(downward, -Y_HI)
+    pieces += [upward, downward]
+
     later = jnp.concatenate([own, back_one], axis=0)
     earlier = jnp.concatenate([back_one, back_two], axis=0)
     peers = jnp.arange(Y_HI, dtype=jnp.int32)[:, None, None]
@@ -380,17 +395,17 @@
             jax.ShapeDtypeStruct((TOK, 2 * HEAD_SIZE), bf16),
             jax.ShapeDtypeStruct((Z, TOK, 2 * HEAD_SIZE), bf16),
         ),
-        in_specs=[whole(), whole(pltpu.HBM), whole(), whole()],
+        in_specs=[whole(pltpu.SMEM), whole()] + [whole(pltpu.HBM)] * (Z + 1) + [whole(), whole()],
         out_specs=(whole(), whole(pltpu.HBM)),
         scratch_shapes=[
             pltpu.VMEM((WIDTH, 4 * HEAD_SIZE), bf16),
             pltpu.VMEM((TOK, 2 * HEAD_SIZE), bf16),
-            pltpu.SemaphoreType.DMA((PARTS,)),
+            pltpu.SemaphoreType.DMA((Z,)),
             pltpu.SemaphoreType.DMA((Z,)),
         ],
         compiler_params=pltpu.CompilerParams(vmem_limit_bytes=50 * 1024 * 1024),
         name="project",
-    )(got, weights, turn_cos, turn_sin)
+    )(bases, got, *pieces, turn_cos, turn_sin)
 
     pairs = lax.all_to_all(pair, "ctx", 0, 0, tiled=True, axis_index_groups=Z_GROUPS)
     pairs = pairs.reshape(Z * TOK, 2 * HEAD_SIZE)

time: 188 us -> 225 us (1.20)
  the two profiles are of different devices: /device:TPU:6 before, /device:TPU:64 now
where the time goes in v6:
time: 225 us; the launch traced here: 224 us
  waiting for transfers between devices  86.5 us (38%)
  starting transfers between devices  71.5 us (32%)
  blocking collectives  39.9 us (18%)
  Pallas kernels  17.4 us (8%)
  other arithmetic  4.64 us (2%)
  local copies, waits for them, and re-layouts  2.98 us (1%)
    ppermute x10, waiting for transfers between devices, ctx_shift(): lax.ppermute(value, 'ctx', [(i, (i + steps) % N_CTX) for i in range(N_CTX)])  46.5 us
    ppermute x10, starting transfers between devices, ctx_shift(): lax.ppermute(value, 'ctx', [(i, (i + steps) % N_CTX) for i in range(N_CTX)])  37.7 us
    all_to_all x2, waiting for transfers between devices, exchange_y(): lax.all_to_all(value, 'ctx', 0, 0, tiled=True, axis_index_groups=Y_GROUPS)  27.6 us
    all_to_all x1, blocking collectives, exchange_heads(): return lax.all_to_all(value, 'heads', 0, 0, tiled=True)  25.4 us
    all_gather x1, blocking collectives, shards(): lax.all_gather(query, 'ctx', axis=0, tiled=True, axis_index_groups=Y_GROUPS)  14.5 us
    all_to_all x1, waiting for transfers between devices, shards(): lax.all_to_all(sent, 'ctx', 0, 0, tiled=True, axis_index_groups=LEVEL_PAIRS)  12.3 us
    all_to_all x2, starting transfers between devices, exchange_y(): lax.all_to_all(value, 'ctx', 0, 0, tiled=True, axis_index_groups=Y_GROUPS)  11.1 us
    all_to_all x1, starting transfers between devices, shards(): lax.all_to_all(pair, 'ctx', 0, 0, tiled=True, axis_index_groups=Z_GROUPS)  8.4 us
  transfers between devices with their start and end apart: 15, of which 9 were waited for; matrix products, arithmetic and copies ran while one was open for 3% of the time, Pallas kernels for 1%

profile of v6, /device:TPU:64, one launch (start us, length us, event | category | flops | bytes accessed | tf_op | source)
XLA Modules:
  0.0 223.7 jit_solution(214538890593091394)
XLA Ops:
  0.7 2.6 %prepare.1 = (bf16[128,256]{1,0:T(8,128)(2,1)}, bf16[4,168,512]{2,1,0:T(8,128)(2,1)}) custom-call(bf16[128,128]{1,0:T(8,128)(2,1)} %keys.1, bf16[128,128]{1,0:T(8,128)(2,1)} %values.1, bf16[168,256]{1,0:T(8,128)(2,1)} %proj_query.1, bf16[168,128]{1,0:T(8,128)(2,1)} %key_projection.1, bf16[168,128]{1,0:T(8,128)(2,1)} %value_projection.1), custom_call_target="tpu_custom_call" | custom-call | tf_op jit(solution)/shard_map/prepare/pallas_call | solution.py:312
  3.3 6.1 %collective-permute-start.1 = (bf16[128,256]{1,0:T(8,128)(2,1)}, bf16[128,256]{1,0:T(8,128)(2,1)S(1)}, u32[]{:S(2)}, u32[]{:S(2)}) collective-permute-start(bf16[128,256]{1,0:T(8,128)(2,1)} %get-tuple-element.6), channel_id=1, source_target_pairs={{0,128},{16,144},{32,160},{48,176},{64,192},{80,208},{96,224},{112... | collective-permute-start | bytes 196616 | tf_op jit(solution)/shard_map/ppermute | solution.py:290
  9.4 5.5 %collective-permute-start = (bf16[128,256]{1,0:T(8,128)(2,1)}, bf16[128,256]{1,0:T(8,128)(2,1)S(1)}, u32[]{:S(2)}, u32[]{:S(2)}) collective-permute-start(bf16[128,256]{1,0:T(8,128)(2,1)} %get-tuple-element.6), channel_id=1, source_target_pairs={{0,64},{16,80},{32,96},{48,112},{64,128},{80,144},{96,160},{112,17... | collective-permute-start | bytes 196616 | tf_op jit(solution)/shard_map/ppermute | solution.py:290
  19.0 7.1 %all-to-all-start = ((bf16[4,256,256]{2,1,0:T(8,128)(2,1)}), bf16[4,256,256]{2,1,0:T(8,128)(2,1)S(1)}, u32[]{:S(2)}, u32[]{:S(2)}) async-start(bf16[4,256,256]{2,1,0:T(8,128)(2,1)} %broadcast_select_fusion), calls=%async_computation | async-start | bytes 1048576 | tf_op jit(solution)/shard_map/all_to_all | solution.py:286
  28.0 13.3 %all-to-all-done.blocks = bf16[4,256,256]{2,1,0:T(8,128)(2,1)S(1)} async-done(((bf16[4,256,256]{2,1,0:T(8,128)(2,1)}), bf16[4,256,256]{2,1,0:T(8,128)(2,1)S(1)}, u32[]{:S(2)}, u32[]{:S(2)}) %all-to-all-start) | async-done | bytes 524320 | tf_op jit(solution)/shard_map/all_to_all | solution.py:286
  43.4 25.4 %all_to_all.30.got = bf16[16,8,5760]{2,1,0:T(8,128)(2,1)S(1)} all-to-all(bf16[16,8,5760]{2,1,0:T(8,128)(2,1)S(1)} %first_layer.1), channel_id=1, replica_groups=mesh['ctx'=32,'heads'=16] {'heads'}, dimensions={0} | all-to-all | bytes 2949120 | tf_op jit(solution)/shard_map/all_to_all | solution.py:282
  68.7 4.0 %all-to-all-start.3 = ((bf16[4,168,512]{2,1,0:T(8,128)(2,1)}), bf16[4,168,512]{2,1,0:T(8,128)(2,1)S(1)}, u32[]{:S(2)}, u32[]{:S(2)}) async-start(bf16[4,168,512]{2,1,0:T(8,128)(2,1)} %get-tuple-element.7), calls=%async_computation.3 | async-start | bytes 1376256 | tf_op jit(solution)/shard_map/all_to_all | solution.py:286
  74.5 14.3 %all-to-all-done.3 = bf16[4,168,512]{2,1,0:T(8,128)(2,1)S(1)} async-done(((bf16[4,168,512]{2,1,0:T(8,128)(2,1)}), bf16[4,168,512]{2,1,0:T(8,128)(2,1)S(1)}, u32[]{:S(2)}, u32[]{:S(2)}) %all-to-all-start.3) | async-done | bytes 688160 | tf_op jit(solution)/shard_map/all_to_all | solution.py:286
  88.8 7.3 %all-to-all-start.2 = ((bf16[16,8,5760]{2,1,0:T(8,128)(2,1)}), bf16[16,8,5760]{2,1,0:T(8,128)(2,1)}, u32[]{:S(2)}, u32[]{:S(2)}) async-start(bf16[16,8,5760]{2,1,0:T(8,128)(2,1)} %norms.1), calls=%async_computation.2 | async-start | bytes 2949120 | tf_op jit(solution)/shard_map/all_to_all | solution.py:282
  96.1 2.8 %collective-permute-start.2 = (bf16[672,512]{1,0:T(8,128)(2,1)S(1)}, bf16[672,512]{1,0:T(8,128)(2,1)S(1)}, u32[]{:S(2)}, u32[]{:S(2)}) collective-permute-start(bf16[672,512]{1,0:T(8,128)(2,1)S(1)} %bitcast.9), channel_id=1, source_target_pairs={{0,64},{16,80},{32,96},{48,112},{64,128},{80,144},{96,160},{112,17... | collective-permute-start | bytes 2064392 | tf_op jit(solution)/shard_map/ppermute | solution.py:290
  98.8 3.1 %collective-permute-start.3 = (bf16[672,512]{1,0:T(8,128)(2,1)S(1)}, bf16[672,512]{1,0:T(8,128)(2,1)S(1)}, u32[]{:S(2)}, u32[]{:S(2)}) collective-permute-start(bf16[672,512]{1,0:T(8,128)(2,1)S(1)} %bitcast.10), channel_id=1, source_target_pairs={{0,448},{16,464},{32,480},{48,496},{64,0},{80,16},{96,32},{112,48}... | collective-permute-start | bytes 2064392 | tf_op jit(solution)/shard_map/ppermute | solution.py:290
  101.9 14.0 %collective-permute-done.2.refs_1_ = bf16[672,512]{1,0:T(8,128)(2,1)S(1)} collective-permute-done((bf16[672,512]{1,0:T(8,128)(2,1)S(1)}, bf16[672,512]{1,0:T(8,128)(2,1)S(1)}, u32[]{:S(2)}, u32[]{:S(2)}) %collective-permute-start.2) | collective-permute-done | bytes 688160 | tf_op jit(solution)/shard_map/ppermute | solution.py:290
  118.4 4.3 %collective-permute-start.5 = (bf16[672,512]{1,0:T(8,128)(2,1)S(1)}, bf16[672,512]{1,0:T(8,128)(2,1)S(1)}, u32[]{:S(2)}, u32[]{:S(2)}) collective-permute-start(bf16[672,512]{1,0:T(8,128)(2,1)S(1)} %collective-permute-done.3.refs_2_), channel_id=1, source_target_pairs={{0,448},{16,464},{32,480},{48,496},{64,0},{80,16},{96,32},{112,48}... | collective-permute-start | bytes 2064392 | tf_op jit(solution)/shard_map/ppermute | solution.py:290
  122.7 13.2 %collective-permute-done.4.refs_3_ = bf16[672,512]{1,0:T(8,128)(2,1)S(1)} collective-permute-done((bf16[672,512]{1,0:T(8,128)(2,1)S(1)}, bf16[672,512]{1,0:T(8,128)(2,1)S(1)}, u32[]{:S(2)}, u32[]{:S(2)}) %collective-permute-start.4) | collective-permute-done | bytes 688160 | tf_op jit(solution)/shard_map/ppermute | solution.py:290
  137.9 4.9 %collective-permute-start.7 = (bf16[672,512]{1,0:T(8,128)(2,1)S(1)}, bf16[672,512]{1,0:T(8,128)(2,1)S(1)}, u32[]{:S(2)}, u32[]{:S(2)}) collective-permute-start(bf16[672,512]{1,0:T(8,128)(2,1)S(1)} %collective-permute-done.5.refs_4_), channel_id=1, source_target_pairs={{0,448},{16,464},{32,480},{48,496},{64,0},{80,16},{96,32},{112,48}... | collective-permute-start | bytes 2064392 | tf_op jit(solution)/shard_map/ppermute | solution.py:290
  143.5 11.6 %collective-permute-done.6.refs_5_ = bf16[672,512]{1,0:T(8,128)(2,1)S(1)} collective-permute-done((bf16[672,512]{1,0:T(8,128)(2,1)S(1)}, bf16[672,512]{1,0:T(8,128)(2,1)S(1)}, u32[]{:S(2)}, u32[]{:S(2)}) %collective-permute-start.6) | collective-permute-done | bytes 688160 | tf_op jit(solution)/shard_map/ppermute | solution.py:290
  157.1 4.9 %collective-permute-start.9 = (bf16[336,512]{1,0:T(8,128)(2,1)S(1)}, bf16[336,512]{1,0:T(8,128)(2,1)S(1)}, u32[]{:S(2)}, u32[]{:S(2)}) collective-permute-start(bf16[336,512]{1,0:T(8,128)(2,1)S(1)} %slice.14), channel_id=1, source_target_pairs={{0,448},{16,464},{32,480},{48,496},{64,0},{80,16},{96,32},{112,48}... | collective-permute-start | bytes 1032200 | tf_op jit(solution)/shard_map/ppermute | solution.py:290
  162.4 3.7 %collective-permute-done.8.refs_7_ = bf16[336,512]{1,0:T(8,128)(2,1)S(1)} collective-permute-done((bf16[336,512]{1,0:T(8,128)(2,1)S(1)}, bf16[336,512]{1,0:T(8,128)(2,1)S(1)}, u32[]{:S(2)}, u32[]{:S(2)}) %collective-permute-start.8) | collective-permute-done | bytes 344096 | tf_op jit(solution)/shard_map/ppermute | solution.py:290
  167.9 5.7 %project.1 = (bf16[128,256]{1,0:T(8,128)(2,1)S(1)}, bf16[8,128,256]{2,1,0:T(8,128)(2,1)}) custom-call(s32[3]{0:T(128)S(1)} %pad_add_fusion.base, bf16[16,8,5760]{2,1,0:T(8,128)(2,1)} %all-to-all-done.2.got, bf16[672,512]{1,0:T(8,128)(2,1)S(1)} %bitcast.11, bf16[672,512]{1,0:T(8,128)(2,1)S(1)} %collective-permute-done.2.refs_1_, ...), custom_call_target="tpu_custom_call" | custom-call | tf_op jit(solution)/shard_map/project/pallas_call | solution.py:392
  173.5 8.4 %all-to-all-start.4 = ((bf16[8,128,256]{2,1,0:T(8,128)(2,1)}), bf16[8,128,256]{2,1,0:T(8,128)(2,1)S(1)}, u32[]{:S(2)}, u32[]{:S(2)}) async-start(bf16[8,128,256]{2,1,0:T(8,128)(2,1)} %get-tuple-element.9), calls=%async_computation.4 | async-start | bytes 1048576 | tf_op jit(solution)/shard_map/all_to_all | solution.py:410
  182.7 14.5 %all_gather.3.queries = bf16[512,256]{1,0:T(8,128)(2,1)S(1)} all-gather(bf16[128,256]{1,0:T(8,128)(2,1)S(1)} %get-tuple-element.8), channel_id=1, replica_groups={{0,16,32,48},{64,80,96,112},{128,144,160,176},{192,208,224,240},{256,27..., dimensions={0}, use_global_device_ids=true | all-gather | bytes 327680 | tf_op jit(solution)/shard_map/all_gather | solution.py:412
  197.3 3.8 %second_layer.1 = bf16[8,64,384]{2,1,0:T(8,128)(2,1)} custom-call(s32[3]{0:T(128)S(1)} %pad_add_fusion.base, bf16[512,256]{1,0:T(8,128)(2,1)S(1)} %all_gather.3.queries, bf16[1024,256]{1,0:T(8,128)(2,1)S(1)} %bitcast.12, s32[512,128]{1,0:T(8,128)S(1)} %broadcast_in_dim.55.low), custom_call_target="tpu_custom_call" | custom-call | tf_op jit(solution)/shard_map/second_layer/pallas_call | solution.py:421
  201.1 6.9 %all-to-all-start.5 = ((bf16[8,64,384]{2,1,0:T(8,128)(2,1)}), bf16[8,64,384]{2,1,0:T(8,128)(2,1)S(1)}, u32[]{:S(2)}, u32[]{:S(2)}) async-start(bf16[8,64,384]{2,1,0:T(8,128)(2,1)} %second_layer.1), calls=%async_computation.5 | async-start | bytes 786432 | tf_op jit(solution)/shard_map/all_to_all | solution.py:430
  209.7 12.3 %all-to-all-done.5.got = bf16[8,64,384]{2,1,0:T(8,128)(2,1)S(1)} async-done(((bf16[8,64,384]{2,1,0:T(8,128)(2,1)}), bf16[8,64,384]{2,1,0:T(8,128)(2,1)S(1)}, u32[]{:S(2)}, u32[]{:S(2)}) %all-to-all-start.5) | async-done | bytes 393248 | tf_op jit(solution)/shard_map/all_to_all | solution.py:430
  (52 shorter events, 23.3 us)
Async XLA Ops:
  0.6 27.3 %copy-start.8 = (s32[2]{0:T(128)S(1)}, s32[2]{0:T(128)}, u32[]{:S(2)}) copy-start(s32[2]{0:T(128)} %param.22) | copy-start | bytes 28
  0.6 40.7 %copy-start.1 = (bf16[128,256]{1,0:T(8,128)(2,1)S(1)}, bf16[128,256]{1,0:T(8,128)(2,1)}, u32[]{:S(2)}) copy-start(bf16[128,256]{1,0:T(8,128)(2,1)} %query.1) | copy-start | bytes 196612
  0.7 40.7 %copy-start = (bf16[256,5376]{1,0:T(8,128)(2,1)S(1)}, bf16[256,5376]{1,0:T(8,128)(2,1)}, u32[]{:S(2)}) copy-start(bf16[256,5376]{1,0:T(8,128)(2,1)} %out_one.1) | copy-start | bytes 8257540
  3.3 13.9 %collective-permute-start.1 = (bf16[128,256]{1,0:T(8,128)(2,1)}, bf16[128,256]{1,0:T(8,128)(2,1)S(1)}, u32[]{:S(2)}, u32[]{:S(2)}) collective-permute-start(bf16[128,256]{1,0:T(8,128)(2,1)} %get-tuple-element.6), channel_id=1, source_target_pairs={{0,128},{16,144},{32,160},{48,176},{64,192},{80,208},{96,224},{112... | collective-permute-start | bytes 196616 | tf_op jit(solution)/shard_map/ppermute | solution.py:290
  9.4 7.8 %collective-permute-start = (bf16[128,256]{1,0:T(8,128)(2,1)}, bf16[128,256]{1,0:T(8,128)(2,1)S(1)}, u32[]{:S(2)}, u32[]{:S(2)}) collective-permute-start(bf16[128,256]{1,0:T(8,128)(2,1)} %get-tuple-element.6), channel_id=1, source_target_pairs={{0,64},{16,80},{32,96},{48,112},{64,128},{80,144},{96,160},{112,17... | collective-permute-start | bytes 196616 | tf_op jit(solution)/shard_map/ppermute | solution.py:290
  19.0 22.3 %all-to-all-start = ((bf16[4,256,256]{2,1,0:T(8,128)(2,1)}), bf16[4,256,256]{2,1,0:T(8,128)(2,1)S(1)}, u32[]{:S(2)}, u32[]{:S(2)}) async-start(bf16[4,256,256]{2,1,0:T(8,128)(2,1)} %broadcast_select_fusion), calls=%async_computation | async-start | bytes 1048576 | tf_op jit(solution)/shard_map/all_to_all | solution.py:286
  43.3 29.4 %copy-start.6 = (f32[5376]{0:T(1024)S(1)}, f32[5376]{0:T(1024)}, u32[]{:S(2)}) copy-start(f32[5376]{0:T(1024)} %param.17) | copy-start | bytes 64516
  43.4 29.4 %copy-start.7 = (f32[5376]{0:T(1024)S(1)}, f32[5376]{0:T(1024)}, u32[]{:S(2)}) copy-start(f32[5376]{0:T(1024)} %param.18) | copy-start | bytes 64516
  68.7 20.0 %all-to-all-start.3 = ((bf16[4,168,512]{2,1,0:T(8,128)(2,1)}), bf16[4,168,512]{2,1,0:T(8,128)(2,1)S(1)}, u32[]{:S(2)}, u32[]{:S(2)}) async-start(bf16[4,168,512]{2,1,0:T(8,128)(2,1)} %get-tuple-element.7), calls=%async_computation.3 | async-start | bytes 1376256 | tf_op jit(solution)/shard_map/all_to_all | solution.py:286
  88.8 79.1 %all-to-all-start.2 = ((bf16[16,8,5760]{2,1,0:T(8,128)(2,1)}), bf16[16,8,5760]{2,1,0:T(8,128)(2,1)}, u32[]{:S(2)}, u32[]{:S(2)}) async-start(bf16[16,8,5760]{2,1,0:T(8,128)(2,1)} %norms.1), calls=%async_computation.2 | async-start | bytes 2949120 | tf_op jit(solution)/shard_map/all_to_all | solution.py:282
  96.1 19.8 %collective-permute-start.2 = (bf16[672,512]{1,0:T(8,128)(2,1)S(1)}, bf16[672,512]{1,0:T(8,128)(2,1)S(1)}, u32[]{:S(2)}, u32[]{:S(2)}) collective-permute-start(bf16[672,512]{1,0:T(8,128)(2,1)S(1)} %bitcast.9), channel_id=1, source_target_pairs={{0,64},{16,80},{32,96},{48,112},{64,128},{80,144},{96,160},{112,17... | collective-permute-start | bytes 2064392 | tf_op jit(solution)/shard_map/ppermute | solution.py:290
  98.8 19.6 %collective-permute-start.3 = (bf16[672,512]{1,0:T(8,128)(2,1)S(1)}, bf16[672,512]{1,0:T(8,128)(2,1)S(1)}, u32[]{:S(2)}, u32[]{:S(2)}) collective-permute-start(bf16[672,512]{1,0:T(8,128)(2,1)S(1)} %bitcast.10), channel_id=1, source_target_pairs={{0,448},{16,464},{32,480},{48,496},{64,0},{80,16},{96,32},{112,48}... | collective-permute-start | bytes 2064392 | tf_op jit(solution)/shard_map/ppermute | solution.py:290
  115.9 20.0 %collective-permute-start.4 = (bf16[672,512]{1,0:T(8,128)(2,1)S(1)}, bf16[672,512]{1,0:T(8,128)(2,1)S(1)}, u32[]{:S(2)}, u32[]{:S(2)}) collective-permute-start(bf16[672,512]{1,0:T(8,128)(2,1)S(1)} %collective-permute-done.2.refs_1_), channel_id=1, source_target_pairs={{0,64},{16,80},{32,96},{48,112},{64,128},{80,144},{96,160},{112,17... | collective-permute-start | bytes 2064392 | tf_op jit(solution)/shard_map/ppermute | solution.py:290
  118.4 19.4 %collective-permute-start.5 = (bf16[672,512]{1,0:T(8,128)(2,1)S(1)}, bf16[672,512]{1,0:T(8,128)(2,1)S(1)}, u32[]{:S(2)}, u32[]{:S(2)}) collective-permute-start(bf16[672,512]{1,0:T(8,128)(2,1)S(1)} %collective-permute-done.3.refs_2_), channel_id=1, source_target_pairs={{0,448},{16,464},{32,480},{48,496},{64,0},{80,16},{96,32},{112,48}... | collective-permute-start | bytes 2064392 | tf_op jit(solution)/shard_map/ppermute | solution.py:290
  135.9 7.6 %copy-start.4 = (bf16[672,512]{1,0:T(8,128)(2,1)}, bf16[672,512]{1,0:T(8,128)(2,1)S(1)}, u32[]{:S(2)}) copy-start(bf16[672,512]{1,0:T(8,128)(2,1)S(1)} %collective-permute-done.4.refs_3_) | copy-start | bytes 2064388
  135.9 19.2 %collective-permute-start.6 = (bf16[672,512]{1,0:T(8,128)(2,1)S(1)}, bf16[672,512]{1,0:T(8,128)(2,1)S(1)}, u32[]{:S(2)}, u32[]{:S(2)}) collective-permute-start(bf16[672,512]{1,0:T(8,128)(2,1)S(1)} %collective-permute-done.4.refs_3_), channel_id=1, source_target_pairs={{0,64},{16,80},{32,96},{48,112},{64,128},{80,144},{96,160},{112,17... | collective-permute-start | bytes 2064392 | tf_op jit(solution)/shard_map/ppermute | solution.py:290
  137.9 28.2 %copy-start.5 = (bf16[672,512]{1,0:T(8,128)(2,1)}, bf16[672,512]{1,0:T(8,128)(2,1)S(1)}, u32[]{:S(2)}) copy-start(bf16[672,512]{1,0:T(8,128)(2,1)S(1)} %collective-permute-done.5.refs_4_) | copy-start | bytes 2064388
  137.9 19.2 %collective-permute-start.7 = (bf16[672,512]{1,0:T(8,128)(2,1)S(1)}, bf16[672,512]{1,0:T(8,128)(2,1)S(1)}, u32[]{:S(2)}, u32[]{:S(2)}) collective-permute-start(bf16[672,512]{1,0:T(8,128)(2,1)S(1)} %collective-permute-done.5.refs_4_), channel_id=1, source_target_pairs={{0,448},{16,464},{32,480},{48,496},{64,0},{80,16},{96,32},{112,48}... | collective-permute-start | bytes 2064392 | tf_op jit(solution)/shard_map/ppermute | solution.py:290
  155.1 11.0 %copy-start.2 = (bf16[672,512]{1,0:T(8,128)(2,1)}, bf16[672,512]{1,0:T(8,128)(2,1)S(1)}, u32[]{:S(2)}) copy-start(bf16[672,512]{1,0:T(8,128)(2,1)S(1)} %collective-permute-done.6.refs_5_) | copy-start | bytes 2064388
  155.1 11.0 %collective-permute-start.8 = (bf16[336,512]{1,0:T(8,128)(2,1)S(1)}, bf16[336,512]{1,0:T(8,128)(2,1)S(1)}, u32[]{:S(2)}, u32[]{:S(2)}) collective-permute-start(bf16[336,512]{1,0:T(8,128)(2,1)S(1)} %slice.13), channel_id=1, source_target_pairs={{0,64},{16,80},{32,96},{48,112},{64,128},{80,144},{96,160},{112,17... | collective-permute-start | bytes 1032200 | tf_op jit(solution)/shard_map/ppermute | solution.py:290
  157.1 9.0 %copy-start.3 = (bf16[672,512]{1,0:T(8,128)(2,1)}, bf16[672,512]{1,0:T(8,128)(2,1)S(1)}, u32[]{:S(2)}) copy-start(bf16[672,512]{1,0:T(8,128)(2,1)S(1)} %collective-permute-done.7.refs_6_) | copy-start | bytes 2064388
  157.1 10.7 %collective-permute-start.9 = (bf16[336,512]{1,0:T(8,128)(2,1)S(1)}, bf16[336,512]{1,0:T(8,128)(2,1)S(1)}, u32[]{:S(2)}, u32[]{:S(2)}) collective-permute-start(bf16[336,512]{1,0:T(8,128)(2,1)S(1)} %slice.14), channel_id=1, source_target_pairs={{0,448},{16,464},{32,480},{48,496},{64,0},{80,16},{96,32},{112,48}... | collective-permute-start | bytes 1032200 | tf_op jit(solution)/shard_map/ppermute | solution.py:290
  173.5 23.6 %all-to-all-start.4 = ((bf16[8,128,256]{2,1,0:T(8,128)(2,1)}), bf16[8,128,256]{2,1,0:T(8,128)(2,1)S(1)}, u32[]{:S(2)}, u32[]{:S(2)}) async-start(bf16[8,128,256]{2,1,0:T(8,128)(2,1)} %get-tuple-element.9), calls=%async_computation.4 | async-start | bytes 1048576 | tf_op jit(solution)/shard_map/all_to_all | solution.py:410
  201.1 20.9 %all-to-all-start.5 = ((bf16[8,64,384]{2,1,0:T(8,128)(2,1)}), bf16[8,64,384]{2,1,0:T(8,128)(2,1)S(1)}, u32[]{:S(2)}, u32[]{:S(2)}) async-start(bf16[8,64,384]{2,1,0:T(8,128)(2,1)} %second_layer.1), calls=%async_computation.5 | async-start | bytes 786432 | tf_op jit(solution)/shard_map/all_to_all | solution.py:430

commit v7 on v6

--- a/solution.py
+++ b/solution.py
@@ -31,6 +31,9 @@
 ]
 Z_GROUPS = [[z * Y_HI + y for z in range(Z)] for y in range(Y_HI)]
 VMEM_LIMIT = 24 * 1024 * 1024
+FIRST_LIMIT = 24 * 1024 * 1024
+NORM_LIMIT = 24 * 1024 * 1024
+PROJECT_LIMIT = 56 * 1024 * 1024
 
 
 def whole(memory_space=pltpu.VMEM):
@@ -175,14 +178,13 @@
 
 
 def project_kernel(base, got, *refs):
-    pieces, refs = refs[: Z + 1], refs[Z + 1 :]
+    pieces, refs = refs[:Z], refs[Z:]
     turn_cos, turn_sin, query, pair, held, block, in_sem, out_sem = refs
     level_rows = WIDTH // Z
-    offsets = [0, -1, 1, -2, 2, -3, 3, 4, 4]
-    for index, (piece, offset) in enumerate(zip(pieces, offsets)):
+    offsets = [0, -1, -2, -3, -4, 1, 2, 3]
+    for piece, offset in zip(pieces, offsets):
         level = lax.rem(base[0] + (offset + Z), Z)
-        at = level * level_rows + (level_rows // 2 if index == Z else 0)
-        target = held.at[pl.ds(pl.multiple_of(at, 16), piece.shape[0])]
+        target = held.at[pl.ds(pl.multiple_of(level * level_rows, 16), level_rows)]
         pltpu.make_async_copy(piece, target, in_sem.at[level]).start()
     depth = WIDTH // PARTS
     total = jnp.zeros((TOK, 4 * HEAD_SIZE), jnp.float32)
@@ -308,6 +310,9 @@
     place_z, place_y = ctx_place // Y_HI, ctx_place % Y_HI
     bf16, f32 = jnp.bfloat16, jnp.float32
     params = partial(pltpu.CompilerParams, vmem_limit_bytes=VMEM_LIMIT)
+    first_params = pltpu.CompilerParams(vmem_limit_bytes=FIRST_LIMIT)
+    norm_params = pltpu.CompilerParams(vmem_limit_bytes=NORM_LIMIT)
+    project_params = pltpu.CompilerParams(vmem_limit_bytes=PROJECT_LIMIT)
 
     own, spread = pl.pallas_call(
         prepare_kernel,
@@ -329,16 +334,11 @@
     weights = exchange_y(spread).reshape(-1, 4 * HEAD_SIZE)
     bases = jnp.stack([place_z, place_y, place_z // (Z // 2)])
     pieces = [weights]
-    upward, downward = weights, weights
-    for _ in range(1, Z // 2):
-        upward = ctx_shift(upward, Y_HI)
-        downward = ctx_shift(downward, -Y_HI)
-        pieces += [upward, downward]
-    half_rows = weights.shape[0] // 2
-    upward, downward = upward[:half_rows], downward[half_rows:]
-    upward = ctx_shift(upward, Y_HI)
-    downward = ctx_shift(downward, -Y_HI)
-    pieces += [upward, downward]
+    for count, sign in ((Z // 2, 1), (Z // 2 - 1, -1)):
+        piece = weights
+        for _ in range(1, count + 1):
+            piece = ctx_shift(piece, sign * Y_HI)
+            pieces.append(piece)
 
     later = jnp.concatenate([own, back_one], axis=0)
     earlier = jnp.concatenate([back_one, back_two], axis=0)
@@ -357,7 +357,7 @@
         in_specs=[whole(pltpu.SMEM)] + [whole()] * 6,
         out_specs=whole(),
         scratch_shapes=[pltpu.VMEM((2 * TOK, 9 * TOK), f32)],
-        compiler_params=params(),
+        compiler_params=first_params,
         cost_estimate=pl.CostEstimate(
             flops=600_000_000, bytes_accessed=6_000_000, transcendentals=300_000
         ),
@@ -378,7 +378,7 @@
         in_specs=[whole()] * 3,
         out_specs=whole(),
         scratch_shapes=[pltpu.VMEM((ROWS, WIDTH), f32)] * 2,
-        compiler_params=params(),
+        compiler_params=norm_params,
         name="norms",
     )(got, post_gain[None, :], pre_gain[None, :])
     got = exchange_heads(sent)
@@ -395,7 +395,7 @@
             jax.ShapeDtypeStruct((TOK, 2 * HEAD_SIZE), bf16),
             jax.ShapeDtypeStruct((Z, TOK, 2 * HEAD_SIZE), bf16),
         ),
-        in_specs=[whole(pltpu.SMEM), whole()] + [whole(pltpu.HBM)] * (Z + 1) + [whole(), whole()],
+        in_specs=[whole(pltpu.SMEM), whole()] + [whole(pltpu.HBM)] * Z + [whole(), whole()],
         out_specs=(whole(), whole(pltpu.HBM)),
         scratch_shapes=[
             pltpu.VMEM((WIDTH, 4 * HEAD_SIZE), bf16),
@@ -403,7 +403,7 @@
             pltpu.SemaphoreType.DMA((Z,)),
             pltpu.SemaphoreType.DMA((Z,)),
         ],
-        compiler_params=pltpu.CompilerParams(vmem_limit_bytes=50 * 1024 * 1024),
+        compiler_params=project_params,
         name="project",
     )(bases, got, *pieces, turn_cos, turn_sin)
 

time: 225 us -> 231 us (1.027)
  the two profiles are of different devices: /device:TPU:64 before, /device:TPU:74 now
where the time goes in v7:
time: 231 us; the launch traced here: 230 us
  waiting for transfers between devices  99.6 us (43%)
  starting transfers between devices  62.8 us (27%)
  blocking collectives  38.5 us (17%)
  Pallas kernels  18.1 us (8%)
  other arithmetic  5.28 us (2%)
  local copies, waits for them, and re-layouts  4.93 us (2%)
    ppermute x9, waiting for transfers between devices, ctx_shift(): lax.ppermute(value, 'ctx', [(i, (i + steps) % N_CTX) for i in range(N_CTX)])  54.3 us
    ppermute x9, starting transfers between devices, ctx_shift(): lax.ppermute(value, 'ctx', [(i, (i + steps) % N_CTX) for i in range(N_CTX)])  32.8 us
    all_to_all x2, waiting for transfers between devices, exchange_y(): lax.all_to_all(value, 'ctx', 0, 0, tiled=True, axis_index_groups=Y_GROUPS)  32.1 us
    all_to_all x1, blocking collectives, exchange_heads(): return lax.all_to_all(value, 'heads', 0, 0, tiled=True)  23.9 us
    all_gather x1, blocking collectives, shards(): lax.all_gather(query, 'ctx', axis=0, tiled=True, axis_index_groups=Y_GROUPS)  14.6 us
    all_to_all x1, waiting for transfers between devices, shards(): lax.all_to_all(sent, 'ctx', 0, 0, tiled=True, axis_index_groups=LEVEL_PAIRS)  13.1 us
    all_to_all x2, starting transfers between devices, exchange_y(): lax.all_to_all(value, 'ctx', 0, 0, tiled=True, axis_index_groups=Y_GROUPS)  10.2 us
    all_to_all x1, starting transfers between devices, shards(): lax.all_to_all(pair, 'ctx', 0, 0, tiled=True, axis_index_groups=Z_GROUPS)  7.45 us
  transfers between devices with their start and end apart: 14, of which 8 were waited for; matrix products, arithmetic and copies ran while one was open for 3% of the time, Pallas kernels for 1%

profile of v7, /device:TPU:74, one launch (start us, length us, event | category | flops | bytes accessed | tf_op | source)
XLA Modules:
  0.0 230.2 jit_solution(12657085540766158726)
XLA Ops:
  0.7 2.6 %prepare.1 = (bf16[128,256]{1,0:T(8,128)(2,1)}, bf16[4,168,512]{2,1,0:T(8,128)(2,1)}) custom-call(bf16[128,128]{1,0:T(8,128)(2,1)} %keys.1, bf16[128,128]{1,0:T(8,128)(2,1)} %values.1, bf16[168,256]{1,0:T(8,128)(2,1)} %proj_query.1, bf16[168,128]{1,0:T(8,128)(2,1)} %key_projection.1, bf16[168,128]{1,0:T(8,128)(2,1)} %value_projection.1), custom_call_target="tpu_custom_call" | custom-call | tf_op jit(solution)/shard_map/prepare/pallas_call | solution.py:317
  3.3 6.1 %collective-permute-start.1 = (bf16[128,256]{1,0:T(8,128)(2,1)}, bf16[128,256]{1,0:T(8,128)(2,1)S(1)}, u32[]{:S(2)}, u32[]{:S(2)}) collective-permute-start(bf16[128,256]{1,0:T(8,128)(2,1)} %get-tuple-element.6), channel_id=1, source_target_pairs={{0,128},{16,144},{32,160},{48,176},{64,192},{80,208},{96,224},{112... | collective-permute-start | bytes 196616 | tf_op jit(solution)/shard_map/ppermute | solution.py:292
  9.4 5.5 %collective-permute-start = (bf16[128,256]{1,0:T(8,128)(2,1)}, bf16[128,256]{1,0:T(8,128)(2,1)S(1)}, u32[]{:S(2)}, u32[]{:S(2)}) collective-permute-start(bf16[128,256]{1,0:T(8,128)(2,1)} %get-tuple-element.6), channel_id=1, source_target_pairs={{0,64},{16,80},{32,96},{48,112},{64,128},{80,144},{96,160},{112,17... | collective-permute-start | bytes 196616 | tf_op jit(solution)/shard_map/ppermute | solution.py:292
  18.9 6.2 %all-to-all-start = ((bf16[4,256,256]{2,1,0:T(8,128)(2,1)}), bf16[4,256,256]{2,1,0:T(8,128)(2,1)S(1)}, u32[]{:S(2)}, u32[]{:S(2)}) async-start(bf16[4,256,256]{2,1,0:T(8,128)(2,1)} %broadcast_select_fusion), calls=%async_computation | async-start | bytes 1048576 | tf_op jit(solution)/shard_map/all_to_all | solution.py:288
  27.0 13.4 %all-to-all-done.blocks = bf16[4,256,256]{2,1,0:T(8,128)(2,1)S(1)} async-done(((bf16[4,256,256]{2,1,0:T(8,128)(2,1)}), bf16[4,256,256]{2,1,0:T(8,128)(2,1)S(1)}, u32[]{:S(2)}, u32[]{:S(2)}) %all-to-all-start) | async-done | bytes 524320 | tf_op jit(solution)/shard_map/all_to_all | solution.py:288
  42.5 23.9 %all_to_all.30.got = bf16[16,8,5760]{2,1,0:T(8,128)(2,1)S(1)} all-to-all(bf16[16,8,5760]{2,1,0:T(8,128)(2,1)S(1)} %first_layer.1), channel_id=1, replica_groups=mesh['ctx'=32,'heads'=16] {'heads'}, dimensions={0} | all-to-all | bytes 2949120 | tf_op jit(solution)/shard_map/all_to_all | solution.py:284
  66.4 4.0 %all-to-all-start.3 = ((bf16[4,168,512]{2,1,0:T(8,128)(2,1)}), bf16[4,168,512]{2,1,0:T(8,128)(2,1)S(1)}, u32[]{:S(2)}, u32[]{:S(2)}) async-start(bf16[4,168,512]{2,1,0:T(8,128)(2,1)} %get-tuple-element.7), calls=%async_computation.3 | async-start | bytes 1376256 | tf_op jit(solution)/shard_map/all_to_all | solution.py:288
  72.2 18.8 %all-to-all-done.3 = bf16[4,168,512]{2,1,0:T(8,128)(2,1)S(1)} async-done(((bf16[4,168,512]{2,1,0:T(8,128)(2,1)}), bf16[4,168,512]{2,1,0:T(8,128)(2,1)S(1)}, u32[]{:S(2)}, u32[]{:S(2)}) %all-to-all-start.3) | async-done | bytes 688160 | tf_op jit(solution)/shard_map/all_to_all | solution.py:288
  90.9 5.4 %all-to-all-start.2 = ((bf16[16,8,5760]{2,1,0:T(8,128)(2,1)}), bf16[16,8,5760]{2,1,0:T(8,128)(2,1)S(1)}, u32[]{:S(2)}, u32[]{:S(2)}) async-start(bf16[16,8,5760]{2,1,0:T(8,128)(2,1)} %norms.1), calls=%async_computation.2 | async-start | bytes 2949120 | tf_op jit(solution)/shard_map/all_to_all | solution.py:284
  96.3 2.7 %collective-permute-start.2 = (bf16[672,512]{1,0:T(8,128)(2,1)S(1)}, bf16[672,512]{1,0:T(8,128)(2,1)S(1)}, u32[]{:S(2)}, u32[]{:S(2)}) collective-permute-start(bf16[672,512]{1,0:T(8,128)(2,1)S(1)} %bitcast.10), channel_id=1, source_target_pairs={{0,64},{16,80},{32,96},{48,112},{64,128},{80,144},{96,160},{112,17... | collective-permute-start | bytes 2064392 | tf_op jit(solution)/shard_map/ppermute | solution.py:292
  99.1 3.1 %collective-permute-start.6 = (bf16[672,512]{1,0:T(8,128)(2,1)S(1)}, bf16[672,512]{1,0:T(8,128)(2,1)S(1)}, u32[]{:S(2)}, u32[]{:S(2)}) collective-permute-start(bf16[672,512]{1,0:T(8,128)(2,1)S(1)} %bitcast.11), channel_id=1, source_target_pairs={{0,448},{16,464},{32,480},{48,496},{64,0},{80,16},{96,32},{112,48}... | collective-permute-start | bytes 2064392 | tf_op jit(solution)/shard_map/ppermute | solution.py:292
  102.2 13.7 %collective-permute-done.2.refs_1_ = bf16[672,512]{1,0:T(8,128)(2,1)S(1)} collective-permute-done((bf16[672,512]{1,0:T(8,128)(2,1)S(1)}, bf16[672,512]{1,0:T(8,128)(2,1)S(1)}, u32[]{:S(2)}, u32[]{:S(2)}) %collective-permute-start.2) | collective-permute-done | bytes 688160 | tf_op jit(solution)/shard_map/ppermute | solution.py:292
  115.9 2.5 %collective-permute-start.3 = (bf16[672,512]{1,0:T(8,128)(2,1)S(1)}, bf16[672,512]{1,0:T(8,128)(2,1)S(1)}, u32[]{:S(2)}, u32[]{:S(2)}) collective-permute-start(bf16[672,512]{1,0:T(8,128)(2,1)S(1)} %collective-permute-done.2.refs_1_), channel_id=1, source_target_pairs={{0,64},{16,80},{32,96},{48,112},{64,128},{80,144},{96,160},{112,17... | collective-permute-start | bytes 2064392 | tf_op jit(solution)/shard_map/ppermute | solution.py:292
  118.4 4.3 %collective-permute-start.7 = (bf16[672,512]{1,0:T(8,128)(2,1)S(1)}, bf16[672,512]{1,0:T(8,128)(2,1)S(1)}, u32[]{:S(2)}, u32[]{:S(2)}) collective-permute-start(bf16[672,512]{1,0:T(8,128)(2,1)S(1)} %collective-permute-done.6.refs_5_), channel_id=1, source_target_pairs={{0,448},{16,464},{32,480},{48,496},{64,0},{80,16},{96,32},{112,48}... | collective-permute-start | bytes 2064392 | tf_op jit(solution)/shard_map/ppermute | solution.py:292
  122.7 12.9 %collective-permute-done.3.refs_2_ = bf16[672,512]{1,0:T(8,128)(2,1)S(1)} collective-permute-done((bf16[672,512]{1,0:T(8,128)(2,1)S(1)}, bf16[672,512]{1,0:T(8,128)(2,1)S(1)}, u32[]{:S(2)}, u32[]{:S(2)}) %collective-permute-start.3) | collective-permute-done | bytes 688160 | tf_op jit(solution)/shard_map/ppermute | solution.py:292
  137.5 4.9 %collective-permute-start.8 = (bf16[672,512]{1,0:T(8,128)(2,1)S(1)}, bf16[672,512]{1,0:T(8,128)(2,1)S(1)}, u32[]{:S(2)}, u32[]{:S(2)}) collective-permute-start(bf16[672,512]{1,0:T(8,128)(2,1)S(1)} %collective-permute-done.7.refs_6_), channel_id=1, source_target_pairs={{0,448},{16,464},{32,480},{48,496},{64,0},{80,16},{96,32},{112,48}... | collective-permute-start | bytes 2064392 | tf_op jit(solution)/shard_map/ppermute | solution.py:292
  142.4 12.0 %collective-permute-done.4.refs_3_ = bf16[672,512]{1,0:T(8,128)(2,1)S(1)} collective-permute-done((bf16[672,512]{1,0:T(8,128)(2,1)S(1)}, bf16[672,512]{1,0:T(8,128)(2,1)S(1)}, u32[]{:S(2)}, u32[]{:S(2)}) %collective-permute-start.4) | collective-permute-done | bytes 688160 | tf_op jit(solution)/shard_map/ppermute | solution.py:292
  159.1 13.5 %collective-permute-done.5.refs_4_ = bf16[672,512]{1,0:T(8,128)(2,1)} collective-permute-done((bf16[672,512]{1,0:T(8,128)(2,1)S(1)}, bf16[672,512]{1,0:T(8,128)(2,1)}, u32[]{:S(2)}, u32[]{:S(2)}) %collective-permute-start.5) | collective-permute-done | bytes 688160 | tf_op jit(solution)/shard_map/ppermute | solution.py:292
  173.7 6.4 %project.1 = (bf16[128,256]{1,0:T(8,128)(2,1)}, bf16[8,128,256]{2,1,0:T(8,128)(2,1)}) custom-call(s32[3]{0:T(128)} %copy-done.2, bf16[16,8,5760]{2,1,0:T(8,128)(2,1)} %copy-done.4, bf16[672,512]{1,0:T(8,128)(2,1)} %bitcast.12, bf16[672,512]{1,0:T(8,128)(2,1)} %copy-done.6, bf16[672,512]{1,0:T(8,128)(2,1)} %copy-done.8, bf16[672,512]{1,0:T(8,128)(2,1)} %copy-done.10, ...), custom_call_target="tpu_custom_call" | custom-call | tf_op jit(solution)/shard_map/project/pallas_call | solution.py:392
  180.1 7.5 %all-to-all-start.4 = ((bf16[8,128,256]{2,1,0:T(8,128)(2,1)}), bf16[8,128,256]{2,1,0:T(8,128)(2,1)S(1)}, u32[]{:S(2)}, u32[]{:S(2)}) async-start(bf16[8,128,256]{2,1,0:T(8,128)(2,1)} %get-tuple-element.9), calls=%async_computation.4 | async-start | bytes 1048576 | tf_op jit(solution)/shard_map/all_to_all | solution.py:410
  188.3 14.6 %all_gather.3.queries = bf16[512,256]{1,0:T(8,128)(2,1)S(1)} all-gather(bf16[128,256]{1,0:T(8,128)(2,1)} %get-tuple-element.8), channel_id=1, replica_groups={{0,16,32,48},{64,80,96,112},{128,144,160,176},{192,208,224,240},{256,27..., dimensions={0}, use_global_device_ids=true | all-gather | bytes 327680 | tf_op jit(solution)/shard_map/all_gather | solution.py:412
  203.1 3.8 %second_layer.1 = bf16[8,64,384]{2,1,0:T(8,128)(2,1)} custom-call(s32[3]{0:T(128)S(1)} %copy-done.3, bf16[512,256]{1,0:T(8,128)(2,1)S(1)} %all_gather.3.queries, bf16[1024,256]{1,0:T(8,128)(2,1)S(1)} %bitcast.9, s32[512,128]{1,0:T(8,128)S(1)} %broadcast_in_dim.55.low), custom_call_target="tpu_custom_call" | custom-call | tf_op jit(solution)/shard_map/second_layer/pallas_call | solution.py:421
  206.9 6.9 %all-to-all-start.5 = ((bf16[8,64,384]{2,1,0:T(8,128)(2,1)}), bf16[8,64,384]{2,1,0:T(8,128)(2,1)S(1)}, u32[]{:S(2)}, u32[]{:S(2)}) async-start(bf16[8,64,384]{2,1,0:T(8,128)(2,1)} %second_layer.1), calls=%async_computation.5 | async-start | bytes 786432 | tf_op jit(solution)/shard_map/all_to_all | solution.py:430
  215.5 13.1 %all-to-all-done.5.got = bf16[8,64,384]{2,1,0:T(8,128)(2,1)S(1)} async-done(((bf16[8,64,384]{2,1,0:T(8,128)(2,1)}), bf16[8,64,384]{2,1,0:T(8,128)(2,1)S(1)}, u32[]{:S(2)}, u32[]{:S(2)}) %all-to-all-start.5) | async-done | bytes 393248 | tf_op jit(solution)/shard_map/all_to_all | solution.py:430
  (60 shorter events, 21.6 us)
Async XLA Ops:
  0.6 26.3 %copy-start.14 = (s32[2]{0:T(128)S(1)}, s32[2]{0:T(128)}, u32[]{:S(2)}) copy-start(s32[2]{0:T(128)} %param.22) | copy-start | bytes 28
  0.6 39.9 %copy-start.1 = (bf16[128,256]{1,0:T(8,128)(2,1)S(1)}, bf16[128,256]{1,0:T(8,128)(2,1)}, u32[]{:S(2)}) copy-start(bf16[128,256]{1,0:T(8,128)(2,1)} %query.1) | copy-start | bytes 196612
  0.7 39.9 %copy-start = (bf16[256,5376]{1,0:T(8,128)(2,1)S(1)}, bf16[256,5376]{1,0:T(8,128)(2,1)}, u32[]{:S(2)}) copy-start(bf16[256,5376]{1,0:T(8,128)(2,1)} %out_one.1) | copy-start | bytes 8257540
  3.3 13.9 %collective-permute-start.1 = (bf16[128,256]{1,0:T(8,128)(2,1)}, bf16[128,256]{1,0:T(8,128)(2,1)S(1)}, u32[]{:S(2)}, u32[]{:S(2)}) collective-permute-start(bf16[128,256]{1,0:T(8,128)(2,1)} %get-tuple-element.6), channel_id=1, source_target_pairs={{0,128},{16,144},{32,160},{48,176},{64,192},{80,208},{96,224},{112... | collective-permute-start | bytes 196616 | tf_op jit(solution)/shard_map/ppermute | solution.py:292
  9.4 7.8 %collective-permute-start = (bf16[128,256]{1,0:T(8,128)(2,1)}, bf16[128,256]{1,0:T(8,128)(2,1)S(1)}, u32[]{:S(2)}, u32[]{:S(2)}) collective-permute-start(bf16[128,256]{1,0:T(8,128)(2,1)} %get-tuple-element.6), channel_id=1, source_target_pairs={{0,64},{16,80},{32,96},{48,112},{64,128},{80,144},{96,160},{112,17... | collective-permute-start | bytes 196616 | tf_op jit(solution)/shard_map/ppermute | solution.py:292
  18.9 21.5 %all-to-all-start = ((bf16[4,256,256]{2,1,0:T(8,128)(2,1)}), bf16[4,256,256]{2,1,0:T(8,128)(2,1)S(1)}, u32[]{:S(2)}, u32[]{:S(2)}) async-start(bf16[4,256,256]{2,1,0:T(8,128)(2,1)} %broadcast_select_fusion), calls=%async_computation | async-start | bytes 1048576 | tf_op jit(solution)/shard_map/all_to_all | solution.py:288
  26.2 16.2 %copy-start.2 = (s32[3]{0:T(128)}, s32[3]{0:T(128)S(1)}, u32[]{:S(2)}) copy-start(s32[3]{0:T(128)S(1)} %pad_add_fusion.base) | copy-start | bytes 40
  42.4 28.0 %copy-start.12 = (f32[5376]{0:T(1024)S(1)}, f32[5376]{0:T(1024)}, u32[]{:S(2)}) copy-start(f32[5376]{0:T(1024)} %param.17) | copy-start | bytes 64516
  42.5 28.0 %copy-start.13 = (f32[5376]{0:T(1024)S(1)}, f32[5376]{0:T(1024)}, u32[]{:S(2)}) copy-start(f32[5376]{0:T(1024)} %param.18) | copy-start | bytes 64516
  66.4 24.5 %all-to-all-start.3 = ((bf16[4,168,512]{2,1,0:T(8,128)(2,1)}), bf16[4,168,512]{2,1,0:T(8,128)(2,1)S(1)}, u32[]{:S(2)}, u32[]{:S(2)}) async-start(bf16[4,168,512]{2,1,0:T(8,128)(2,1)} %get-tuple-element.7), calls=%async_computation.3 | async-start | bytes 1376256 | tf_op jit(solution)/shard_map/all_to_all | solution.py:288
  90.9 81.6 %all-to-all-start.2 = ((bf16[16,8,5760]{2,1,0:T(8,128)(2,1)}), bf16[16,8,5760]{2,1,0:T(8,128)(2,1)S(1)}, u32[]{:S(2)}, u32[]{:S(2)}) async-start(bf16[16,8,5760]{2,1,0:T(8,128)(2,1)} %norms.1), calls=%async_computation.2 | async-start | bytes 2949120 | tf_op jit(solution)/shard_map/all_to_all | solution.py:284
  96.3 19.6 %collective-permute-start.2 = (bf16[672,512]{1,0:T(8,128)(2,1)S(1)}, bf16[672,512]{1,0:T(8,128)(2,1)S(1)}, u32[]{:S(2)}, u32[]{:S(2)}) collective-permute-start(bf16[672,512]{1,0:T(8,128)(2,1)S(1)} %bitcast.10), channel_id=1, source_target_pairs={{0,64},{16,80},{32,96},{48,112},{64,128},{80,144},{96,160},{112,17... | collective-permute-start | bytes 2064392 | tf_op jit(solution)/shard_map/ppermute | solution.py:292
  99.1 19.3 %collective-permute-start.6 = (bf16[672,512]{1,0:T(8,128)(2,1)S(1)}, bf16[672,512]{1,0:T(8,128)(2,1)S(1)}, u32[]{:S(2)}, u32[]{:S(2)}) collective-permute-start(bf16[672,512]{1,0:T(8,128)(2,1)S(1)} %bitcast.11), channel_id=1, source_target_pairs={{0,448},{16,464},{32,480},{48,496},{64,0},{80,16},{96,32},{112,48}... | collective-permute-start | bytes 2064392 | tf_op jit(solution)/shard_map/ppermute | solution.py:292
  115.9 56.6 %copy-start.6 = (bf16[672,512]{1,0:T(8,128)(2,1)}, bf16[672,512]{1,0:T(8,128)(2,1)S(1)}, u32[]{:S(2)}) copy-start(bf16[672,512]{1,0:T(8,128)(2,1)S(1)} %collective-permute-done.2.refs_1_) | copy-start | bytes 2064388
  115.9 19.7 %collective-permute-start.3 = (bf16[672,512]{1,0:T(8,128)(2,1)S(1)}, bf16[672,512]{1,0:T(8,128)(2,1)S(1)}, u32[]{:S(2)}, u32[]{:S(2)}) collective-permute-start(bf16[672,512]{1,0:T(8,128)(2,1)S(1)} %collective-permute-done.2.refs_1_), channel_id=1, source_target_pairs={{0,64},{16,80},{32,96},{48,112},{64,128},{80,144},{96,160},{112,17... | collective-permute-start | bytes 2064392 | tf_op jit(solution)/shard_map/ppermute | solution.py:292
  118.4 54.1 %copy-start.7 = (bf16[672,512]{1,0:T(8,128)(2,1)}, bf16[672,512]{1,0:T(8,128)(2,1)S(1)}, u32[]{:S(2)}) copy-start(bf16[672,512]{1,0:T(8,128)(2,1)S(1)} %collective-permute-done.6.refs_5_) | copy-start | bytes 2064388
  118.4 19.1 %collective-permute-start.7 = (bf16[672,512]{1,0:T(8,128)(2,1)S(1)}, bf16[672,512]{1,0:T(8,128)(2,1)S(1)}, u32[]{:S(2)}, u32[]{:S(2)}) collective-permute-start(bf16[672,512]{1,0:T(8,128)(2,1)S(1)} %collective-permute-done.6.refs_5_), channel_id=1, source_target_pairs={{0,448},{16,464},{32,480},{48,496},{64,0},{80,16},{96,32},{112,48}... | collective-permute-start | bytes 2064392 | tf_op jit(solution)/shard_map/ppermute | solution.py:292
  135.6 18.8 %collective-permute-start.4 = (bf16[672,512]{1,0:T(8,128)(2,1)S(1)}, bf16[672,512]{1,0:T(8,128)(2,1)S(1)}, u32[]{:S(2)}, u32[]{:S(2)}) collective-permute-start(bf16[672,512]{1,0:T(8,128)(2,1)S(1)} %collective-permute-done.3.refs_2_), channel_id=1, source_target_pairs={{0,64},{16,80},{32,96},{48,112},{64,128},{80,144},{96,160},{112,17... | collective-permute-start | bytes 2064392 | tf_op jit(solution)/shard_map/ppermute | solution.py:292
  137.5 35.0 %copy-start.9 = (bf16[672,512]{1,0:T(8,128)(2,1)}, bf16[672,512]{1,0:T(8,128)(2,1)S(1)}, u32[]{:S(2)}) copy-start(bf16[672,512]{1,0:T(8,128)(2,1)S(1)} %collective-permute-done.7.refs_6_) | copy-start | bytes 2064388
  137.5 20.7 %collective-permute-start.8 = (bf16[672,512]{1,0:T(8,128)(2,1)S(1)}, bf16[672,512]{1,0:T(8,128)(2,1)S(1)}, u32[]{:S(2)}, u32[]{:S(2)}) collective-permute-start(bf16[672,512]{1,0:T(8,128)(2,1)S(1)} %collective-permute-done.7.refs_6_), channel_id=1, source_target_pairs={{0,448},{16,464},{32,480},{48,496},{64,0},{80,16},{96,32},{112,48}... | collective-permute-start | bytes 2064392 | tf_op jit(solution)/shard_map/ppermute | solution.py:292
  154.4 18.1 %collective-permute-start.5 = (bf16[672,512]{1,0:T(8,128)(2,1)S(1)}, bf16[672,512]{1,0:T(8,128)(2,1)}, u32[]{:S(2)}, u32[]{:S(2)}) collective-permute-start(bf16[672,512]{1,0:T(8,128)(2,1)S(1)} %collective-permute-done.4.refs_3_), channel_id=1, source_target_pairs={{0,64},{16,80},{32,96},{48,112},{64,128},{80,144},{96,160},{112,17... | collective-permute-start | bytes 2064392 | tf_op jit(solution)/shard_map/ppermute | solution.py:292
  180.1 23.0 %copy-start.3 = (s32[3]{0:T(128)S(1)}, s32[3]{0:T(128)}, u32[]{:S(2)}) copy-start(s32[3]{0:T(128)} %copy-done.2) | copy-start | bytes 40
  180.1 22.9 %all-to-all-start.4 = ((bf16[8,128,256]{2,1,0:T(8,128)(2,1)}), bf16[8,128,256]{2,1,0:T(8,128)(2,1)S(1)}, u32[]{:S(2)}, u32[]{:S(2)}) async-start(bf16[8,128,256]{2,1,0:T(8,128)(2,1)} %get-tuple-element.9), calls=%async_computation.4 | async-start | bytes 1048576 | tf_op jit(solution)/shard_map/all_to_all | solution.py:410
  206.9 21.7 %all-to-all-start.5 = ((bf16[8,64,384]{2,1,0:T(8,128)(2,1)}), bf16[8,64,384]{2,1,0:T(8,128)(2,1)S(1)}, u32[]{:S(2)}, u32[]{:S(2)}) async-start(bf16[8,64,384]{2,1,0:T(8,128)(2,1)} %second_layer.1), calls=%async_computation.5 | async-start | bytes 786432 | tf_op jit(solution)/shard_map/all_to_all | solution.py:430
  (5 other events, 15.9 us)

commit v8 on v7

--- a/solution.py
+++ b/solution.py
@@ -179,19 +179,31 @@
 
 def project_kernel(base, got, *refs):
     pieces, refs = refs[:Z], refs[Z:]
-    turn_cos, turn_sin, query, pair, held, block, in_sem, out_sem = refs
+    turn_cos, turn_sin, query, pair, held, normed, block, in_sem, row_sem, out_sem = refs
     level_rows = WIDTH // Z
+    depth = WIDTH // PARTS
     offsets = [0, -1, -2, -3, -4, 1, 2, 3]
-    for piece, offset in zip(pieces, offsets):
-        level = lax.rem(base[0] + (offset + Z), Z)
-        target = held.at[pl.ds(pl.multiple_of(level * level_rows, 16), level_rows)]
-        pltpu.make_async_copy(piece, target, in_sem.at[level]).start()
-    depth = WIDTH // PARTS
+
+    def row_move(part):
+        span = pl.ds(part * depth, depth)
+        return pltpu.make_async_copy(got.at[:, :, span], normed.at[:, :, span], row_sem.at[part])
+
+    for level in range(Z):
+        if level < PARTS:
+            row_move(level).start()
+        target = held.at[level * level_rows : (level + 1) * level_rows]
+        for piece, offset in zip(pieces, offsets):
+
+            @pl.when(lax.rem(base[0] + (offset + Z), Z) == level)
+            def _(piece=piece):
+                pltpu.make_async_copy(piece, target, in_sem.at[level]).start()
+
     total = jnp.zeros((TOK, 4 * HEAD_SIZE), jnp.float32)
     arrived = 0
     for part in range(PARTS):
         span = slice(part * depth, (part + 1) * depth)
-        rows = got[:, :, span].astype(jnp.float32).reshape(TOK, depth).astype(jnp.bfloat16)
+        row_move(part).wait()
+        rows = normed[:, :, span].astype(jnp.float32).reshape(TOK, depth).astype(jnp.bfloat16)
         while arrived * level_rows < (part + 1) * depth:
             rows_of = slice(arrived * level_rows, (arrived + 1) * level_rows)
             pltpu.make_async_copy(pieces[0], held.at[rows_of], in_sem.at[arrived]).wait()
@@ -395,12 +407,14 @@
             jax.ShapeDtypeStruct((TOK, 2 * HEAD_SIZE), bf16),
             jax.ShapeDtypeStruct((Z, TOK, 2 * HEAD_SIZE), bf16),
         ),
-        in_specs=[whole(pltpu.SMEM), whole()] + [whole(pltpu.HBM)] * Z + [whole(), whole()],
+        in_specs=[whole(pltpu.SMEM)] + [whole(pltpu.HBM)] * (Z + 1) + [whole(), whole()],
         out_specs=(whole(), whole(pltpu.HBM)),
         scratch_shapes=[
             pltpu.VMEM((WIDTH, 4 * HEAD_SIZE), bf16),
+            pltpu.VMEM((N_HEADS, ROWS, WIDTH), bf16),
             pltpu.VMEM((TOK, 2 * HEAD_SIZE), bf16),
             pltpu.SemaphoreType.DMA((Z,)),
+            pltpu.SemaphoreType.DMA((PARTS,)),
             pltpu.SemaphoreType.DMA((Z,)),
         ],
         compiler_params=project_params,

time: 231 us -> 231 us (level)
  the two profiles are of different devices: /device:TPU:74 before, /device:TPU:64 now
where the time goes in v8:
time: 231 us; the launch traced here: 230 us
  waiting for transfers between devices  95.4 us (41%)
  starting transfers between devices  65.5 us (28%)
  blocking collectives  40.2 us (17%)
  Pallas kernels  17.9 us (8%)
  other arithmetic  5.28 us (2%)
  local copies, waits for them, and re-layouts  4.93 us (2%)
    ppermute x9, waiting for transfers between devices, ctx_shift(): lax.ppermute(value, 'ctx', [(i, (i + steps) % N_CTX) for i in range(N_CTX)])  55.5 us
    ppermute x9, starting transfers between devices, ctx_shift(): lax.ppermute(value, 'ctx', [(i, (i + steps) % N_CTX) for i in range(N_CTX)])  32.9 us
    all_to_all x2, waiting for transfers between devices, exchange_y(): lax.all_to_all(value, 'ctx', 0, 0, tiled=True, axis_index_groups=Y_GROUPS)  27.6 us
    all_to_all x1, blocking collectives, exchange_heads(): return lax.all_to_all(value, 'heads', 0, 0, tiled=True)  25.4 us
    all_gather x1, blocking collectives, shards(): lax.all_gather(query, 'ctx', axis=0, tiled=True, axis_index_groups=Y_GROUPS)  14.8 us
    all_to_all x1, waiting for transfers between devices, shards(): lax.all_to_all(sent, 'ctx', 0, 0, tiled=True, axis_index_groups=LEVEL_PAIRS)  12.3 us
    all_to_all x2, starting transfers between devices, exchange_y(): lax.all_to_all(value, 'ctx', 0, 0, tiled=True, axis_index_groups=Y_GROUPS)  11.1 us
    all_to_all x1, starting transfers between devices, shards(): lax.all_to_all(pair, 'ctx', 0, 0, tiled=True, axis_index_groups=Z_GROUPS)  7.61 us
  transfers between devices with their start and end apart: 14, of which 8 were waited for; matrix products, arithmetic and copies ran while one was open for 3% of the time, Pallas kernels for 1%

profile of v8, /device:TPU:64, one launch (start us, length us, event | category | flops | bytes accessed | tf_op | source)
XLA Modules:
  0.0 230.2 jit_solution(3991705792949963718)
XLA Ops:
  0.7 2.6 %prepare.1 = (bf16[128,256]{1,0:T(8,128)(2,1)}, bf16[4,168,512]{2,1,0:T(8,128)(2,1)}) custom-call(bf16[128,128]{1,0:T(8,128)(2,1)} %keys.1, bf16[128,128]{1,0:T(8,128)(2,1)} %values.1, bf16[168,256]{1,0:T(8,128)(2,1)} %proj_query.1, bf16[168,128]{1,0:T(8,128)(2,1)} %key_projection.1, bf16[168,128]{1,0:T(8,128)(2,1)} %value_projection.1), custom_call_target="tpu_custom_call" | custom-call | tf_op jit(solution)/shard_map/prepare/pallas_call | solution.py:329
  3.3 6.1 %collective-permute-start.1 = (bf16[128,256]{1,0:T(8,128)(2,1)}, bf16[128,256]{1,0:T(8,128)(2,1)S(1)}, u32[]{:S(2)}, u32[]{:S(2)}) collective-permute-start(bf16[128,256]{1,0:T(8,128)(2,1)} %get-tuple-element.6), channel_id=1, source_target_pairs={{0,128},{16,144},{32,160},{48,176},{64,192},{80,208},{96,224},{112... | collective-permute-start | bytes 196616 | tf_op jit(solution)/shard_map/ppermute | solution.py:304
  9.4 5.5 %collective-permute-start = (bf16[128,256]{1,0:T(8,128)(2,1)}, bf16[128,256]{1,0:T(8,128)(2,1)S(1)}, u32[]{:S(2)}, u32[]{:S(2)}) collective-permute-start(bf16[128,256]{1,0:T(8,128)(2,1)} %get-tuple-element.6), channel_id=1, source_target_pairs={{0,64},{16,80},{32,96},{48,112},{64,128},{80,144},{96,160},{112,17... | collective-permute-start | bytes 196616 | tf_op jit(solution)/shard_map/ppermute | solution.py:304
  18.9 7.1 %all-to-all-start = ((bf16[4,256,256]{2,1,0:T(8,128)(2,1)}), bf16[4,256,256]{2,1,0:T(8,128)(2,1)S(1)}, u32[]{:S(2)}, u32[]{:S(2)}) async-start(bf16[4,256,256]{2,1,0:T(8,128)(2,1)} %broadcast_select_fusion), calls=%async_computation | async-start | bytes 1048576 | tf_op jit(solution)/shard_map/all_to_all | solution.py:300
  27.9 13.3 %all-to-all-done.blocks = bf16[4,256,256]{2,1,0:T(8,128)(2,1)S(1)} async-done(((bf16[4,256,256]{2,1,0:T(8,128)(2,1)}), bf16[4,256,256]{2,1,0:T(8,128)(2,1)S(1)}, u32[]{:S(2)}, u32[]{:S(2)}) %all-to-all-start) | async-done | bytes 524320 | tf_op jit(solution)/shard_map/all_to_all | solution.py:300
  43.3 25.4 %all_to_all.30.got = bf16[16,8,5760]{2,1,0:T(8,128)(2,1)S(1)} all-to-all(bf16[16,8,5760]{2,1,0:T(8,128)(2,1)S(1)} %first_layer.1), channel_id=1, replica_groups=mesh['ctx'=32,'heads'=16] {'heads'}, dimensions={0} | all-to-all | bytes 2949120 | tf_op jit(solution)/shard_map/all_to_all | solution.py:296
  68.7 4.0 %all-to-all-start.3 = ((bf16[4,168,512]{2,1,0:T(8,128)(2,1)}), bf16[4,168,512]{2,1,0:T(8,128)(2,1)S(1)}, u32[]{:S(2)}, u32[]{:S(2)}) async-start(bf16[4,168,512]{2,1,0:T(8,128)(2,1)} %get-tuple-element.7), calls=%async_computation.3 | async-start | bytes 1376256 | tf_op jit(solution)/shard_map/all_to_all | solution.py:300
  74.5 14.3 %all-to-all-done.3 = bf16[4,168,512]{2,1,0:T(8,128)(2,1)S(1)} async-done(((bf16[4,168,512]{2,1,0:T(8,128)(2,1)}), bf16[4,168,512]{2,1,0:T(8,128)(2,1)S(1)}, u32[]{:S(2)}, u32[]{:S(2)}) %all-to-all-start.3) | async-done | bytes 688160 | tf_op jit(solution)/shard_map/all_to_all | solution.py:300
  88.7 7.2 %all-to-all-start.2 = ((bf16[16,8,5760]{2,1,0:T(8,128)(2,1)}), bf16[16,8,5760]{2,1,0:T(8,128)(2,1)S(1)}, u32[]{:S(2)}, u32[]{:S(2)}) async-start(bf16[16,8,5760]{2,1,0:T(8,128)(2,1)} %norms.1), calls=%async_computation.2 | async-start | bytes 2949120 | tf_op jit(solution)/shard_map/all_to_all | solution.py:296
  96.0 2.7 %collective-permute-start.2 = (bf16[672,512]{1,0:T(8,128)(2,1)S(1)}, bf16[672,512]{1,0:T(8,128)(2,1)S(1)}, u32[]{:S(2)}, u32[]{:S(2)}) collective-permute-start(bf16[672,512]{1,0:T(8,128)(2,1)S(1)} %bitcast.10), channel_id=1, source_target_pairs={{0,64},{16,80},{32,96},{48,112},{64,128},{80,144},{96,160},{112,17... | collective-permute-start | bytes 2064392 | tf_op jit(solution)/shard_map/ppermute | solution.py:304
  98.8 3.1 %collective-permute-start.6 = (bf16[672,512]{1,0:T(8,128)(2,1)S(1)}, bf16[672,512]{1,0:T(8,128)(2,1)S(1)}, u32[]{:S(2)}, u32[]{:S(2)}) collective-permute-start(bf16[672,512]{1,0:T(8,128)(2,1)S(1)} %bitcast.11), channel_id=1, source_target_pairs={{0,448},{16,464},{32,480},{48,496},{64,0},{80,16},{96,32},{112,48}... | collective-permute-start | bytes 2064392 | tf_op jit(solution)/shard_map/ppermute | solution.py:304
  101.9 14.0 %collective-permute-done.2.refs_1_ = bf16[672,512]{1,0:T(8,128)(2,1)S(1)} collective-permute-done((bf16[672,512]{1,0:T(8,128)(2,1)S(1)}, bf16[672,512]{1,0:T(8,128)(2,1)S(1)}, u32[]{:S(2)}, u32[]{:S(2)}) %collective-permute-start.2) | collective-permute-done | bytes 688160 | tf_op jit(solution)/shard_map/ppermute | solution.py:304
  115.9 2.5 %collective-permute-start.3 = (bf16[672,512]{1,0:T(8,128)(2,1)S(1)}, bf16[672,512]{1,0:T(8,128)(2,1)S(1)}, u32[]{:S(2)}, u32[]{:S(2)}) collective-permute-start(bf16[672,512]{1,0:T(8,128)(2,1)S(1)} %collective-permute-done.2.refs_1_), channel_id=1, source_target_pairs={{0,64},{16,80},{32,96},{48,112},{64,128},{80,144},{96,160},{112,17... | collective-permute-start | bytes 2064392 | tf_op jit(solution)/shard_map/ppermute | solution.py:304
  118.4 4.3 %collective-permute-start.7 = (bf16[672,512]{1,0:T(8,128)(2,1)S(1)}, bf16[672,512]{1,0:T(8,128)(2,1)S(1)}, u32[]{:S(2)}, u32[]{:S(2)}) collective-permute-start(bf16[672,512]{1,0:T(8,128)(2,1)S(1)} %collective-permute-done.6.refs_5_), channel_id=1, source_target_pairs={{0,448},{16,464},{32,480},{48,496},{64,0},{80,16},{96,32},{112,48}... | collective-permute-start | bytes 2064392 | tf_op jit(solution)/shard_map/ppermute | solution.py:304
  122.7 13.2 %collective-permute-done.3.refs_2_ = bf16[672,512]{1,0:T(8,128)(2,1)S(1)} collective-permute-done((bf16[672,512]{1,0:T(8,128)(2,1)S(1)}, bf16[672,512]{1,0:T(8,128)(2,1)S(1)}, u32[]{:S(2)}, u32[]{:S(2)}) %collective-permute-start.3) | collective-permute-done | bytes 688160 | tf_op jit(solution)/shard_map/ppermute | solution.py:304
  137.8 4.9 %collective-permute-start.8 = (bf16[672,512]{1,0:T(8,128)(2,1)S(1)}, bf16[672,512]{1,0:T(8,128)(2,1)S(1)}, u32[]{:S(2)}, u32[]{:S(2)}) collective-permute-start(bf16[672,512]{1,0:T(8,128)(2,1)S(1)} %collective-permute-done.7.refs_6_), channel_id=1, source_target_pairs={{0,448},{16,464},{32,480},{48,496},{64,0},{80,16},{96,32},{112,48}... | collective-permute-start | bytes 2064392 | tf_op jit(solution)/shard_map/ppermute | solution.py:304
  142.6 12.3 %collective-permute-done.4.refs_3_ = bf16[672,512]{1,0:T(8,128)(2,1)S(1)} collective-permute-done((bf16[672,512]{1,0:T(8,128)(2,1)S(1)}, bf16[672,512]{1,0:T(8,128)(2,1)S(1)}, u32[]{:S(2)}, u32[]{:S(2)}) %collective-permute-start.4) | collective-permute-done | bytes 688160 | tf_op jit(solution)/shard_map/ppermute | solution.py:304
  159.6 13.7 %collective-permute-done.5.refs_4_ = bf16[672,512]{1,0:T(8,128)(2,1)} collective-permute-done((bf16[672,512]{1,0:T(8,128)(2,1)S(1)}, bf16[672,512]{1,0:T(8,128)(2,1)}, u32[]{:S(2)}, u32[]{:S(2)}) %collective-permute-start.5) | collective-permute-done | bytes 688160 | tf_op jit(solution)/shard_map/ppermute | solution.py:304
  174.5 6.3 %project.1 = (bf16[128,256]{1,0:T(8,128)(2,1)}, bf16[8,128,256]{2,1,0:T(8,128)(2,1)}) custom-call(s32[3]{0:T(128)} %copy-done.2, bf16[16,8,5760]{2,1,0:T(8,128)(2,1)} %copy-done.4, bf16[672,512]{1,0:T(8,128)(2,1)} %bitcast.12, bf16[672,512]{1,0:T(8,128)(2,1)} %copy-done.6, bf16[672,512]{1,0:T(8,128)(2,1)} %copy-done.8, bf16[672,512]{1,0:T(8,128)(2,1)} %copy-done.10, ...), custom_call_target="tpu_custom_call" | custom-call | tf_op jit(solution)/shard_map/project/pallas_call | solution.py:404
  180.8 7.6 %all-to-all-start.4 = ((bf16[8,128,256]{2,1,0:T(8,128)(2,1)}), bf16[8,128,256]{2,1,0:T(8,128)(2,1)S(1)}, u32[]{:S(2)}, u32[]{:S(2)}) async-start(bf16[8,128,256]{2,1,0:T(8,128)(2,1)} %get-tuple-element.9), calls=%async_computation.4 | async-start | bytes 1048576 | tf_op jit(solution)/shard_map/all_to_all | solution.py:424
  189.1 14.8 %all_gather.3.queries = bf16[512,256]{1,0:T(8,128)(2,1)S(1)} all-gather(bf16[128,256]{1,0:T(8,128)(2,1)} %get-tuple-element.8), channel_id=1, replica_groups={{0,16,32,48},{64,80,96,112},{128,144,160,176},{192,208,224,240},{256,27..., dimensions={0}, use_global_device_ids=true | all-gather | bytes 327680 | tf_op jit(solution)/shard_map/all_gather | solution.py:426
  204.1 3.8 %second_layer.1 = bf16[8,64,384]{2,1,0:T(8,128)(2,1)} custom-call(s32[3]{0:T(128)S(1)} %copy-done.3, bf16[512,256]{1,0:T(8,128)(2,1)S(1)} %all_gather.3.queries, bf16[1024,256]{1,0:T(8,128)(2,1)S(1)} %bitcast.9, s32[512,128]{1,0:T(8,128)S(1)} %broadcast_in_dim.55.low), custom_call_target="tpu_custom_call" | custom-call | tf_op jit(solution)/shard_map/second_layer/pallas_call | solution.py:435
  207.9 6.7 %all-to-all-start.5 = ((bf16[8,64,384]{2,1,0:T(8,128)(2,1)}), bf16[8,64,384]{2,1,0:T(8,128)(2,1)S(1)}, u32[]{:S(2)}, u32[]{:S(2)}) async-start(bf16[8,64,384]{2,1,0:T(8,128)(2,1)} %second_layer.1), calls=%async_computation.5 | async-start | bytes 786432 | tf_op jit(solution)/shard_map/all_to_all | solution.py:444
  216.2 12.3 %all-to-all-done.5.got = bf16[8,64,384]{2,1,0:T(8,128)(2,1)S(1)} async-done(((bf16[8,64,384]{2,1,0:T(8,128)(2,1)}), bf16[8,64,384]{2,1,0:T(8,128)(2,1)S(1)}, u32[]{:S(2)}, u32[]{:S(2)}) %all-to-all-start.5) | async-done | bytes 393248 | tf_op jit(solution)/shard_map/all_to_all | solution.py:444
  (60 shorter events, 21.6 us)
Async XLA Ops:
  0.6 27.2 %copy-start.14 = (s32[2]{0:T(128)S(1)}, s32[2]{0:T(128)}, u32[]{:S(2)}) copy-start(s32[2]{0:T(128)} %param.22) | copy-start | bytes 28
  0.6 40.7 %copy-start.1 = (bf16[128,256]{1,0:T(8,128)(2,1)S(1)}, bf16[128,256]{1,0:T(8,128)(2,1)}, u32[]{:S(2)}) copy-start(bf16[128,256]{1,0:T(8,128)(2,1)} %query.1) | copy-start | bytes 196612
  0.7 40.7 %copy-start = (bf16[256,5376]{1,0:T(8,128)(2,1)S(1)}, bf16[256,5376]{1,0:T(8,128)(2,1)}, u32[]{:S(2)}) copy-start(bf16[256,5376]{1,0:T(8,128)(2,1)} %out_one.1) | copy-start | bytes 8257540
  3.3 13.9 %collective-permute-start.1 = (bf16[128,256]{1,0:T(8,128)(2,1)}, bf16[128,256]{1,0:T(8,128)(2,1)S(1)}, u32[]{:S(2)}, u32[]{:S(2)}) collective-permute-start(bf16[128,256]{1,0:T(8,128)(2,1)} %get-tuple-element.6), channel_id=1, source_target_pairs={{0,128},{16,144},{32,160},{48,176},{64,192},{80,208},{96,224},{112... | collective-permute-start | bytes 196616 | tf_op jit(solution)/shard_map/ppermute | solution.py:304
  9.4 7.8 %collective-permute-start = (bf16[128,256]{1,0:T(8,128)(2,1)}, bf16[128,256]{1,0:T(8,128)(2,1)S(1)}, u32[]{:S(2)}, u32[]{:S(2)}) collective-permute-start(bf16[128,256]{1,0:T(8,128)(2,1)} %get-tuple-element.6), channel_id=1, source_target_pairs={{0,64},{16,80},{32,96},{48,112},{64,128},{80,144},{96,160},{112,17... | collective-permute-start | bytes 196616 | tf_op jit(solution)/shard_map/ppermute | solution.py:304
  18.9 22.3 %all-to-all-start = ((bf16[4,256,256]{2,1,0:T(8,128)(2,1)}), bf16[4,256,256]{2,1,0:T(8,128)(2,1)S(1)}, u32[]{:S(2)}, u32[]{:S(2)}) async-start(bf16[4,256,256]{2,1,0:T(8,128)(2,1)} %broadcast_select_fusion), calls=%async_computation | async-start | bytes 1048576 | tf_op jit(solution)/shard_map/all_to_all | solution.py:300
  27.1 16.2 %copy-start.2 = (s32[3]{0:T(128)}, s32[3]{0:T(128)S(1)}, u32[]{:S(2)}) copy-start(s32[3]{0:T(128)S(1)} %pad_add_fusion.base) | copy-start | bytes 40
  43.3 29.4 %copy-start.12 = (f32[5376]{0:T(1024)S(1)}, f32[5376]{0:T(1024)}, u32[]{:S(2)}) copy-start(f32[5376]{0:T(1024)} %param.17) | copy-start | bytes 64516
  43.3 29.4 %copy-start.13 = (f32[5376]{0:T(1024)S(1)}, f32[5376]{0:T(1024)}, u32[]{:S(2)}) copy-start(f32[5376]{0:T(1024)} %param.18) | copy-start | bytes 64516
  68.7 20.0 %all-to-all-start.3 = ((bf16[4,168,512]{2,1,0:T(8,128)(2,1)}), bf16[4,168,512]{2,1,0:T(8,128)(2,1)S(1)}, u32[]{:S(2)}, u32[]{:S(2)}) async-start(bf16[4,168,512]{2,1,0:T(8,128)(2,1)} %get-tuple-element.7), calls=%async_computation.3 | async-start | bytes 1376256 | tf_op jit(solution)/shard_map/all_to_all | solution.py:300
  88.7 84.6 %all-to-all-start.2 = ((bf16[16,8,5760]{2,1,0:T(8,128)(2,1)}), bf16[16,8,5760]{2,1,0:T(8,128)(2,1)S(1)}, u32[]{:S(2)}, u32[]{:S(2)}) async-start(bf16[16,8,5760]{2,1,0:T(8,128)(2,1)} %norms.1), calls=%async_computation.2 | async-start | bytes 2949120 | tf_op jit(solution)/shard_map/all_to_all | solution.py:296
  96.0 19.9 %collective-permute-start.2 = (bf16[672,512]{1,0:T(8,128)(2,1)S(1)}, bf16[672,512]{1,0:T(8,128)(2,1)S(1)}, u32[]{:S(2)}, u32[]{:S(2)}) collective-permute-start(bf16[672,512]{1,0:T(8,128)(2,1)S(1)} %bitcast.10), channel_id=1, source_target_pairs={{0,64},{16,80},{32,96},{48,112},{64,128},{80,144},{96,160},{112,17... | collective-permute-start | bytes 2064392 | tf_op jit(solution)/shard_map/ppermute | solution.py:304
  98.8 19.6 %collective-permute-start.6 = (bf16[672,512]{1,0:T(8,128)(2,1)S(1)}, bf16[672,512]{1,0:T(8,128)(2,1)S(1)}, u32[]{:S(2)}, u32[]{:S(2)}) collective-permute-start(bf16[672,512]{1,0:T(8,128)(2,1)S(1)} %bitcast.11), channel_id=1, source_target_pairs={{0,448},{16,464},{32,480},{48,496},{64,0},{80,16},{96,32},{112,48}... | collective-permute-start | bytes 2064392 | tf_op jit(solution)/shard_map/ppermute | solution.py:304
  115.9 57.5 %copy-start.6 = (bf16[672,512]{1,0:T(8,128)(2,1)}, bf16[672,512]{1,0:T(8,128)(2,1)S(1)}, u32[]{:S(2)}) copy-start(bf16[672,512]{1,0:T(8,128)(2,1)S(1)} %collective-permute-done.2.refs_1_) | copy-start | bytes 2064388
  115.9 20.0 %collective-permute-start.3 = (bf16[672,512]{1,0:T(8,128)(2,1)S(1)}, bf16[672,512]{1,0:T(8,128)(2,1)S(1)}, u32[]{:S(2)}, u32[]{:S(2)}) collective-permute-start(bf16[672,512]{1,0:T(8,128)(2,1)S(1)} %collective-permute-done.2.refs_1_), channel_id=1, source_target_pairs={{0,64},{16,80},{32,96},{48,112},{64,128},{80,144},{96,160},{112,17... | collective-permute-start | bytes 2064392 | tf_op jit(solution)/shard_map/ppermute | solution.py:304
  118.4 54.9 %copy-start.7 = (bf16[672,512]{1,0:T(8,128)(2,1)}, bf16[672,512]{1,0:T(8,128)(2,1)S(1)}, u32[]{:S(2)}) copy-start(bf16[672,512]{1,0:T(8,128)(2,1)S(1)} %collective-permute-done.6.refs_5_) | copy-start | bytes 2064388
  118.4 19.4 %collective-permute-start.7 = (bf16[672,512]{1,0:T(8,128)(2,1)S(1)}, bf16[672,512]{1,0:T(8,128)(2,1)S(1)}, u32[]{:S(2)}, u32[]{:S(2)}) collective-permute-start(bf16[672,512]{1,0:T(8,128)(2,1)S(1)} %collective-permute-done.6.refs_5_), channel_id=1, source_target_pairs={{0,448},{16,464},{32,480},{48,496},{64,0},{80,16},{96,32},{112,48}... | collective-permute-start | bytes 2064392 | tf_op jit(solution)/shard_map/ppermute | solution.py:304
  135.8 19.1 %collective-permute-start.4 = (bf16[672,512]{1,0:T(8,128)(2,1)S(1)}, bf16[672,512]{1,0:T(8,128)(2,1)S(1)}, u32[]{:S(2)}, u32[]{:S(2)}) collective-permute-start(bf16[672,512]{1,0:T(8,128)(2,1)S(1)} %collective-permute-done.3.refs_2_), channel_id=1, source_target_pairs={{0,64},{16,80},{32,96},{48,112},{64,128},{80,144},{96,160},{112,17... | collective-permute-start | bytes 2064392 | tf_op jit(solution)/shard_map/ppermute | solution.py:304
  137.8 35.6 %copy-start.9 = (bf16[672,512]{1,0:T(8,128)(2,1)}, bf16[672,512]{1,0:T(8,128)(2,1)S(1)}, u32[]{:S(2)}) copy-start(bf16[672,512]{1,0:T(8,128)(2,1)S(1)} %collective-permute-done.7.refs_6_) | copy-start | bytes 2064388
  137.8 20.9 %collective-permute-start.8 = (bf16[672,512]{1,0:T(8,128)(2,1)S(1)}, bf16[672,512]{1,0:T(8,128)(2,1)S(1)}, u32[]{:S(2)}, u32[]{:S(2)}) collective-permute-start(bf16[672,512]{1,0:T(8,128)(2,1)S(1)} %collective-permute-done.7.refs_6_), channel_id=1, source_target_pairs={{0,448},{16,464},{32,480},{48,496},{64,0},{80,16},{96,32},{112,48}... | collective-permute-start | bytes 2064392 | tf_op jit(solution)/shard_map/ppermute | solution.py:304
  155.0 18.4 %collective-permute-start.5 = (bf16[672,512]{1,0:T(8,128)(2,1)S(1)}, bf16[672,512]{1,0:T(8,128)(2,1)}, u32[]{:S(2)}, u32[]{:S(2)}) collective-permute-start(bf16[672,512]{1,0:T(8,128)(2,1)S(1)} %collective-permute-done.4.refs_3_), channel_id=1, source_target_pairs={{0,64},{16,80},{32,96},{48,112},{64,128},{80,144},{96,160},{112,17... | collective-permute-start | bytes 2064392 | tf_op jit(solution)/shard_map/ppermute | solution.py:304
  180.7 23.4 %copy-start.3 = (s32[3]{0:T(128)S(1)}, s32[3]{0:T(128)}, u32[]{:S(2)}) copy-start(s32[3]{0:T(128)} %copy-done.2) | copy-start | bytes 40
  180.8 23.2 %all-to-all-start.4 = ((bf16[8,128,256]{2,1,0:T(8,128)(2,1)}), bf16[8,128,256]{2,1,0:T(8,128)(2,1)S(1)}, u32[]{:S(2)}, u32[]{:S(2)}) async-start(bf16[8,128,256]{2,1,0:T(8,128)(2,1)} %get-tuple-element.9), calls=%async_computation.4 | async-start | bytes 1048576 | tf_op jit(solution)/shard_map/all_to_all | solution.py:424
  207.9 20.7 %all-to-all-start.5 = ((bf16[8,64,384]{2,1,0:T(8,128)(2,1)}), bf16[8,64,384]{2,1,0:T(8,128)(2,1)S(1)}, u32[]{:S(2)}, u32[]{:S(2)}) async-start(bf16[8,64,384]{2,1,0:T(8,128)(2,1)} %second_layer.1), calls=%async_computation.5 | async-start | bytes 786432 | tf_op jit(solution)/shard_map/all_to_all | solution.py:444
  (5 other events, 17.7 us)

commit v9 on v6

--- a/solution.py
+++ b/solution.py
@@ -31,6 +31,9 @@
 ]
 Z_GROUPS = [[z * Y_HI + y for z in range(Z)] for y in range(Y_HI)]
 VMEM_LIMIT = 24 * 1024 * 1024
+FIRST_LIMIT = 24 * 1024 * 1024
+NORM_LIMIT = 24 * 1024 * 1024
+PROJECT_LIMIT = 56 * 1024 * 1024
 
 
 def whole(memory_space=pltpu.VMEM):
@@ -176,20 +179,28 @@
 
 def project_kernel(base, got, *refs):
     pieces, refs = refs[: Z + 1], refs[Z + 1 :]
-    turn_cos, turn_sin, query, pair, held, block, in_sem, out_sem = refs
+    turn_cos, turn_sin, query, pair, held, normed, block, in_sem, row_sem, out_sem = refs
     level_rows = WIDTH // Z
+    depth = WIDTH // PARTS
     offsets = [0, -1, 1, -2, 2, -3, 3, 4, 4]
     for index, (piece, offset) in enumerate(zip(pieces, offsets)):
         level = lax.rem(base[0] + (offset + Z), Z)
         at = level * level_rows + (level_rows // 2 if index == Z else 0)
         target = held.at[pl.ds(pl.multiple_of(at, 16), piece.shape[0])]
         pltpu.make_async_copy(piece, target, in_sem.at[level]).start()
-    depth = WIDTH // PARTS
+
+    def row_move(part):
+        span = pl.ds(part * depth, depth)
+        return pltpu.make_async_copy(got.at[:, :, span], normed.at[:, :, span], row_sem.at[part])
+
+    for part in range(PARTS):
+        row_move(part).start()
     total = jnp.zeros((TOK, 4 * HEAD_SIZE), jnp.float32)
     arrived = 0
     for part in range(PARTS):
         span = slice(part * depth, (part + 1) * depth)
-        rows = got[:, :, span].astype(jnp.float32).reshape(TOK, depth).astype(jnp.bfloat16)
+        row_move(part).wait()
+        rows = normed[:, :, span].astype(jnp.float32).reshape(TOK, depth).astype(jnp.bfloat16)
         while arrived * level_rows < (part + 1) * depth:
             rows_of = slice(arrived * level_rows, (arrived + 1) * level_rows)
             pltpu.make_async_copy(pieces[0], held.at[rows_of], in_sem.at[arrived]).wait()
@@ -308,6 +319,9 @@
     place_z, place_y = ctx_place // Y_HI, ctx_place % Y_HI
     bf16, f32 = jnp.bfloat16, jnp.float32
     params = partial(pltpu.CompilerParams, vmem_limit_bytes=VMEM_LIMIT)
+    first_params = pltpu.CompilerParams(vmem_limit_bytes=FIRST_LIMIT)
+    norm_params = pltpu.CompilerParams(vmem_limit_bytes=NORM_LIMIT)
+    project_params = pltpu.CompilerParams(vmem_limit_bytes=PROJECT_LIMIT)
 
     own, spread = pl.pallas_call(
         prepare_kernel,
@@ -357,7 +371,7 @@
         in_specs=[whole(pltpu.SMEM)] + [whole()] * 6,
         out_specs=whole(),
         scratch_shapes=[pltpu.VMEM((2 * TOK, 9 * TOK), f32)],
-        compiler_params=params(),
+        compiler_params=first_params,
         cost_estimate=pl.CostEstimate(
             flops=600_000_000, bytes_accessed=6_000_000, transcendentals=300_000
         ),
@@ -378,7 +392,7 @@
         in_specs=[whole()] * 3,
         out_specs=whole(),
         scratch_shapes=[pltpu.VMEM((ROWS, WIDTH), f32)] * 2,
-        compiler_params=params(),
+        compiler_params=norm_params,
         name="norms",
     )(got, post_gain[None, :], pre_gain[None, :])
     got = exchange_heads(sent)
@@ -395,15 +409,17 @@
             jax.ShapeDtypeStruct((TOK, 2 * HEAD_SIZE), bf16),
             jax.ShapeDtypeStruct((Z, TOK, 2 * HEAD_SIZE), bf16),
         ),
-        in_specs=[whole(pltpu.SMEM), whole()] + [whole(pltpu.HBM)] * (Z + 1) + [whole(), whole()],
+        in_specs=[whole(pltpu.SMEM)] + [whole(pltpu.HBM)] * (Z + 2) + [whole(), whole()],
         out_specs=(whole(), whole(pltpu.HBM)),
         scratch_shapes=[
             pltpu.VMEM((WIDTH, 4 * HEAD_SIZE), bf16),
+            pltpu.VMEM((N_HEADS, ROWS, WIDTH), bf16),
             pltpu.VMEM((TOK, 2 * HEAD_SIZE), bf16),
             pltpu.SemaphoreType.DMA((Z,)),
+            pltpu.SemaphoreType.DMA((PARTS,)),
             pltpu.SemaphoreType.DMA((Z,)),
         ],
-        compiler_params=pltpu.CompilerParams(vmem_limit_bytes=50 * 1024 * 1024),
+        compiler_params=project_params,
         name="project",
     )(bases, got, *pieces, turn_cos, turn_sin)
 

time: 225 us -> 226 us (level)
  the two profiles are of different devices: /device:TPU:64 before, /device:TPU:74 now
where the time goes in v9:
time: 226 us; the launch traced here: 225 us
  waiting for transfers between devices  89.2 us (39%)
  starting transfers between devices  68.2 us (30%)
  blocking collectives  39 us (17%)
  Pallas kernels  17.8 us (8%)
  other arithmetic  5.27 us (2%)
  local copies, waits for them, and re-layouts  4.85 us (2%)
    ppermute x10, waiting for transfers between devices, ctx_shift(): lax.ppermute(value, 'ctx', [(i, (i + steps) % N_CTX) for i in range(N_CTX)])  44 us
    ppermute x10, starting transfers between devices, ctx_shift(): lax.ppermute(value, 'ctx', [(i, (i + steps) % N_CTX) for i in range(N_CTX)])  37.7 us
    all_to_all x2, waiting for transfers between devices, exchange_y(): lax.all_to_all(value, 'ctx', 0, 0, tiled=True, axis_index_groups=Y_GROUPS)  32.1 us
    all_to_all x1, blocking collectives, exchange_heads(): return lax.all_to_all(value, 'heads', 0, 0, tiled=True)  23.9 us
    all_gather x1, blocking collectives, shards(): lax.all_gather(query, 'ctx', axis=0, tiled=True, axis_index_groups=Y_GROUPS)  15.1 us
    all_to_all x1, waiting for transfers between devices, shards(): lax.all_to_all(sent, 'ctx', 0, 0, tiled=True, axis_index_groups=LEVEL_PAIRS)  13.1 us
    all_to_all x2, starting transfers between devices, exchange_y(): lax.all_to_all(value, 'ctx', 0, 0, tiled=True, axis_index_groups=Y_GROUPS)  10.2 us
    all_to_all x1, starting transfers between devices, shards(): lax.all_to_all(pair, 'ctx', 0, 0, tiled=True, axis_index_groups=Z_GROUPS)  8.22 us
  transfers between devices with their start and end apart: 15, of which 9 were waited for; matrix products, arithmetic and copies ran while one was open for 3% of the time, Pallas kernels for 1%

profile of v9, /device:TPU:74, one launch (start us, length us, event | category | flops | bytes accessed | tf_op | source)
XLA Modules:
  0.0 225.2 jit_solution(5832559424585308034)
XLA Ops:
  0.7 2.6 %prepare.1 = (bf16[128,256]{1,0:T(8,128)(2,1)}, bf16[4,168,512]{2,1,0:T(8,128)(2,1)}) custom-call(bf16[128,128]{1,0:T(8,128)(2,1)} %keys.1, bf16[128,128]{1,0:T(8,128)(2,1)} %values.1, bf16[168,256]{1,0:T(8,128)(2,1)} %proj_query.1, bf16[168,128]{1,0:T(8,128)(2,1)} %key_projection.1, bf16[168,128]{1,0:T(8,128)(2,1)} %value_projection.1), custom_call_target="tpu_custom_call" | custom-call | tf_op jit(solution)/shard_map/prepare/pallas_call | solution.py:326
  3.3 6.1 %collective-permute-start.1 = (bf16[128,256]{1,0:T(8,128)(2,1)}, bf16[128,256]{1,0:T(8,128)(2,1)S(1)}, u32[]{:S(2)}, u32[]{:S(2)}) collective-permute-start(bf16[128,256]{1,0:T(8,128)(2,1)} %get-tuple-element.6), channel_id=1, source_target_pairs={{0,128},{16,144},{32,160},{48,176},{64,192},{80,208},{96,224},{112... | collective-permute-start | bytes 196616 | tf_op jit(solution)/shard_map/ppermute | solution.py:301
  9.4 5.5 %collective-permute-start = (bf16[128,256]{1,0:T(8,128)(2,1)}, bf16[128,256]{1,0:T(8,128)(2,1)S(1)}, u32[]{:S(2)}, u32[]{:S(2)}) collective-permute-start(bf16[128,256]{1,0:T(8,128)(2,1)} %get-tuple-element.6), channel_id=1, source_target_pairs={{0,64},{16,80},{32,96},{48,112},{64,128},{80,144},{96,160},{112,17... | collective-permute-start | bytes 196616 | tf_op jit(solution)/shard_map/ppermute | solution.py:301
  18.9 6.2 %all-to-all-start = ((bf16[4,256,256]{2,1,0:T(8,128)(2,1)}), bf16[4,256,256]{2,1,0:T(8,128)(2,1)S(1)}, u32[]{:S(2)}, u32[]{:S(2)}) async-start(bf16[4,256,256]{2,1,0:T(8,128)(2,1)} %broadcast_select_fusion), calls=%async_computation | async-start | bytes 1048576 | tf_op jit(solution)/shard_map/all_to_all | solution.py:297
  27.0 13.4 %all-to-all-done.blocks = bf16[4,256,256]{2,1,0:T(8,128)(2,1)S(1)} async-done(((bf16[4,256,256]{2,1,0:T(8,128)(2,1)}), bf16[4,256,256]{2,1,0:T(8,128)(2,1)S(1)}, u32[]{:S(2)}, u32[]{:S(2)}) %all-to-all-start) | async-done | bytes 524320 | tf_op jit(solution)/shard_map/all_to_all | solution.py:297
  42.5 23.9 %all_to_all.30.got = bf16[16,8,5760]{2,1,0:T(8,128)(2,1)S(1)} all-to-all(bf16[16,8,5760]{2,1,0:T(8,128)(2,1)S(1)} %first_layer.1), channel_id=1, replica_groups=mesh['ctx'=32,'heads'=16] {'heads'}, dimensions={0} | all-to-all | bytes 2949120 | tf_op jit(solution)/shard_map/all_to_all | solution.py:293
  66.4 4.0 %all-to-all-start.3 = ((bf16[4,168,512]{2,1,0:T(8,128)(2,1)}), bf16[4,168,512]{2,1,0:T(8,128)(2,1)S(1)}, u32[]{:S(2)}, u32[]{:S(2)}) async-start(bf16[4,168,512]{2,1,0:T(8,128)(2,1)} %get-tuple-element.7), calls=%async_computation.3 | async-start | bytes 1376256 | tf_op jit(solution)/shard_map/all_to_all | solution.py:297
  72.1 18.8 %all-to-all-done.3 = bf16[4,168,512]{2,1,0:T(8,128)(2,1)S(1)} async-done(((bf16[4,168,512]{2,1,0:T(8,128)(2,1)}), bf16[4,168,512]{2,1,0:T(8,128)(2,1)S(1)}, u32[]{:S(2)}, u32[]{:S(2)}) %all-to-all-start.3) | async-done | bytes 688160 | tf_op jit(solution)/shard_map/all_to_all | solution.py:297
  90.9 5.4 %all-to-all-start.2 = ((bf16[16,8,5760]{2,1,0:T(8,128)(2,1)}), bf16[16,8,5760]{2,1,0:T(8,128)(2,1)S(1)}, u32[]{:S(2)}, u32[]{:S(2)}) async-start(bf16[16,8,5760]{2,1,0:T(8,128)(2,1)} %norms.1), calls=%async_computation.2 | async-start | bytes 2949120 | tf_op jit(solution)/shard_map/all_to_all | solution.py:293
  96.3 2.7 %collective-permute-start.2 = (bf16[672,512]{1,0:T(8,128)(2,1)S(1)}, bf16[672,512]{1,0:T(8,128)(2,1)S(1)}, u32[]{:S(2)}, u32[]{:S(2)}) collective-permute-start(bf16[672,512]{1,0:T(8,128)(2,1)S(1)} %bitcast.10), channel_id=1, source_target_pairs={{0,64},{16,80},{32,96},{48,112},{64,128},{80,144},{96,160},{112,17... | collective-permute-start | bytes 2064392 | tf_op jit(solution)/shard_map/ppermute | solution.py:301
  99.1 3.1 %collective-permute-start.3 = (bf16[672,512]{1,0:T(8,128)(2,1)S(1)}, bf16[672,512]{1,0:T(8,128)(2,1)S(1)}, u32[]{:S(2)}, u32[]{:S(2)}) collective-permute-start(bf16[672,512]{1,0:T(8,128)(2,1)S(1)} %bitcast.11), channel_id=1, source_target_pairs={{0,448},{16,464},{32,480},{48,496},{64,0},{80,16},{96,32},{112,48}... | collective-permute-start | bytes 2064392 | tf_op jit(solution)/shard_map/ppermute | solution.py:301
  102.2 13.7 %collective-permute-done.2.refs_1_ = bf16[672,512]{1,0:T(8,128)(2,1)S(1)} collective-permute-done((bf16[672,512]{1,0:T(8,128)(2,1)S(1)}, bf16[672,512]{1,0:T(8,128)(2,1)S(1)}, u32[]{:S(2)}, u32[]{:S(2)}) %collective-permute-start.2) | collective-permute-done | bytes 688160 | tf_op jit(solution)/shard_map/ppermute | solution.py:301
  118.4 4.3 %collective-permute-start.5 = (bf16[672,512]{1,0:T(8,128)(2,1)S(1)}, bf16[672,512]{1,0:T(8,128)(2,1)S(1)}, u32[]{:S(2)}, u32[]{:S(2)}) collective-permute-start(bf16[672,512]{1,0:T(8,128)(2,1)S(1)} %collective-permute-done.3.refs_2_), channel_id=1, source_target_pairs={{0,448},{16,464},{32,480},{48,496},{64,0},{80,16},{96,32},{112,48}... | collective-permute-start | bytes 2064392 | tf_op jit(solution)/shard_map/ppermute | solution.py:301
  122.7 12.9 %collective-permute-done.4.refs_3_ = bf16[672,512]{1,0:T(8,128)(2,1)S(1)} collective-permute-done((bf16[672,512]{1,0:T(8,128)(2,1)S(1)}, bf16[672,512]{1,0:T(8,128)(2,1)S(1)}, u32[]{:S(2)}, u32[]{:S(2)}) %collective-permute-start.4) | collective-permute-done | bytes 688160 | tf_op jit(solution)/shard_map/ppermute | solution.py:301
  137.5 4.9 %collective-permute-start.7 = (bf16[672,512]{1,0:T(8,128)(2,1)S(1)}, bf16[672,512]{1,0:T(8,128)(2,1)S(1)}, u32[]{:S(2)}, u32[]{:S(2)}) collective-permute-start(bf16[672,512]{1,0:T(8,128)(2,1)S(1)} %collective-permute-done.5.refs_4_), channel_id=1, source_target_pairs={{0,448},{16,464},{32,480},{48,496},{64,0},{80,16},{96,32},{112,48}... | collective-permute-start | bytes 2064392 | tf_op jit(solution)/shard_map/ppermute | solution.py:301
  143.2 11.2 %collective-permute-done.6.refs_5_ = bf16[672,512]{1,0:T(8,128)(2,1)S(1)} collective-permute-done((bf16[672,512]{1,0:T(8,128)(2,1)S(1)}, bf16[672,512]{1,0:T(8,128)(2,1)S(1)}, u32[]{:S(2)}, u32[]{:S(2)}) %collective-permute-start.6) | collective-permute-done | bytes 688160 | tf_op jit(solution)/shard_map/ppermute | solution.py:301
  156.4 4.9 %collective-permute-start.9 = (bf16[336,512]{1,0:T(8,128)(2,1)S(1)}, bf16[336,512]{1,0:T(8,128)(2,1)}, u32[]{:S(2)}, u32[]{:S(2)}) collective-permute-start(bf16[336,512]{1,0:T(8,128)(2,1)S(1)} %slice.14), channel_id=1, source_target_pairs={{0,448},{16,464},{32,480},{48,496},{64,0},{80,16},{96,32},{112,48}... | collective-permute-start | bytes 1032200 | tf_op jit(solution)/shard_map/ppermute | solution.py:301
  162.4 2.7 %collective-permute-done.8.refs_7_ = bf16[336,512]{1,0:T(8,128)(2,1)S(1)} collective-permute-done((bf16[336,512]{1,0:T(8,128)(2,1)S(1)}, bf16[336,512]{1,0:T(8,128)(2,1)S(1)}, u32[]{:S(2)}, u32[]{:S(2)}) %collective-permute-start.8) | collective-permute-done | bytes 344096 | tf_op jit(solution)/shard_map/ppermute | solution.py:301
  168.1 6.1 %project.1 = (bf16[128,256]{1,0:T(8,128)(2,1)}, bf16[8,128,256]{2,1,0:T(8,128)(2,1)}) custom-call(s32[3]{0:T(128)} %copy-done.2, bf16[16,8,5760]{2,1,0:T(8,128)(2,1)} %copy-done.4, bf16[672,512]{1,0:T(8,128)(2,1)} %bitcast.12, bf16[672,512]{1,0:T(8,128)(2,1)} %copy-done.8, bf16[672,512]{1,0:T(8,128)(2,1)} %copy-done.9, bf16[672,512]{1,0:T(8,128)(2,1)} %copy-done.10, ...), custom_call_target="tpu_custom_call" | custom-call | tf_op jit(solution)/shard_map/project/pallas_call | solution.py:406
  174.2 8.2 %all-to-all-start.4 = ((bf16[8,128,256]{2,1,0:T(8,128)(2,1)}), bf16[8,128,256]{2,1,0:T(8,128)(2,1)S(1)}, u32[]{:S(2)}, u32[]{:S(2)}) async-start(bf16[8,128,256]{2,1,0:T(8,128)(2,1)} %get-tuple-element.9), calls=%async_computation.4 | async-start | bytes 1048576 | tf_op jit(solution)/shard_map/all_to_all | solution.py:426
  183.2 15.1 %all_gather.3.queries = bf16[512,256]{1,0:T(8,128)(2,1)S(1)} all-gather(bf16[128,256]{1,0:T(8,128)(2,1)} %get-tuple-element.8), channel_id=1, replica_groups={{0,16,32,48},{64,80,96,112},{128,144,160,176},{192,208,224,240},{256,27..., dimensions={0}, use_global_device_ids=true | all-gather | bytes 327680 | tf_op jit(solution)/shard_map/all_gather | solution.py:428
  198.4 3.8 %second_layer.1 = bf16[8,64,384]{2,1,0:T(8,128)(2,1)} custom-call(s32[3]{0:T(128)S(1)} %copy-done.3, bf16[512,256]{1,0:T(8,128)(2,1)S(1)} %all_gather.3.queries, bf16[1024,256]{1,0:T(8,128)(2,1)S(1)} %bitcast.9, s32[512,128]{1,0:T(8,128)S(1)} %broadcast_in_dim.55.low), custom_call_target="tpu_custom_call" | custom-call | tf_op jit(solution)/shard_map/second_layer/pallas_call | solution.py:437
  202.2 6.6 %all-to-all-start.5 = ((bf16[8,64,384]{2,1,0:T(8,128)(2,1)}), bf16[8,64,384]{2,1,0:T(8,128)(2,1)S(1)}, u32[]{:S(2)}, u32[]{:S(2)}) async-start(bf16[8,64,384]{2,1,0:T(8,128)(2,1)} %second_layer.1), calls=%async_computation.5 | async-start | bytes 786432 | tf_op jit(solution)/shard_map/all_to_all | solution.py:446
  210.5 13.1 %all-to-all-done.5.got = bf16[8,64,384]{2,1,0:T(8,128)(2,1)S(1)} async-done(((bf16[8,64,384]{2,1,0:T(8,128)(2,1)}), bf16[8,64,384]{2,1,0:T(8,128)(2,1)S(1)}, u32[]{:S(2)}, u32[]{:S(2)}) %all-to-all-start.5) | async-done | bytes 393248 | tf_op jit(solution)/shard_map/all_to_all | solution.py:446
  (66 shorter events, 25.1 us)
Async XLA Ops:
  0.6 26.3 %copy-start.15 = (s32[2]{0:T(128)S(1)}, s32[2]{0:T(128)}, u32[]{:S(2)}) copy-start(s32[2]{0:T(128)} %param.22) | copy-start | bytes 28
  0.6 39.9 %copy-start.1 = (bf16[128,256]{1,0:T(8,128)(2,1)S(1)}, bf16[128,256]{1,0:T(8,128)(2,1)}, u32[]{:S(2)}) copy-start(bf16[128,256]{1,0:T(8,128)(2,1)} %query.1) | copy-start | bytes 196612
  0.7 39.9 %copy-start = (bf16[256,5376]{1,0:T(8,128)(2,1)S(1)}, bf16[256,5376]{1,0:T(8,128)(2,1)}, u32[]{:S(2)}) copy-start(bf16[256,5376]{1,0:T(8,128)(2,1)} %out_one.1) | copy-start | bytes 8257540
  3.3 13.9 %collective-permute-start.1 = (bf16[128,256]{1,0:T(8,128)(2,1)}, bf16[128,256]{1,0:T(8,128)(2,1)S(1)}, u32[]{:S(2)}, u32[]{:S(2)}) collective-permute-start(bf16[128,256]{1,0:T(8,128)(2,1)} %get-tuple-element.6), channel_id=1, source_target_pairs={{0,128},{16,144},{32,160},{48,176},{64,192},{80,208},{96,224},{112... | collective-permute-start | bytes 196616 | tf_op jit(solution)/shard_map/ppermute | solution.py:301
  9.4 7.8 %collective-permute-start = (bf16[128,256]{1,0:T(8,128)(2,1)}, bf16[128,256]{1,0:T(8,128)(2,1)S(1)}, u32[]{:S(2)}, u32[]{:S(2)}) collective-permute-start(bf16[128,256]{1,0:T(8,128)(2,1)} %get-tuple-element.6), channel_id=1, source_target_pairs={{0,64},{16,80},{32,96},{48,112},{64,128},{80,144},{96,160},{112,17... | collective-permute-start | bytes 196616 | tf_op jit(solution)/shard_map/ppermute | solution.py:301
  18.9 21.5 %all-to-all-start = ((bf16[4,256,256]{2,1,0:T(8,128)(2,1)}), bf16[4,256,256]{2,1,0:T(8,128)(2,1)S(1)}, u32[]{:S(2)}, u32[]{:S(2)}) async-start(bf16[4,256,256]{2,1,0:T(8,128)(2,1)} %broadcast_select_fusion), calls=%async_computation | async-start | bytes 1048576 | tf_op jit(solution)/shard_map/all_to_all | solution.py:297
  42.4 28.0 %copy-start.13 = (f32[5376]{0:T(1024)S(1)}, f32[5376]{0:T(1024)}, u32[]{:S(2)}) copy-start(f32[5376]{0:T(1024)} %param.17) | copy-start | bytes 64516
  42.5 28.0 %copy-start.14 = (f32[5376]{0:T(1024)S(1)}, f32[5376]{0:T(1024)}, u32[]{:S(2)}) copy-start(f32[5376]{0:T(1024)} %param.18) | copy-start | bytes 64516
  66.4 24.5 %all-to-all-start.3 = ((bf16[4,168,512]{2,1,0:T(8,128)(2,1)}), bf16[4,168,512]{2,1,0:T(8,128)(2,1)S(1)}, u32[]{:S(2)}, u32[]{:S(2)}) async-start(bf16[4,168,512]{2,1,0:T(8,128)(2,1)} %get-tuple-element.7), calls=%async_computation.3 | async-start | bytes 1376256 | tf_op jit(solution)/shard_map/all_to_all | solution.py:297
  90.9 76.0 %all-to-all-start.2 = ((bf16[16,8,5760]{2,1,0:T(8,128)(2,1)}), bf16[16,8,5760]{2,1,0:T(8,128)(2,1)S(1)}, u32[]{:S(2)}, u32[]{:S(2)}) async-start(bf16[16,8,5760]{2,1,0:T(8,128)(2,1)} %norms.1), calls=%async_computation.2 | async-start | bytes 2949120 | tf_op jit(solution)/shard_map/all_to_all | solution.py:293
  96.3 19.6 %collective-permute-start.2 = (bf16[672,512]{1,0:T(8,128)(2,1)S(1)}, bf16[672,512]{1,0:T(8,128)(2,1)S(1)}, u32[]{:S(2)}, u32[]{:S(2)}) collective-permute-start(bf16[672,512]{1,0:T(8,128)(2,1)S(1)} %bitcast.10), channel_id=1, source_target_pairs={{0,64},{16,80},{32,96},{48,112},{64,128},{80,144},{96,160},{112,17... | collective-permute-start | bytes 2064392 | tf_op jit(solution)/shard_map/ppermute | solution.py:301
  99.1 19.3 %collective-permute-start.3 = (bf16[672,512]{1,0:T(8,128)(2,1)S(1)}, bf16[672,512]{1,0:T(8,128)(2,1)S(1)}, u32[]{:S(2)}, u32[]{:S(2)}) collective-permute-start(bf16[672,512]{1,0:T(8,128)(2,1)S(1)} %bitcast.11), channel_id=1, source_target_pairs={{0,448},{16,464},{32,480},{48,496},{64,0},{80,16},{96,32},{112,48}... | collective-permute-start | bytes 2064392 | tf_op jit(solution)/shard_map/ppermute | solution.py:301
  115.9 51.1 %copy-start.8 = (bf16[672,512]{1,0:T(8,128)(2,1)}, bf16[672,512]{1,0:T(8,128)(2,1)S(1)}, u32[]{:S(2)}) copy-start(bf16[672,512]{1,0:T(8,128)(2,1)S(1)} %collective-permute-done.2.refs_1_) | copy-start | bytes 2064388
  115.9 19.7 %collective-permute-start.4 = (bf16[672,512]{1,0:T(8,128)(2,1)S(1)}, bf16[672,512]{1,0:T(8,128)(2,1)S(1)}, u32[]{:S(2)}, u32[]{:S(2)}) collective-permute-start(bf16[672,512]{1,0:T(8,128)(2,1)S(1)} %collective-permute-done.2.refs_1_), channel_id=1, source_target_pairs={{0,64},{16,80},{32,96},{48,112},{64,128},{80,144},{96,160},{112,17... | collective-permute-start | bytes 2064392 | tf_op jit(solution)/shard_map/ppermute | solution.py:301
  118.4 19.1 %copy-start.9 = (bf16[672,512]{1,0:T(8,128)(2,1)}, bf16[672,512]{1,0:T(8,128)(2,1)S(1)}, u32[]{:S(2)}) copy-start(bf16[672,512]{1,0:T(8,128)(2,1)S(1)} %collective-permute-done.3.refs_2_) | copy-start | bytes 2064388
  118.4 19.1 %collective-permute-start.5 = (bf16[672,512]{1,0:T(8,128)(2,1)S(1)}, bf16[672,512]{1,0:T(8,128)(2,1)S(1)}, u32[]{:S(2)}, u32[]{:S(2)}) collective-permute-start(bf16[672,512]{1,0:T(8,128)(2,1)S(1)} %collective-permute-done.3.refs_2_), channel_id=1, source_target_pairs={{0,448},{16,464},{32,480},{48,496},{64,0},{80,16},{96,32},{112,48}... | collective-permute-start | bytes 2064392 | tf_op jit(solution)/shard_map/ppermute | solution.py:301
  135.6 18.8 %collective-permute-start.6 = (bf16[672,512]{1,0:T(8,128)(2,1)S(1)}, bf16[672,512]{1,0:T(8,128)(2,1)S(1)}, u32[]{:S(2)}, u32[]{:S(2)}) collective-permute-start(bf16[672,512]{1,0:T(8,128)(2,1)S(1)} %collective-permute-done.4.refs_3_), channel_id=1, source_target_pairs={{0,64},{16,80},{32,96},{48,112},{64,128},{80,144},{96,160},{112,17... | collective-permute-start | bytes 2064392 | tf_op jit(solution)/shard_map/ppermute | solution.py:301
  137.5 27.6 %copy-start.11 = (bf16[672,512]{1,0:T(8,128)(2,1)}, bf16[672,512]{1,0:T(8,128)(2,1)S(1)}, u32[]{:S(2)}) copy-start(bf16[672,512]{1,0:T(8,128)(2,1)S(1)} %collective-permute-done.5.refs_4_) | copy-start | bytes 2064388
  137.5 18.8 %collective-permute-start.7 = (bf16[672,512]{1,0:T(8,128)(2,1)S(1)}, bf16[672,512]{1,0:T(8,128)(2,1)S(1)}, u32[]{:S(2)}, u32[]{:S(2)}) collective-permute-start(bf16[672,512]{1,0:T(8,128)(2,1)S(1)} %collective-permute-done.5.refs_4_), channel_id=1, source_target_pairs={{0,448},{16,464},{32,480},{48,496},{64,0},{80,16},{96,32},{112,48}... | collective-permute-start | bytes 2064392 | tf_op jit(solution)/shard_map/ppermute | solution.py:301
  154.4 10.6 %collective-permute-start.8 = (bf16[336,512]{1,0:T(8,128)(2,1)S(1)}, bf16[336,512]{1,0:T(8,128)(2,1)S(1)}, u32[]{:S(2)}, u32[]{:S(2)}) collective-permute-start(bf16[336,512]{1,0:T(8,128)(2,1)S(1)} %slice.13), channel_id=1, source_target_pairs={{0,64},{16,80},{32,96},{48,112},{64,128},{80,144},{96,160},{112,17... | collective-permute-start | bytes 1032200 | tf_op jit(solution)/shard_map/ppermute | solution.py:301
  156.4 10.5 %collective-permute-start.9 = (bf16[336,512]{1,0:T(8,128)(2,1)S(1)}, bf16[336,512]{1,0:T(8,128)(2,1)}, u32[]{:S(2)}, u32[]{:S(2)}) collective-permute-start(bf16[336,512]{1,0:T(8,128)(2,1)S(1)} %slice.14), channel_id=1, source_target_pairs={{0,448},{16,464},{32,480},{48,496},{64,0},{80,16},{96,32},{112,48}... | collective-permute-start | bytes 1032200 | tf_op jit(solution)/shard_map/ppermute | solution.py:301
  174.2 24.2 %copy-start.3 = (s32[3]{0:T(128)S(1)}, s32[3]{0:T(128)}, u32[]{:S(2)}) copy-start(s32[3]{0:T(128)} %copy-done.2) | copy-start | bytes 40
  174.2 24.1 %all-to-all-start.4 = ((bf16[8,128,256]{2,1,0:T(8,128)(2,1)}), bf16[8,128,256]{2,1,0:T(8,128)(2,1)S(1)}, u32[]{:S(2)}, u32[]{:S(2)}) async-start(bf16[8,128,256]{2,1,0:T(8,128)(2,1)} %get-tuple-element.9), calls=%async_computation.4 | async-start | bytes 1048576 | tf_op jit(solution)/shard_map/all_to_all | solution.py:426
  202.2 21.4 %all-to-all-start.5 = ((bf16[8,64,384]{2,1,0:T(8,128)(2,1)}), bf16[8,64,384]{2,1,0:T(8,128)(2,1)S(1)}, u32[]{:S(2)}, u32[]{:S(2)}) async-start(bf16[8,64,384]{2,1,0:T(8,128)(2,1)} %second_layer.1), calls=%async_computation.5 | async-start | bytes 786432 | tf_op jit(solution)/shard_map/all_to_all | solution.py:446
  (7 other events, 56.9 us)

commit v10 on v7

--- a/solution.py
+++ b/solution.py
@@ -33,7 +33,7 @@
 VMEM_LIMIT = 24 * 1024 * 1024
 FIRST_LIMIT = 24 * 1024 * 1024
 NORM_LIMIT = 24 * 1024 * 1024
-PROJECT_LIMIT = 56 * 1024 * 1024
+PROJECT_LIMIT = 50 * 1024 * 1024
 
 
 def whole(memory_space=pltpu.VMEM):
@@ -181,12 +181,19 @@
     pieces, refs = refs[:Z], refs[Z:]
     turn_cos, turn_sin, query, pair, held, block, in_sem, out_sem = refs
     level_rows = WIDTH // Z
+    depth = WIDTH // PARTS
     offsets = [0, -1, -2, -3, -4, 1, 2, 3]
-    for piece, offset in zip(pieces, offsets):
-        level = lax.rem(base[0] + (offset + Z), Z)
-        target = held.at[pl.ds(pl.multiple_of(level * level_rows, 16), level_rows)]
-        pltpu.make_async_copy(piece, target, in_sem.at[level]).start()
-    depth = WIDTH // PARTS
+
+    piece_of = {offset % Z: piece for piece, offset in zip(pieces, offsets)}
+    for place in range(Z):
+
+        @pl.when(base[0] == place)
+        def _(place=place):
+            for level in range(Z):
+                target = held.at[level * level_rows : (level + 1) * level_rows]
+                piece = piece_of[(level - place) % Z]
+                pltpu.make_async_copy(piece, target, in_sem.at[level]).start()
+
     total = jnp.zeros((TOK, 4 * HEAD_SIZE), jnp.float32)
     arrived = 0
     for part in range(PARTS):
@@ -339,6 +346,7 @@
         for _ in range(1, count + 1):
             piece = ctx_shift(piece, sign * Y_HI)
             pieces.append(piece)
+    pieces = [pltpu.with_memory_space_constraint(piece, pltpu.HBM) for piece in pieces]
 
     later = jnp.concatenate([own, back_one], axis=0)
     earlier = jnp.concatenate([back_one, back_two], axis=0)

time: 231 us -> 228 us (0.987)
  the two profiles are of different devices: /device:TPU:74 before, /device:TPU:64 now
where the time goes in v10:
time: 228 us; the launch traced here: 227 us
  waiting for transfers between devices  96.9 us (42%)
  starting transfers between devices  65.5 us (29%)
  blocking collectives  40 us (18%)
  Pallas kernels  16 us (7%)
  other arithmetic  4.63 us (2%)
  local copies, waits for them, and re-layouts  2.88 us (1%)
    ppermute x9, waiting for transfers between devices, ctx_shift(): lax.ppermute(value, 'ctx', [(i, (i + steps) % N_CTX) for i in range(N_CTX)])  56.1 us
    ppermute x9, starting transfers between devices, ctx_shift(): lax.ppermute(value, 'ctx', [(i, (i + steps) % N_CTX) for i in range(N_CTX)])  32.9 us
    all_to_all x2, waiting for transfers between devices, exchange_y(): lax.all_to_all(value, 'ctx', 0, 0, tiled=True, axis_index_groups=Y_GROUPS)  27.6 us
    all_to_all x1, blocking collectives, exchange_heads(): return lax.all_to_all(value, 'heads', 0, 0, tiled=True)  25.4 us
    all_gather x1, blocking collectives, shards(): lax.all_gather(query, 'ctx', axis=0, tiled=True, axis_index_groups=Y_GROUPS)  14.6 us
    all_to_all x1, waiting for transfers between devices, shards(): lax.all_to_all(sent, 'ctx', 0, 0, tiled=True, axis_index_groups=LEVEL_PAIRS)  13.2 us
    all_to_all x2, starting transfers between devices, exchange_y(): lax.all_to_all(value, 'ctx', 0, 0, tiled=True, axis_index_groups=Y_GROUPS)  11.1 us
    all_to_all x1, starting transfers between devices, shards(): lax.all_to_all(pair, 'ctx', 0, 0, tiled=True, axis_index_groups=Z_GROUPS)  7.61 us
  transfers between devices with their start and end apart: 14, of which 8 were waited for; matrix products, arithmetic and copies ran while one was open for 2% of the time, Pallas kernels for 1%

profile of v10, /device:TPU:64, one launch (start us, length us, event | category | flops | bytes accessed | tf_op | source)
XLA Modules:
  0.0 227.0 jit_solution(8684007608100294375)
XLA Ops:
  0.7 2.6 %prepare.1 = (bf16[128,256]{1,0:T(8,128)(2,1)}, bf16[4,168,512]{2,1,0:T(8,128)(2,1)}) custom-call(bf16[128,128]{1,0:T(8,128)(2,1)} %keys.1, bf16[128,128]{1,0:T(8,128)(2,1)} %values.1, bf16[168,256]{1,0:T(8,128)(2,1)} %proj_query.1, bf16[168,128]{1,0:T(8,128)(2,1)} %key_projection.1, bf16[168,128]{1,0:T(8,128)(2,1)} %value_projection.1), custom_call_target="tpu_custom_call" | custom-call | tf_op jit(solution)/shard_map/prepare/pallas_call | solution.py:324
  3.3 6.1 %collective-permute-start.1 = (bf16[128,256]{1,0:T(8,128)(2,1)}, bf16[128,256]{1,0:T(8,128)(2,1)S(1)}, u32[]{:S(2)}, u32[]{:S(2)}) collective-permute-start(bf16[128,256]{1,0:T(8,128)(2,1)} %get-tuple-element.6), channel_id=1, source_target_pairs={{0,128},{16,144},{32,160},{48,176},{64,192},{80,208},{96,224},{112... | collective-permute-start | bytes 196616 | tf_op jit(solution)/shard_map/ppermute | solution.py:299
  9.4 5.5 %collective-permute-start = (bf16[128,256]{1,0:T(8,128)(2,1)}, bf16[128,256]{1,0:T(8,128)(2,1)S(1)}, u32[]{:S(2)}, u32[]{:S(2)}) collective-permute-start(bf16[128,256]{1,0:T(8,128)(2,1)} %get-tuple-element.6), channel_id=1, source_target_pairs={{0,64},{16,80},{32,96},{48,112},{64,128},{80,144},{96,160},{112,17... | collective-permute-start | bytes 196616 | tf_op jit(solution)/shard_map/ppermute | solution.py:299
  18.9 7.1 %all-to-all-start = ((bf16[4,256,256]{2,1,0:T(8,128)(2,1)}), bf16[4,256,256]{2,1,0:T(8,128)(2,1)S(1)}, u32[]{:S(2)}, u32[]{:S(2)}) async-start(bf16[4,256,256]{2,1,0:T(8,128)(2,1)} %broadcast_select_fusion), calls=%async_computation | async-start | bytes 1048576 | tf_op jit(solution)/shard_map/all_to_all | solution.py:295
  27.9 13.3 %all-to-all-done.blocks = bf16[4,256,256]{2,1,0:T(8,128)(2,1)S(1)} async-done(((bf16[4,256,256]{2,1,0:T(8,128)(2,1)}), bf16[4,256,256]{2,1,0:T(8,128)(2,1)S(1)}, u32[]{:S(2)}, u32[]{:S(2)}) %all-to-all-start) | async-done | bytes 524320 | tf_op jit(solution)/shard_map/all_to_all | solution.py:295
  43.3 25.4 %all_to_all.30.got = bf16[16,8,5760]{2,1,0:T(8,128)(2,1)S(1)} all-to-all(bf16[16,8,5760]{2,1,0:T(8,128)(2,1)S(1)} %first_layer.1), channel_id=1, replica_groups=mesh['ctx'=32,'heads'=16] {'heads'}, dimensions={0} | all-to-all | bytes 2949120 | tf_op jit(solution)/shard_map/all_to_all | solution.py:291
  68.7 4.0 %all-to-all-start.3 = ((bf16[4,168,512]{2,1,0:T(8,128)(2,1)}), bf16[4,168,512]{2,1,0:T(8,128)(2,1)S(1)}, u32[]{:S(2)}, u32[]{:S(2)}) async-start(bf16[4,168,512]{2,1,0:T(8,128)(2,1)} %get-tuple-element.7), calls=%async_computation.3 | async-start | bytes 1376256 | tf_op jit(solution)/shard_map/all_to_all | solution.py:295
  74.5 14.2 %all-to-all-done.3 = bf16[4,168,512]{2,1,0:T(8,128)(2,1)S(1)} async-done(((bf16[4,168,512]{2,1,0:T(8,128)(2,1)}), bf16[4,168,512]{2,1,0:T(8,128)(2,1)S(1)}, u32[]{:S(2)}, u32[]{:S(2)}) %all-to-all-start.3) | async-done | bytes 688160 | tf_op jit(solution)/shard_map/all_to_all | solution.py:295
  88.8 7.2 %all-to-all-start.2 = ((bf16[16,8,5760]{2,1,0:T(8,128)(2,1)}), bf16[16,8,5760]{2,1,0:T(8,128)(2,1)S(1)}, u32[]{:S(2)}, u32[]{:S(2)}) async-start(bf16[16,8,5760]{2,1,0:T(8,128)(2,1)} %norms.1), calls=%async_computation.2 | async-start | bytes 2949120 | tf_op jit(solution)/shard_map/all_to_all | solution.py:291
  96.0 2.7 %collective-permute-start.2 = (bf16[672,512]{1,0:T(8,128)(2,1)S(1)}, bf16[672,512]{1,0:T(8,128)(2,1)S(1)}, u32[]{:S(2)}, u32[]{:S(2)}) collective-permute-start(bf16[672,512]{1,0:T(8,128)(2,1)S(1)} %bitcast.10), channel_id=1, source_target_pairs={{0,64},{16,80},{32,96},{48,112},{64,128},{80,144},{96,160},{112,17... | collective-permute-start | bytes 2064392 | tf_op jit(solution)/shard_map/ppermute | solution.py:299
  98.8 3.1 %collective-permute-start.6 = (bf16[672,512]{1,0:T(8,128)(2,1)S(1)}, bf16[672,512]{1,0:T(8,128)(2,1)S(1)}, u32[]{:S(2)}, u32[]{:S(2)}) collective-permute-start(bf16[672,512]{1,0:T(8,128)(2,1)S(1)} %bitcast.11), channel_id=1, source_target_pairs={{0,448},{16,464},{32,480},{48,496},{64,0},{80,16},{96,32},{112,48}... | collective-permute-start | bytes 2064392 | tf_op jit(solution)/shard_map/ppermute | solution.py:299
  101.9 14.0 %collective-permute-done.2.refs_1_ = bf16[672,512]{1,0:T(8,128)(2,1)S(1)} collective-permute-done((bf16[672,512]{1,0:T(8,128)(2,1)S(1)}, bf16[672,512]{1,0:T(8,128)(2,1)S(1)}, u32[]{:S(2)}, u32[]{:S(2)}) %collective-permute-start.2) | collective-permute-done | bytes 688160 | tf_op jit(solution)/shard_map/ppermute | solution.py:299
  115.9 2.5 %collective-permute-start.3 = (bf16[672,512]{1,0:T(8,128)(2,1)S(1)}, bf16[672,512]{1,0:T(8,128)(2,1)S(1)}, u32[]{:S(2)}, u32[]{:S(2)}) collective-permute-start(bf16[672,512]{1,0:T(8,128)(2,1)S(1)} %collective-permute-done.2.refs_1_), channel_id=1, source_target_pairs={{0,64},{16,80},{32,96},{48,112},{64,128},{80,144},{96,160},{112,17... | collective-permute-start | bytes 2064392 | tf_op jit(solution)/shard_map/ppermute | solution.py:299
  118.4 4.3 %collective-permute-start.7 = (bf16[672,512]{1,0:T(8,128)(2,1)S(1)}, bf16[672,512]{1,0:T(8,128)(2,1)S(1)}, u32[]{:S(2)}, u32[]{:S(2)}) collective-permute-start(bf16[672,512]{1,0:T(8,128)(2,1)S(1)} %collective-permute-done.6.refs_5_), channel_id=1, source_target_pairs={{0,448},{16,464},{32,480},{48,496},{64,0},{80,16},{96,32},{112,48}... | collective-permute-start | bytes 2064392 | tf_op jit(solution)/shard_map/ppermute | solution.py:299
  122.7 13.2 %collective-permute-done.3.refs_2_ = bf16[672,512]{1,0:T(8,128)(2,1)S(1)} collective-permute-done((bf16[672,512]{1,0:T(8,128)(2,1)S(1)}, bf16[672,512]{1,0:T(8,128)(2,1)S(1)}, u32[]{:S(2)}, u32[]{:S(2)}) %collective-permute-start.3) | collective-permute-done | bytes 688160 | tf_op jit(solution)/shard_map/ppermute | solution.py:299
  137.8 4.9 %collective-permute-start.8 = (bf16[672,512]{1,0:T(8,128)(2,1)S(1)}, bf16[672,512]{1,0:T(8,128)(2,1)S(1)}, u32[]{:S(2)}, u32[]{:S(2)}) collective-permute-start(bf16[672,512]{1,0:T(8,128)(2,1)S(1)} %collective-permute-done.7.refs_6_), channel_id=1, source_target_pairs={{0,448},{16,464},{32,480},{48,496},{64,0},{80,16},{96,32},{112,48}... | collective-permute-start | bytes 2064392 | tf_op jit(solution)/shard_map/ppermute | solution.py:299
  142.7 12.3 %collective-permute-done.4.refs_3_ = bf16[672,512]{1,0:T(8,128)(2,1)S(1)} collective-permute-done((bf16[672,512]{1,0:T(8,128)(2,1)S(1)}, bf16[672,512]{1,0:T(8,128)(2,1)S(1)}, u32[]{:S(2)}, u32[]{:S(2)}) %collective-permute-start.4) | collective-permute-done | bytes 688160 | tf_op jit(solution)/shard_map/ppermute | solution.py:299
  159.0 14.4 %collective-permute-done.5.refs_4_ = bf16[672,512]{1,0:T(8,128)(2,1)} collective-permute-done((bf16[672,512]{1,0:T(8,128)(2,1)S(1)}, bf16[672,512]{1,0:T(8,128)(2,1)}, u32[]{:S(2)}, u32[]{:S(2)}) %collective-permute-start.5) | collective-permute-done | bytes 688160 | tf_op jit(solution)/shard_map/ppermute | solution.py:299
  173.4 4.4 %project.1 = (bf16[128,256]{1,0:T(8,128)(2,1)S(1)}, bf16[8,128,256]{2,1,0:T(8,128)(2,1)}) custom-call(s32[3]{0:T(128)S(1)} %pad_add_fusion.base, bf16[16,8,5760]{2,1,0:T(8,128)(2,1)S(1)} %all-to-all-done.2.got, bf16[672,512]{1,0:T(8,128)(2,1)} %bitcast.12, bf16[672,512]{1,0:T(8,128)(2,1)} %copy-done.3, bf16[672,512]{1,0:T(8,128)(2,1)} %copy-done.5, ...), custom_call_target="tpu_custom_call" | custom-call | tf_op jit(solution)/shard_map/project/pallas_call | solution.py:400
  177.8 7.6 %all-to-all-start.4 = ((bf16[8,128,256]{2,1,0:T(8,128)(2,1)}), bf16[8,128,256]{2,1,0:T(8,128)(2,1)S(1)}, u32[]{:S(2)}, u32[]{:S(2)}) async-start(bf16[8,128,256]{2,1,0:T(8,128)(2,1)} %get-tuple-element.9), calls=%async_computation.4 | async-start | bytes 1048576 | tf_op jit(solution)/shard_map/all_to_all | solution.py:418
  186.1 14.6 %all_gather.3.queries = bf16[512,256]{1,0:T(8,128)(2,1)S(1)} all-gather(bf16[128,256]{1,0:T(8,128)(2,1)S(1)} %get-tuple-element.8), channel_id=1, replica_groups={{0,16,32,48},{64,80,96,112},{128,144,160,176},{192,208,224,240},{256,27..., dimensions={0}, use_global_device_ids=true | all-gather | bytes 327680 | tf_op jit(solution)/shard_map/all_gather | solution.py:420
  200.9 3.7 %second_layer.1 = bf16[8,64,384]{2,1,0:T(8,128)(2,1)} custom-call(s32[3]{0:T(128)S(1)} %pad_add_fusion.base, bf16[512,256]{1,0:T(8,128)(2,1)S(1)} %all_gather.3.queries, bf16[1024,256]{1,0:T(8,128)(2,1)S(1)} %bitcast.9, s32[512,128]{1,0:T(8,128)S(1)} %broadcast_in_dim.55.low), custom_call_target="tpu_custom_call" | custom-call | tf_op jit(solution)/shard_map/second_layer/pallas_call | solution.py:429
  204.6 6.7 %all-to-all-start.5 = ((bf16[8,64,384]{2,1,0:T(8,128)(2,1)}), bf16[8,64,384]{2,1,0:T(8,128)(2,1)S(1)}, u32[]{:S(2)}, u32[]{:S(2)}) async-start(bf16[8,64,384]{2,1,0:T(8,128)(2,1)} %second_layer.1), calls=%async_computation.5 | async-start | bytes 786432 | tf_op jit(solution)/shard_map/all_to_all | solution.py:438
  212.1 13.2 %all-to-all-done.5.got = bf16[8,64,384]{2,1,0:T(8,128)(2,1)S(1)} async-done(((bf16[8,64,384]{2,1,0:T(8,128)(2,1)}), bf16[8,64,384]{2,1,0:T(8,128)(2,1)S(1)}, u32[]{:S(2)}, u32[]{:S(2)}) %all-to-all-start.5) | async-done | bytes 393248 | tf_op jit(solution)/shard_map/all_to_all | solution.py:438
  (54 shorter events, 18.9 us)
Async XLA Ops:
  0.6 27.2 %copy-start.11 = (s32[2]{0:T(128)S(1)}, s32[2]{0:T(128)}, u32[]{:S(2)}) copy-start(s32[2]{0:T(128)} %param.22) | copy-start | bytes 28
  0.6 40.7 %copy-start.1 = (bf16[128,256]{1,0:T(8,128)(2,1)S(1)}, bf16[128,256]{1,0:T(8,128)(2,1)}, u32[]{:S(2)}) copy-start(bf16[128,256]{1,0:T(8,128)(2,1)} %query.1) | copy-start | bytes 196612
  0.7 40.7 %copy-start = (bf16[256,5376]{1,0:T(8,128)(2,1)S(1)}, bf16[256,5376]{1,0:T(8,128)(2,1)}, u32[]{:S(2)}) copy-start(bf16[256,5376]{1,0:T(8,128)(2,1)} %out_one.1) | copy-start | bytes 8257540
  3.3 13.9 %collective-permute-start.1 = (bf16[128,256]{1,0:T(8,128)(2,1)}, bf16[128,256]{1,0:T(8,128)(2,1)S(1)}, u32[]{:S(2)}, u32[]{:S(2)}) collective-permute-start(bf16[128,256]{1,0:T(8,128)(2,1)} %get-tuple-element.6), channel_id=1, source_target_pairs={{0,128},{16,144},{32,160},{48,176},{64,192},{80,208},{96,224},{112... | collective-permute-start | bytes 196616 | tf_op jit(solution)/shard_map/ppermute | solution.py:299
  9.4 7.8 %collective-permute-start = (bf16[128,256]{1,0:T(8,128)(2,1)}, bf16[128,256]{1,0:T(8,128)(2,1)S(1)}, u32[]{:S(2)}, u32[]{:S(2)}) collective-permute-start(bf16[128,256]{1,0:T(8,128)(2,1)} %get-tuple-element.6), channel_id=1, source_target_pairs={{0,64},{16,80},{32,96},{48,112},{64,128},{80,144},{96,160},{112,17... | collective-permute-start | bytes 196616 | tf_op jit(solution)/shard_map/ppermute | solution.py:299
  18.9 22.3 %all-to-all-start = ((bf16[4,256,256]{2,1,0:T(8,128)(2,1)}), bf16[4,256,256]{2,1,0:T(8,128)(2,1)S(1)}, u32[]{:S(2)}, u32[]{:S(2)}) async-start(bf16[4,256,256]{2,1,0:T(8,128)(2,1)} %broadcast_select_fusion), calls=%async_computation | async-start | bytes 1048576 | tf_op jit(solution)/shard_map/all_to_all | solution.py:295
  43.3 29.4 %copy-start.9 = (f32[5376]{0:T(1024)S(1)}, f32[5376]{0:T(1024)}, u32[]{:S(2)}) copy-start(f32[5376]{0:T(1024)} %param.17) | copy-start | bytes 64516
  43.3 29.4 %copy-start.10 = (f32[5376]{0:T(1024)S(1)}, f32[5376]{0:T(1024)}, u32[]{:S(2)}) copy-start(f32[5376]{0:T(1024)} %param.18) | copy-start | bytes 64516
  68.7 20.0 %all-to-all-start.3 = ((bf16[4,168,512]{2,1,0:T(8,128)(2,1)}), bf16[4,168,512]{2,1,0:T(8,128)(2,1)S(1)}, u32[]{:S(2)}, u32[]{:S(2)}) async-start(bf16[4,168,512]{2,1,0:T(8,128)(2,1)} %get-tuple-element.7), calls=%async_computation.3 | async-start | bytes 1376256 | tf_op jit(solution)/shard_map/all_to_all | solution.py:295
  88.8 10.0 %copy-start.2 = (bf16[4,168,512]{2,1,0:T(8,128)(2,1)}, bf16[4,168,512]{2,1,0:T(8,128)(2,1)S(1)}, u32[]{:S(2)}) copy-start(bf16[4,168,512]{2,1,0:T(8,128)(2,1)S(1)} %all-to-all-done.3) | copy-start | bytes 2064388
  88.8 84.6 %all-to-all-start.2 = ((bf16[16,8,5760]{2,1,0:T(8,128)(2,1)}), bf16[16,8,5760]{2,1,0:T(8,128)(2,1)S(1)}, u32[]{:S(2)}, u32[]{:S(2)}) async-start(bf16[16,8,5760]{2,1,0:T(8,128)(2,1)} %norms.1), calls=%async_computation.2 | async-start | bytes 2949120 | tf_op jit(solution)/shard_map/all_to_all | solution.py:291
  96.0 19.9 %collective-permute-start.2 = (bf16[672,512]{1,0:T(8,128)(2,1)S(1)}, bf16[672,512]{1,0:T(8,128)(2,1)S(1)}, u32[]{:S(2)}, u32[]{:S(2)}) collective-permute-start(bf16[672,512]{1,0:T(8,128)(2,1)S(1)} %bitcast.10), channel_id=1, source_target_pairs={{0,64},{16,80},{32,96},{48,112},{64,128},{80,144},{96,160},{112,17... | collective-permute-start | bytes 2064392 | tf_op jit(solution)/shard_map/ppermute | solution.py:299
  98.8 19.6 %collective-permute-start.6 = (bf16[672,512]{1,0:T(8,128)(2,1)S(1)}, bf16[672,512]{1,0:T(8,128)(2,1)S(1)}, u32[]{:S(2)}, u32[]{:S(2)}) collective-permute-start(bf16[672,512]{1,0:T(8,128)(2,1)S(1)} %bitcast.11), channel_id=1, source_target_pairs={{0,448},{16,464},{32,480},{48,496},{64,0},{80,16},{96,32},{112,48}... | collective-permute-start | bytes 2064392 | tf_op jit(solution)/shard_map/ppermute | solution.py:299
  115.9 57.5 %copy-start.3 = (bf16[672,512]{1,0:T(8,128)(2,1)}, bf16[672,512]{1,0:T(8,128)(2,1)S(1)}, u32[]{:S(2)}) copy-start(bf16[672,512]{1,0:T(8,128)(2,1)S(1)} %collective-permute-done.2.refs_1_) | copy-start | bytes 2064388
  115.9 20.0 %collective-permute-start.3 = (bf16[672,512]{1,0:T(8,128)(2,1)S(1)}, bf16[672,512]{1,0:T(8,128)(2,1)S(1)}, u32[]{:S(2)}, u32[]{:S(2)}) collective-permute-start(bf16[672,512]{1,0:T(8,128)(2,1)S(1)} %collective-permute-done.2.refs_1_), channel_id=1, source_target_pairs={{0,64},{16,80},{32,96},{48,112},{64,128},{80,144},{96,160},{112,17... | collective-permute-start | bytes 2064392 | tf_op jit(solution)/shard_map/ppermute | solution.py:299
  118.4 17.5 %copy-start.4 = (bf16[672,512]{1,0:T(8,128)(2,1)}, bf16[672,512]{1,0:T(8,128)(2,1)S(1)}, u32[]{:S(2)}) copy-start(bf16[672,512]{1,0:T(8,128)(2,1)S(1)} %collective-permute-done.6.refs_5_) | copy-start | bytes 2064388
  118.4 19.4 %collective-permute-start.7 = (bf16[672,512]{1,0:T(8,128)(2,1)S(1)}, bf16[672,512]{1,0:T(8,128)(2,1)S(1)}, u32[]{:S(2)}, u32[]{:S(2)}) collective-permute-start(bf16[672,512]{1,0:T(8,128)(2,1)S(1)} %collective-permute-done.6.refs_5_), channel_id=1, source_target_pairs={{0,448},{16,464},{32,480},{48,496},{64,0},{80,16},{96,32},{112,48}... | collective-permute-start | bytes 2064392 | tf_op jit(solution)/shard_map/ppermute | solution.py:299
  135.9 19.1 %collective-permute-start.4 = (bf16[672,512]{1,0:T(8,128)(2,1)S(1)}, bf16[672,512]{1,0:T(8,128)(2,1)S(1)}, u32[]{:S(2)}, u32[]{:S(2)}) collective-permute-start(bf16[672,512]{1,0:T(8,128)(2,1)S(1)} %collective-permute-done.3.refs_2_), channel_id=1, source_target_pairs={{0,64},{16,80},{32,96},{48,112},{64,128},{80,144},{96,160},{112,17... | collective-permute-start | bytes 2064392 | tf_op jit(solution)/shard_map/ppermute | solution.py:299
  137.8 35.6 %copy-start.6 = (bf16[672,512]{1,0:T(8,128)(2,1)}, bf16[672,512]{1,0:T(8,128)(2,1)S(1)}, u32[]{:S(2)}) copy-start(bf16[672,512]{1,0:T(8,128)(2,1)S(1)} %collective-permute-done.7.refs_6_) | copy-start | bytes 2064388
  137.8 20.3 %collective-permute-start.8 = (bf16[672,512]{1,0:T(8,128)(2,1)S(1)}, bf16[672,512]{1,0:T(8,128)(2,1)S(1)}, u32[]{:S(2)}, u32[]{:S(2)}) collective-permute-start(bf16[672,512]{1,0:T(8,128)(2,1)S(1)} %collective-permute-done.7.refs_6_), channel_id=1, source_target_pairs={{0,448},{16,464},{32,480},{48,496},{64,0},{80,16},{96,32},{112,48}... | collective-permute-start | bytes 2064392 | tf_op jit(solution)/shard_map/ppermute | solution.py:299
  155.0 3.1 %copy-start.7 = (bf16[672,512]{1,0:T(8,128)(2,1)}, bf16[672,512]{1,0:T(8,128)(2,1)S(1)}, u32[]{:S(2)}) copy-start(bf16[672,512]{1,0:T(8,128)(2,1)S(1)} %collective-permute-done.4.refs_3_) | copy-start | bytes 2064388
  155.0 18.4 %collective-permute-start.5 = (bf16[672,512]{1,0:T(8,128)(2,1)S(1)}, bf16[672,512]{1,0:T(8,128)(2,1)}, u32[]{:S(2)}, u32[]{:S(2)}) collective-permute-start(bf16[672,512]{1,0:T(8,128)(2,1)S(1)} %collective-permute-done.4.refs_3_), channel_id=1, source_target_pairs={{0,64},{16,80},{32,96},{48,112},{64,128},{80,144},{96,160},{112,17... | collective-permute-start | bytes 2064392 | tf_op jit(solution)/shard_map/ppermute | solution.py:299
  177.8 23.0 %all-to-all-start.4 = ((bf16[8,128,256]{2,1,0:T(8,128)(2,1)}), bf16[8,128,256]{2,1,0:T(8,128)(2,1)S(1)}, u32[]{:S(2)}, u32[]{:S(2)}) async-start(bf16[8,128,256]{2,1,0:T(8,128)(2,1)} %get-tuple-element.9), calls=%async_computation.4 | async-start | bytes 1048576 | tf_op jit(solution)/shard_map/all_to_all | solution.py:418
  204.6 20.7 %all-to-all-start.5 = ((bf16[8,64,384]{2,1,0:T(8,128)(2,1)}), bf16[8,64,384]{2,1,0:T(8,128)(2,1)S(1)}, u32[]{:S(2)}, u32[]{:S(2)}) async-start(bf16[8,64,384]{2,1,0:T(8,128)(2,1)} %second_layer.1), calls=%async_computation.5 | async-start | bytes 786432 | tf_op jit(solution)/shard_map/all_to_all | solution.py:438
  (2 other events, 2.8 us)
